TPU v7x, 768 devices: a whole 4x8x12 slice. The times are simulated.
768 devices in a mesh: dp: 64 (over y, x, core), fsdp: 12 (over z).
Axes of the slice: x: 4, y: 8, z: 12, core: 2. Of those that a mesh axis runs over, the one named last changes fastest.
Arguments:
- enc_out: bfloat16 [12, 20480, 1408], P('fsdp', 'dp')
- norm_gain: float32 [1408], replicated, may hold values from 0.25 to 1.75
- norm_bias: float32 [1408], replicated, may hold values from -3 to 3
- w_e2d: bfloat16 [1408, 512], P('dp'), may hold values from -0.15625 to 0.15625
- token_index: int32 [12, 20480], P('fsdp', 'dp'), may hold values from 0 to 20479, as said below
- counts: int32 [12, 128], P('fsdp'), may hold values from 1 to 320, 20480 in all within a row
- owner: int32 [12, 128], P('fsdp'), may hold values from 0 to 127, each once within a row
- dec_tubes: int32 [12, 128, 512], P('fsdp', 'dp'), may hold values from 0 to 1567, as said below
- mask_token: float32 [512], replicated, may hold values from -4 to 4
- dec_gain: float32 [512], replicated, may hold values from 0.25 to 1.75
- dec_bias: float32 [512], replicated, may hold values from -3 to 3
- w_qkv: bfloat16 [512, 1536], P(None, 'fsdp')
- w_proj: bfloat16 [512, 512], replicated, may hold values from -0.25 to 0.25
- proj_bias: float32 [512], replicated, may hold values from -3 to 3
Outputs:
- dec_state: bfloat16 [12, 128, 512, 512], P('fsdp', 'dp')
Inputs may be any that keep to these rules, and one draw needn't show every extreme that they name: `token_index`: in each group a permutation of all visible tokens; the 320 rows of one device hold, in rising order, the tokens of one residue modulo the devices of dp, so that one device holds at most 320 / (devices of dp) tokens of one clip. Each group's counts sum to 20480. `owner`: each group's slots are a permutation; slot s lies on the device of dp index s // 2. `dec_tubes`: each row holds 512 different tube numbers.
All inputs are finite; a program needn't handle non-finite values.
Results may differ from a plain program's by a relative error of at most 0.0089.
Values may be sent and summed in bfloat16 or wider, within the bound.
No kernel may reach another device: no remote copies, remote signals or barrier semaphores. Data moves between devices by JAX's collectives and lax.ppermute only.
A program may use at most 32 MiB of HBM per device.

v0:
```python
import jax
import jax.numpy as jnp
from jax import lax
from jax.sharding import PartitionSpec as P

DEC_HEADS = 8
VMAX = 320


def layer_norm(values, gain_vec, bias_vec):
    average = jnp.mean(values, axis=-1, keepdims=True)
    centred = values - average
    spread = jnp.mean(centred * centred, axis=-1, keepdims=True)
    return centred * lax.rsqrt(spread + 1e-06) * gain_vec + bias_vec


def tube_codes(tube_ids, code_width):
    column = jnp.arange(code_width, dtype=jnp.int32)
    exponent = (2 * (column // 2)).astype(jnp.float32) / code_width
    angles = tube_ids.astype(jnp.float32)[..., None] * jnp.power(jnp.float32(10000.0), -exponent)
    return jnp.where(column % 2 == 0, jnp.sin(angles), jnp.cos(angles))


def attend(queries, key_rows, value_rows, n_heads):
    length = queries.shape[0]
    head_width = queries.shape[1] // n_heads
    scale_factor = head_width ** (-0.5)

    def split_heads(matrix):
        return matrix.reshape(length, n_heads, head_width).transpose(1, 0, 2)

    def one_head(triple):
        query_h, key_h, value_h = triple
        scores = jnp.dot(query_h, key_h.T, preferred_element_type=jnp.float32) * scale_factor
        row_max = jnp.max(scores, axis=-1, keepdims=True)
        expo_vals = jnp.exp(scores - row_max)
        weights = (expo_vals / jnp.sum(expo_vals, axis=-1, keepdims=True)).astype(jnp.bfloat16)
        return jnp.dot(weights, value_h, preferred_element_type=jnp.float32).astype(jnp.bfloat16)

    outputs = lax.map(
        one_head, (split_heads(queries), split_heads(key_rows), split_heads(value_rows))
    )
    return outputs.transpose(1, 0, 2).reshape(length, n_heads * head_width)


def on_device(
    enc_out,
    norm_gain,
    norm_bias,
    w_e2d,
    token_index,
    counts,
    owner,
    dec_tubes,
    mask_token,
    dec_gain,
    dec_bias,
    w_qkv,
    w_proj,
    proj_bias,
):
    group_size = lax.axis_size("dp")
    my_index = lax.axis_index("dp")
    features = enc_out[0]
    dec_width = w_e2d.shape[1]
    my_clips = dec_tubes.shape[1]
    dec_length = dec_tubes.shape[2]
    per_peer = VMAX // group_size
    peer_rows = my_clips * per_peer
    normed = layer_norm(features.astype(jnp.float32), norm_gain, norm_bias).astype(jnp.bfloat16)
    vis_counts = counts[0]
    slot_ids = owner[0]
    held_ids = token_index[0]
    first_ids = jnp.cumsum(vis_counts) - vis_counts
    member = (held_ids[:, None] >= first_ids[None, :]) & (
        held_ids[:, None] < (first_ids + vis_counts)[None, :]
    )
    clip_first = jnp.sum(jnp.where(member, first_ids[None, :], 0), axis=1)
    clip_slot = jnp.sum(jnp.where(member, slot_ids[None, :], 0), axis=1)
    clip_rank = held_ids - clip_first
    send_pos = (
        clip_slot // my_clips * peer_rows
        + clip_slot % my_clips * per_peer
        + clip_rank // group_size
    )
    payload = jnp.dot(
        normed, lax.all_gather(w_e2d, "dp", axis=0, tiled=True), preferred_element_type=jnp.float32
    ).astype(jnp.bfloat16)
    sent = (
        jnp.zeros((group_size * peer_rows, payload.shape[1]), jnp.bfloat16)
        .at[send_pos]
        .set(payload)
    )
    sent_rank = jnp.full((group_size * peer_rows,), -1, jnp.int32).at[send_pos].set(clip_rank)
    received, recv_rank = (
        lax.all_to_all(
            sent.reshape(group_size, peer_rows, payload.shape[1]),
            "dp",
            split_axis=0,
            concat_axis=0,
            tiled=True,
        ),
        lax.all_to_all(
            sent_rank.reshape(group_size, peer_rows), "dp", split_axis=0, concat_axis=0, tiled=True
        ),
    )
    received = received.reshape(group_size * peer_rows, payload.shape[1])
    recv_rank = recv_rank.reshape(group_size * peer_rows)
    local_clip = jnp.arange(group_size * peer_rows, dtype=jnp.int32) % peer_rows // per_peer
    dest_pos = jnp.where(recv_rank >= 0, local_clip * dec_length + recv_rank, my_clips * dec_length)
    placed = (
        jnp.zeros((my_clips * dec_length, dec_width), jnp.bfloat16)
        .at[dest_pos]
        .set(received, mode="drop")
    )
    my_slots = my_index * my_clips + jnp.arange(my_clips, dtype=jnp.int32)
    slot_count = jnp.sum(
        jnp.where(slot_ids[None, :] == my_slots[:, None], vis_counts[None, :], 0), axis=1
    )
    visible = jnp.arange(dec_length, dtype=jnp.int32)[None, :] < slot_count[:, None]
    dec_input = jnp.where(
        visible[..., None],
        placed.reshape(my_clips, dec_length, dec_width).astype(jnp.float32),
        mask_token,
    ) + tube_codes(dec_tubes[0], dec_width)
    dec_normed = (
        layer_norm(dec_input, dec_gain, dec_bias).astype(jnp.bfloat16).reshape(-1, dec_width)
    )
    projected = jnp.dot(
        dec_normed,
        lax.all_gather(w_qkv, "fsdp", axis=1, tiled=True),
        preferred_element_type=jnp.float32,
    ).astype(jnp.bfloat16)
    projected = projected.reshape(my_clips, dec_length, 3 * dec_width)

    def per_slot(block):
        return attend(
            block[:, :dec_width],
            block[:, dec_width : 2 * dec_width],
            block[:, 2 * dec_width :],
            DEC_HEADS,
        )

    attended = lax.map(per_slot, projected)
    mixed = jnp.dot(attended.reshape(-1, dec_width), w_proj, preferred_element_type=jnp.float32)
    result = dec_input.reshape(-1, dec_width) + mixed + proj_bias
    return result.astype(jnp.bfloat16).reshape(1, my_clips, dec_length, dec_width)


def solution(mesh):
    return jax.shard_map(
        on_device,
        mesh=mesh,
        in_specs=(
            P("fsdp", "dp", None),
            P(),
            P(),
            P("dp", None),
            P("fsdp", "dp"),
            P("fsdp", None),
            P("fsdp", None),
            P("fsdp", "dp", None),
            P(),
            P(),
            P(),
            P(None, "fsdp"),
            P(),
            P(),
        ),
        out_specs=P("fsdp", "dp", None, None),
        check_vma=False,
    )
```

profile of v0, /device:TPU:1, one launch (start us, length us, event | category | flops | bytes accessed | tf_op | source)
XLA Modules:
  0.0 244.5 jit_solution(13051680516002244382)
XLA Ops:
  11.3 2.9 %scatter_custom_fusion = s32[640]{0:T(1024)S(1)} fusion(s32[320]{0:T(512)S(1)} %fusion.53, s32[320]{0:T(512)S(1)} %sub.68, s32[]{:T(128)} %constant.135.clone.1), kind=kCustom, calls=%fused_computation.93 | custom fusion | bytes 2564 | tf_op jit(solution)/shard_map/scatter | solution.py:94
  15.0 14.5 %all-to-all-start = ((s32[64,1,10]{2,1,0:T(1,128)}), s32[64,1,10]{2,1,0:T(1,128)S(1)}, u32[]{:S(2)}, u32[]{:S(2)}) async-start(s32[64,1,10]{2,1,0:T(1,128)} %bitcast.18), calls=%async_computation | async-start | bytes 65536 | tf_op jit(solution)/shard_map/all_to_all | solution.py:103
  30.2 1.4 convert_reduce_fusion
  31.7 1.6 fusion.16
  33.3 73.6 %all-gather.6.cloned.1.call-done = bf16[64,22,512]{2,1,0:T(8,128)(2,1)} async-done(((bf16[1,22,512]{2,1,0:T(8,128)(2,1)}), bf16[64,22,512]{2,1,0:T(8,128)(2,1)}) %all-gather.6.cloned.1.call-update) | async-done | bytes 1441808 | tf_op jit(solution)/shard_map/all_gather | solution.py:87
  106.9 2.3 reshape.413
  110.1 1.9 scatter_custom_fusion.1
  112.1 1.2 reshape.383
  113.2 6.9 %all-to-all-start.1 = ((bf16[64,10,512]{2,1,0:T(8,128)(2,1)}), bf16[64,10,512]{2,1,0:T(8,128)(2,1)S(1)}, u32[]{:S(2)}, u32[]{:S(2)}) async-start(bf16[64,10,512]{2,1,0:T(8,128)(2,1)} %reshape.383), calls=%async_computation.1 | async-start | bytes 2097152 | tf_op jit(solution)/shard_map/all_to_all | solution.py:96
  122.1 26.2 %all-to-all-done.1 = bf16[64,10,512]{2,1,0:T(8,128)(2,1)S(1)} async-done(((bf16[64,10,512]{2,1,0:T(8,128)(2,1)}), bf16[64,10,512]{2,1,0:T(8,128)(2,1)S(1)}, u32[]{:S(2)}, u32[]{:S(2)}) %all-to-all-start.1) | async-done | bytes 655392 | tf_op jit(solution)/shard_map/all_to_all | solution.py:96
  148.6 6.0 %scatter_custom_fusion.2 = bf16[1024,512]{1,0:T(8,128)(2,1)S(1)} fusion(s32[640]{0:T(1024)S(1)} %fusion.39, bf16[640,512]{1,0:T(8,128)(2,1)S(1)} %reshape.408, bf16[]{:T(256)} %constant.134.clone.1), kind=kCustom, calls=%fused_computation.52 | custom fusion | bytes 1048578 | tf_op jit(solution)/shard_map/scatter | solution.py:114
  154.6 9.0 %fusion.20 = f32[1024]{0:T(1024)S(1)} fusion(bf16[1024,512]{1,0:T(8,128)(2,1)S(1)} %scatter_custom_fusion.2, f32[512]{0:T(512)S(1)} %fusion.46, f32[1024]{0:T(1024)S(1)} %bitcast.102, f32[512]{0:T(512)S(1)} %copy-done.12, pred[1024]{0:T(1024)(128)(4,1)S(1)} %lt.81, pred[512]{0:T(512)(128)(4,1)S(1)} %fusion.40), kind=kLoop, calls=%fused_computation.38 | loop fusion | flops 3144704 | bytes 1062400 | tf_op jit(solution)/shard_map/reduce_sum | solution.py:11
  163.6 9.6 %multiply_reduce_fusion = f32[1024]{0:T(1024)S(1)} fusion(bf16[1024,512]{1,0:T(8,128)(2,1)S(1)} %scatter_custom_fusion.2, f32[1024]{0:T(1024)S(1)} %broadcast_multiply_fusion, f32[512]{0:T(512)S(1)} %fusion.46, f32[1024]{0:T(1024)S(1)} %bitcast.103, f32[512]{0:T(512)S(1)} %copy-done.12, pred[1024]{0:T(1024)(128)(4,1)S(1)} %lt.81, pred[512]{0:T(512)(128)(4,1)S(1)} %fusion.40), kind=kLoop, calls=%fused_computation.29 | loop fusion | flops 4193280 | bytes 1066496 | tf_op jit(solution)/shard_map/reduce_sum | solution.py:13
  173.3 13.0 %convolution_convert_fusion.1 = bf16[1024,1536]{1,0:T(8,128)(2,1)} fusion(bf16[512,1536]{1,0:T(8,128)(2,1)} %all-gather.4.cloned.1.call-done, bf16[1024,512]{1,0:T(8,128)(2,1)S(1)} %scatter_custom_fusion.2, f32[512]{0:T(512)S(1)} %copy-done.10, f32[512]{0:T(512)S(1)} %copy-done.11, f32[1024]{0:T(1024)S(1)} %add_rsqrt_fusion, ...), kind=kOutput, calls=%fused_computation.20 | convolution fusion | flops 1617428480 | bytes 5789184 | tf_op jit(solution)/shard_map/dot_general | solution.py:129
  186.3 40.6 %while.21 = (s32[]{:T(128)}, bf16[2,512,512]{2,1,0:T(8,128)(2,1)}, bf16[2,512,1536]{2,1,0:T(8,128)(2,1)}, s32[]{:T(128)}, s32[]{:T(128)}, /*index=5*/s32[]{:T(128)}) while((s32[]{:T(128)}, bf16[2,512,512]{2,1,0:T(8,128)(2,1)}, bf16[2,512,1536]{2,1,0:T(8,128)(2,1)}, s32[]{:T(128)}, s32[]{:T(128)}, /*index=5*/s32[]{:T(128)}) %tuple.60), condition=%wide.region_16.17_spmd, body=%wide.region_11.16_spmd.sunk | while | flops 68975616 | bytes 23343360 | solution.py:144
  186.3 2.7 %constant_dynamic-slice_fusion.2 = bf16[1,512,1536]{2,1,0:T(8,128)(2,1)} fusion(bf16[2,512,1536]{2,1,0:T(8,128)(2,1)} %get-tuple-element.202, s32[]{:T(128)} %get-tuple-element.194), kind=kLoop, calls=%fused_computation.19.clone.1 | loop fusion | bytes 3145732 | tf_op jit(solution)/shard_map/while/body/jit(dynamic_index_in_dim)/dynamic_slice | solution.py:144
  189.0 1.7 copy.45
  191.6 13.7 %while.22 = (s32[]{:T(128)}, bf16[8,512,64]{1,2,0:T(8,128)(2,1)S(1)}, bf16[8,512,64]{1,2,0:T(8,128)(2,1)S(1)}, bf16[8,512,64]{1,2,0:T(8,128)(2,1)S(1)}, bf16[8,512,64]{1,2,0:T(8,128)(2,1)}, /*index=5*/s32[]{:T(128)}) while((s32[]{:T(128)}, bf16[8,512,64]{1,2,0:T(8,128)(2,1)S(1)}, bf16[8,512,64]{1,2,0:T(8,128)(2,1)S(1)}, ...), condition=%wide.region_15.15_spmd, body=%wide.region_12.14_spmd.sunk | while | flops 68975616 | bytes 3420229 | solution.py:40
  192.1 1.1 fusion.74
  197.3 1.1 fusion.74
  206.6 2.6 %constant_dynamic-slice_fusion.2 = bf16[1,512,1536]{2,1,0:T(8,128)(2,1)} fusion(bf16[2,512,1536]{2,1,0:T(8,128)(2,1)} %get-tuple-element.202, s32[]{:T(128)} %get-tuple-element.194), kind=kLoop, calls=%fused_computation.19.clone.1 | loop fusion | bytes 3145732 | tf_op jit(solution)/shard_map/while/body/jit(dynamic_index_in_dim)/dynamic_slice | solution.py:144
  209.3 1.7 copy.45
  211.9 13.7 %while.22 = (s32[]{:T(128)}, bf16[8,512,64]{1,2,0:T(8,128)(2,1)S(1)}, bf16[8,512,64]{1,2,0:T(8,128)(2,1)S(1)}, bf16[8,512,64]{1,2,0:T(8,128)(2,1)S(1)}, bf16[8,512,64]{1,2,0:T(8,128)(2,1)}, /*index=5*/s32[]{:T(128)}) while((s32[]{:T(128)}, bf16[8,512,64]{1,2,0:T(8,128)(2,1)S(1)}, bf16[8,512,64]{1,2,0:T(8,128)(2,1)S(1)}, ...), condition=%wide.region_15.15_spmd, body=%wide.region_12.14_spmd.sunk | while | flops 68975616 | bytes 3420229 | solution.py:40
  226.9 10.8 %add_convert_fusion = bf16[1024,512]{1,0:T(8,128)(2,1)} fusion(bf16[1024,512]{1,0:T(8,128)(2,1)} %bitcast.110, bf16[512,512]{1,0:T(8,128)(2,1)S(1)} %copy-done, bf16[1024,512]{1,0:T(8,128)(2,1)} %copy-done.2, f32[512]{0:T(512)S(1)} %copy-done.13, f32[512]{0:T(512)S(1)} %fusion.46, f32[1024]{0:T(1024)S(1)} %bitcast.105, f32[512]{0:T(512)S(1)} %copy-done.12, ...), kind=kOutput, calls=%fused_computation.27 | convolution fusion | flops 541065216 | bytes 3681792 | tf_op jit(solution)/shard_map/dot_general | solution.py:145
  (120 shorter events, 38.4 us)
Async XLA Ops:
  6.5 220.4 %copy-start = (bf16[512,512]{1,0:T(8,128)(2,1)S(1)}, bf16[512,512]{1,0:T(8,128)(2,1)}, u32[]{:S(2)}) copy-start(bf16[512,512]{1,0:T(8,128)(2,1)} %param.30) | copy-start | bytes 1572868
  6.5 100.4 %all-gather.6.cloned.1.call-start = ((), (), s32[]{:S(2)}) async-start(), calls=%async_computation.3 | async-start | bytes 1597440 | tf_op jit(solution)/shard_map/all_gather | solution.py:87
  15.0 98.2 %all-to-all-start = ((s32[64,1,10]{2,1,0:T(1,128)}), s32[64,1,10]{2,1,0:T(1,128)S(1)}, u32[]{:S(2)}, u32[]{:S(2)}) async-start(s32[64,1,10]{2,1,0:T(1,128)} %bitcast.18), calls=%async_computation | async-start | bytes 65536 | tf_op jit(solution)/shard_map/all_to_all | solution.py:103
  29.5 143.8 %all-gather.4.cloned.1.call-start = ((), (), s32[]{:S(2)}) async-start(), calls=%async_computation.2 | async-start | bytes 1703936 | tf_op jit(solution)/shard_map/all_gather | solution.py:131
  31.6 77.7 %copy-start.1 = (bf16[1,320,1408]{2,1,0:T(8,128)(2,1)S(1)}, bf16[1,320,1408]{2,1,0:T(8,128)(2,1)}, u32[]{:S(2)}) copy-start(bf16[1,320,1408]{2,1,0:T(8,128)(2,1)} %param.18) | copy-start | bytes 2703364
  31.6 77.7 %copy-start.8 = (f32[1408]{0:T(1024)S(1)}, f32[1408]{0:T(1024)}, u32[]{:S(2)}) copy-start(f32[1408]{0:T(1024)} %param.20) | copy-start | bytes 16900
  31.6 77.7 %copy-start.9 = (f32[1408]{0:T(1024)S(1)}, f32[1408]{0:T(1024)}, u32[]{:S(2)}) copy-start(f32[1408]{0:T(1024)} %param.19) | copy-start | bytes 16900
  110.1 10.1 %copy-start.4 = (s32[1,128]{1,0:T(1,128)S(1)}, s32[1,128]{1,0:T(1,128)}, u32[]{:S(2)}) copy-start(s32[1,128]{1,0:T(1,128)} %param.23) | copy-start | bytes 1540
  110.1 10.1 %copy-start.5 = (s32[1,128]{1,0:T(1,128)S(1)}, s32[1,128]{1,0:T(1,128)}, u32[]{:S(2)}) copy-start(s32[1,128]{1,0:T(1,128)} %param.24) | copy-start | bytes 1540
  110.1 10.4 %copy-start.3 = (s32[1,2,512]{2,1,0:T(2,128)S(1)}, s32[1,2,512]{2,1,0:T(2,128)}, u32[]{:S(2)}) copy-start(s32[1,2,512]{2,1,0:T(2,128)} %param.25) | copy-start | bytes 12292
  113.2 41.3 %copy-start.12 = (f32[512]{0:T(512)S(1)}, f32[512]{0:T(512)}, u32[]{:S(2)}) copy-start(f32[512]{0:T(512)} %param.26) | copy-start | bytes 6148
  113.2 35.1 %all-to-all-start.1 = ((bf16[64,10,512]{2,1,0:T(8,128)(2,1)}), bf16[64,10,512]{2,1,0:T(8,128)(2,1)S(1)}, u32[]{:S(2)}, u32[]{:S(2)}) async-start(bf16[64,10,512]{2,1,0:T(8,128)(2,1)} %reshape.383), calls=%async_computation.1 | async-start | bytes 2097152 | tf_op jit(solution)/shard_map/all_to_all | solution.py:96
  154.5 31.8 %copy-start.2 = (bf16[1024,512]{1,0:T(8,128)(2,1)}, bf16[1024,512]{1,0:T(8,128)(2,1)S(1)}, u32[]{:S(2)}) copy-start(bf16[1024,512]{1,0:T(8,128)(2,1)S(1)} %scatter_custom_fusion.2) | copy-start | bytes 3145732
  154.6 18.7 %copy-start.10 = (f32[512]{0:T(512)S(1)}, f32[512]{0:T(512)}, u32[]{:S(2)}) copy-start(f32[512]{0:T(512)} %param.28) | copy-start | bytes 6148
  154.6 18.7 %copy-start.11 = (f32[512]{0:T(512)S(1)}, f32[512]{0:T(512)}, u32[]{:S(2)}) copy-start(f32[512]{0:T(512)} %param.27) | copy-start | bytes 6148
  186.3 40.6 %copy-start.13 = (f32[512]{0:T(512)S(1)}, f32[512]{0:T(512)}, u32[]{:S(2)}) copy-start(f32[512]{0:T(512)} %param.31) | copy-start | bytes 6148
  191.6 14.0 %copy-start.6 = (bf16[2,512,512]{2,1,0:T(8,128)(2,1)S(1)}, bf16[2,512,512]{2,1,0:T(8,128)(2,1)}, u32[]{:S(2)}) copy-start(bf16[2,512,512]{2,1,0:T(8,128)(2,1)} %get-tuple-element.195) | copy-start | bytes 3145732 | tf_op jit(solution)/shard_map/while
  205.6 1.0 copy-start.7
  211.9 14.0 %copy-start.6 = (bf16[2,512,512]{2,1,0:T(8,128)(2,1)S(1)}, bf16[2,512,512]{2,1,0:T(8,128)(2,1)}, u32[]{:S(2)}) copy-start(bf16[2,512,512]{2,1,0:T(8,128)(2,1)} %get-tuple-element.195) | copy-start | bytes 3145732 | tf_op jit(solution)/shard_map/while
  225.9 1.0 copy-start.7
Sparse Core Ops, SparseCore 0:
  11.3 95.6 all-gather.5
  109.2 53.6 all-gather.3
where the time goes:
time: 246 us; the launch traced here: 245 us
  waiting for transfers between devices  101 us (41%)
  matrix products  48.6 us (20%)
  local copies, waits for them, and re-layouts  29.9 us (12%)
  other arithmetic  29.2 us (12%)
  starting transfers between devices  21.4 us (9%)
  between operations  13.7 us (6%)
    all_gather x1, waiting for transfers between devices, on_device(): lax.all_gather(w_e2d, 'dp', axis=0, tiled=True)  73.6 us
    all_to_all x1, waiting for transfers between devices, on_device(): lax.all_to_all(sent.reshape(group_size, peer_rows, payload.shape[1]), 'dp...  26.2 us
    dot_general x16, matrix products, one_head(): jnp.dot(weights, value_h, preferred_element_type=jnp.float32)  18.4 us
    all_to_all x1, starting transfers between devices, on_device(): lax.all_to_all(sent_rank.reshape(group_size, peer_rows), 'dp', split_axis...  14.5 us
    dot_general x1, matrix products, on_device(): jnp.dot(dec_normed, lax.all_gather(w_qkv, 'fsdp', axis=1, tiled=True), pr...  13 us
    reduce_sum x2, other arithmetic, layer_norm(): spread = jnp.mean(centred * centred, axis=-1, keepdims=True)  11.3 us
    dot_general x1, matrix products, on_device(): jnp.dot(attended.reshape(-1, dec_width), w_proj, preferred_element_type=j...  10.8 us
    reduce_sum x2, other arithmetic, layer_norm(): average = jnp.mean(values, axis=-1, keepdims=True)  10.4 us
  transfers between devices with their start and end apart: 4, of which 2 were waited for; matrix products, arithmetic and copies ran while one was open for 18% of the time, Pallas kernels for 0%

commit v1 on v0

v1 whole, which is shorter than its diff:
```python
import math

import jax
import jax.numpy as jnp
import numpy as np
from jax import lax
from jax.experimental import pallas as pl
from jax.experimental.pallas import tpu as pltpu
from jax.sharding import Mesh, PartitionSpec as P

DP = ("y", "x", "core")
PLANE = ("y", "x")
HEADS = 8
HEAD = 64
VMAX = 320
NDEV = 64
PER = 5
EPS = 1e-06
MIB = 1 << 20
BF = jnp.bfloat16
F32 = jnp.float32


def iota(shape, dim):
    return lax.broadcasted_iota(jnp.int32, shape, dim)


def prep_kernel(ids_ref, enc_ref, gain_ref, bias_ref, counts_ref, owner_ref, normed_ref, pick_ref, info_ref):
    residue = ids_ref[0]
    my_index = ids_ref[1]
    core = ids_ref[2]
    counts = counts_ref[...].astype(F32)
    row_id = iota((128, 128), 0)
    col_id = iota((128, 128), 1)
    counts_col = jnp.sum(jnp.where(row_id == col_id, counts, 0.0), axis=1, keepdims=True)
    first = jnp.sum(jnp.where(row_id < col_id, counts_col, 0.0), axis=0, keepdims=True)
    owner = owner_ref[...]
    start = jnp.floor((first + (63 - residue).astype(F32)) * (1.0 / 64.0))
    place = iota((640, 128), 0)
    dest = (place * 6554) >> 16
    rest = place - 10 * dest
    slot = 2 * dest + (rest & 1)
    target = jnp.sum(jnp.where(owner == slot, start, 0.0), axis=1, keepdims=True)
    target = target.astype(jnp.int32) + (rest >> 1)[:, :1]
    pick_ref[...] = jnp.where(iota((640, VMAX), 1) == target, 1.0, 0.0).astype(BF)
    line = iota((8, 128), 0)
    mine = 2 * my_index + (line & 1)
    held = jnp.where(line < 2, first, counts)
    info = jnp.sum(jnp.where(owner == mine, held, 0.0), axis=1, keepdims=True)
    info_ref[...] = jnp.broadcast_to(info, (8, 128)).astype(jnp.int32)
    values = enc_ref[...].astype(F32)
    average = jnp.mean(values, axis=1, keepdims=True)
    centred = values - average
    spread = jnp.mean(centred * centred, axis=1, keepdims=True)
    normed = (centred * lax.rsqrt(spread + EPS) * gain_ref[...] + bias_ref[...]).astype(BF)
    for half in range(2):
        side = core if half == 0 else 1 - core
        for tile, (low, high) in enumerate(((0, 512), (384, 1024), (896, 1408))):
            size = high - low
            column = iota((1, 256), 1) + 256 * tile
            block = (column * 2731) >> 16
            inner = column - 24 * block
            source = jnp.where(inner < 22, 44 * block + 22 * side + inner - low, -1)
            spread_out = jnp.where(iota((size, 256), 0) == source, 1.0, 0.0).astype(BF)
            normed_ref[half, :, 256 * tile : 256 * (tile + 1)] = jnp.dot(
                normed[:, low:high], spread_out, preferred_element_type=F32
            ).astype(BF)


def embed_kernel(normed_ref, own_ref, other_ref, pick_ref, out_ref, rows_ref):
    embedded = jnp.dot(normed_ref[0], own_ref[...], preferred_element_type=F32)
    embedded += jnp.dot(normed_ref[1], other_ref[...], preferred_element_type=F32)
    embedded = embedded.astype(BF)
    packed = jnp.dot(pick_ref[...], embedded, preferred_element_type=F32)
    for part in range(4):
        rows_ref[pl.ds(part, 640, stride=4), :] = packed[:, 128 * part : 128 * (part + 1)]
    out_ref[...] = rows_ref[...].astype(BF)


def decode_kernel(
    recv_ref, seat_ref, base_ref, gain_ref, bias_ref, wqk_ref, wvt_ref, wproj_ref, pbias_ref,
    out_ref, rows_ref, x_ref, vt_ref, att_ref,
):
    clip = pl.program_id(0)

    @pl.when(clip == 0)
    def _():
        rows_ref[...] = recv_ref[...].astype(F32)
        vt_ref[:, HEAD:, :] = jnp.ones((HEADS, 16, 512), BF)

    tokens = jnp.concatenate(
        [rows_ref[pl.ds(4 * clip + part, VMAX, stride=8), :] for part in range(4)], axis=1
    ).astype(BF)
    x_ref[:VMAX, :] = base_ref[:VMAX, :] + jnp.dot(seat_ref[0], tokens, preferred_element_type=F32)
    x_ref[VMAX:, :] = base_ref[VMAX:, :]
    values = x_ref[...]
    average = jnp.mean(values, axis=1, keepdims=True)
    centred = values - average
    spread = jnp.mean(centred * centred, axis=1, keepdims=True)
    normed = (centred * lax.rsqrt(spread + EPS) * gain_ref[...] + bias_ref[...]).astype(BF)
    across = (((1,), (1,)), ((), ()))
    queries = jnp.dot(normed, wqk_ref[:, :512], preferred_element_type=F32)
    queries = (queries * (HEAD**-0.5 * math.log2(math.e))).astype(BF)
    keys = jnp.dot(normed, wqk_ref[:, 512:], preferred_element_type=F32).astype(BF)
    vt = lax.dot_general(wvt_ref[...], normed, across, preferred_element_type=F32).astype(BF)
    for head in range(HEADS):
        vt_ref[head, :HEAD, :] = vt[HEAD * head : HEAD * (head + 1), :]
    left = iota((512, 128), 1) < HEAD
    zero = jnp.zeros((512, 128), BF)
    for head in range(HEADS):
        pair = slice(128 * (head // 2), 128 * (head // 2 + 1))
        key = keys[:, pair]
        key = jnp.where(left, key, zero) if head % 2 == 0 else jnp.where(left, zero, key)
        scores = lax.dot_general(key, queries[:, pair], across, preferred_element_type=F32)
        top = jnp.max(scores, axis=0, keepdims=True)
        weights = jnp.exp2(scores - top).astype(BF)
        mixed = jnp.dot(vt_ref[head], weights, preferred_element_type=F32)
        att_ref[HEAD * head : HEAD * (head + 1), :] = (
            mixed[:HEAD] * (1.0 / mixed[HEAD : HEAD + 1])
        ).astype(BF)
    result = lax.dot_general(
        att_ref[...], wproj_ref[...], (((0,), (0,)), ((), ())), preferred_element_type=F32
    )
    out_ref[0] = (x_ref[...] + result + pbias_ref[...]).astype(BF)


def whole(shape):
    return pl.BlockSpec(shape, lambda *_: (0,) * len(shape))


def on_device(
    enc_out, norm_gain, norm_bias, w_e2d, token_index, counts, owner, dec_tubes,
    mask_token, dec_gain, dec_bias, w_qkv, w_proj, proj_bias,
):
    my_index = lax.axis_index(DP).astype(jnp.int32)
    core = lax.axis_index("core").astype(jnp.int32)
    residue = token_index[0, 0] % NDEV
    w_full = lax.all_gather(w_qkv, "fsdp", axis=1, tiled=True)

    mark = jnp.broadcast_to(residue.astype(BF), (2, 512))
    shard = jnp.concatenate([w_e2d, mark], axis=0)
    gathered = lax.all_to_all(
        jnp.broadcast_to(shard[None], (32, 24, 512)), PLANE, 0, 0, tiled=True
    )
    own = gathered.reshape(768, 512)
    other = lax.ppermute(own, "core", [(0, 1), (1, 0)])

    ids = jnp.stack([residue, my_index, core])
    normed, pick, info = pl.pallas_call(
        prep_kernel,
        out_shape=(
            jax.ShapeDtypeStruct((2, VMAX, 768), BF),
            jax.ShapeDtypeStruct((640, VMAX), BF),
            jax.ShapeDtypeStruct((8, 128), jnp.int32),
        ),
        in_specs=[pl.BlockSpec(memory_space=pltpu.SMEM)] + [pl.BlockSpec(memory_space=pltpu.VMEM)] * 5,
        compiler_params=pltpu.CompilerParams(vmem_limit_bytes=24 * MIB),
        cost_estimate=pl.CostEstimate(flops=4_000_000_000, bytes_accessed=4_000_000, transcendentals=0),
        name="prep",
    )(ids, enc_out[0], norm_gain[None], norm_bias[None], counts, owner)

    sent = pl.pallas_call(
        embed_kernel,
        out_shape=jax.ShapeDtypeStruct((2560, 128), BF),
        scratch_shapes=[pltpu.VMEM((2560, 128), F32)],
        compiler_params=pltpu.CompilerParams(vmem_limit_bytes=24 * MIB),
        cost_estimate=pl.CostEstimate(flops=1_000_000_000, bytes_accessed=4_000_000, transcendentals=0),
        name="embed",
    )(normed, own, other, pick)
    received = lax.all_to_all(sent.reshape(NDEV, 40, 128), DP, 0, 0, tiled=True).reshape(2560, 128)

    column = np.arange(512)
    rate = np.power(10000.0, -(2 * (column // 2)) / 512.0).astype(np.float32)
    phase = np.where(column % 2 == 0, 0.0, math.pi / 2).astype(np.float32)
    codes = jnp.sin(dec_tubes[0].astype(F32)[..., None] * rate + phase)
    position = jnp.arange(512, dtype=jnp.int32)
    visible = position[None, :] < info[2:4, :1]
    base = jnp.where(visible[..., None], 0.0, mask_token) + codes

    own_mark = own.reshape(32, 24, 512)[:, 22, 0]
    other_mark = other.reshape(32, 24, 512)[:, 22, 0]
    first_mark = jnp.where(core == 0, own_mark, other_mark)
    second_mark = jnp.where(core == 0, other_mark, own_mark)
    marks = jnp.stack([first_mark, second_mark], axis=1).reshape(NDEV).astype(jnp.int32)
    offered = (marks[:, None] * 8 + jnp.arange(PER, dtype=jnp.int32)).reshape(NDEV * PER)
    rank = position[:VMAX]
    wanted = ((info[0:2, :1] + rank[None, :]) & 63) * 8 + (rank >> 6)[None, :]
    wanted = jnp.where(rank[None, :] < info[2:4, :1], wanted, -1)
    seat = (wanted[:, :, None] == offered[None, None, :]).astype(BF)

    return pl.pallas_call(
        decode_kernel,
        grid=(2,),
        out_shape=jax.ShapeDtypeStruct((1, 2, 512, 512), BF),
        in_specs=[
            whole((2560, 128)),
            pl.BlockSpec((1, VMAX, VMAX), lambda clip: (clip, 0, 0)),
            pl.BlockSpec((512, 512), lambda clip: (clip, 0)),
            whole((1, 512)),
            whole((1, 512)),
            whole((512, 1024)),
            whole((512, 512)),
            whole((512, 512)),
            whole((1, 512)),
        ],
        out_specs=pl.BlockSpec((None, 1, 512, 512), lambda clip: (0, clip, 0, 0)),
        scratch_shapes=[
            pltpu.VMEM((2560, 128), F32),
            pltpu.VMEM((512, 512), F32),
            pltpu.VMEM((HEADS, HEAD + 16, 512), BF),
            pltpu.VMEM((512, 512), BF),
        ],
        compiler_params=pltpu.CompilerParams(vmem_limit_bytes=32 * MIB),
        cost_estimate=pl.CostEstimate(flops=4_000_000_000, bytes_accessed=8_000_000, transcendentals=4_000_000),
        name="decode",
    )(
        received, seat, base.reshape(1024, 512), dec_gain[None], dec_bias[None],
        w_full[:, :1024], w_full[:, 1024:].T, w_proj, proj_bias[None],
    )


def solution(mesh):
    grid = Mesh(np.asarray(mesh.devices).reshape(8, 4, 2, 12), (*DP, "fsdp"))
    return jax.shard_map(
        on_device,
        mesh=grid,
        in_specs=(
            P("fsdp", DP, None), P(), P(), P(DP, None), P("fsdp", DP), P("fsdp", None), P("fsdp", None),
            P("fsdp", DP, None), P(), P(), P(), P(None, "fsdp"), P(), P(),
        ),
        out_specs=P("fsdp", DP, None, None),
        check_vma=False,
    )
```

time: 246 us -> 120 us (0.49)
  the two profiles are of different devices: /device:TPU:1 before, /device:TPU:2 now
where the time goes in v1:
time: 120 us; the launch traced here: 119 us
  waiting for transfers between devices  42.9 us (36%)
  starting transfers between devices  21.1 us (18%)
  Pallas kernels  16.4 us (14%)
  between operations  15.6 us (13%)
  local copies, waits for them, and re-layouts  13.2 us (11%)
  other arithmetic  10.2 us (8%)
    all_gather x1, waiting for transfers between devices, on_device(): w_full = lax.all_gather(w_qkv, 'fsdp', axis=1, tiled=True)  24.3 us
    all_to_all x1, waiting for transfers between devices, on_device(): lax.all_to_all(jnp.broadcast_to(shard[None], (32, 24, 512)), PLANE, 0, 0,...  18.6 us
    all_to_all x1, starting transfers between devices, on_device(): lax.all_to_all(jnp.broadcast_to(shard[None], (32, 24, 512)), PLANE, 0, 0,...  13.1 us
    pallas_call x1, Pallas kernels, on_device(): pl.pallas_call(decode_kernel, grid=(2,), out_shape=jax.ShapeDtypeStruct((...  12.4 us
    add x1, other arithmetic, on_device(): base = jnp.where(visible[..., None], 0.0, mask_token) + codes  7.79 us
    all_to_all x1, starting transfers between devices, on_device(): lax.all_to_all(sent.reshape(NDEV, 40, 128), DP, 0, 0, tiled=True)  6.08 us
    slice x2, local copies, waits for them, and re-layouts, on_device(): w_full[:, :1024]  4.58 us
    unnamed x32, local copies, waits for them, and re-layouts  4.1 us
  transfers between devices with their start and end apart: 4, of which 2 were waited for; matrix products, arithmetic and copies ran while one was open for 14% of the time, Pallas kernels for 3%

profile of v1, /device:TPU:2, one launch (start us, length us, event | category | flops | bytes accessed | tf_op | source)
XLA Modules:
  0.0 119.5 jit_solution(7031066680927395157)
XLA Ops:
  6.6 1.3 %slice.33 = s32[1,1]{1,0:T(1,128)} slice(s32[1,320]{1,0:T(1,128)} %param.20), slice={[0:1], [0:1]} | slice | bytes 8 | tf_op jit(solution)/shard_map/slice | solution.py:137
  9.8 0.7 concatenate.3
  10.5 0.9 broadcast_in_dim.55
  11.4 13.1 %all-to-all-start = ((bf16[32,24,512]{2,1,0:T(8,128)(2,1)}), bf16[32,24,512]{2,1,0:T(8,128)(2,1)S(1)}, u32[]{:S(2)}, u32[]{:S(2)}) async-start(bf16[32,24,512]{2,1,0:T(8,128)(2,1)} %broadcast_in_dim.55), calls=%async_computation | async-start | bytes 1572864 | tf_op jit(solution)/shard_map/all_to_all | solution.py:142
  24.6 0.8 copy.31
  25.5 18.6 %all-to-all-done = bf16[32,24,512]{2,1,0:T(8,128)(2,1)S(1)} async-done(((bf16[32,24,512]{2,1,0:T(8,128)(2,1)}), bf16[32,24,512]{2,1,0:T(8,128)(2,1)S(1)}, u32[]{:S(2)}, u32[]{:S(2)}) %all-to-all-start) | async-done | bytes 786464 | tf_op jit(solution)/shard_map/all_to_all | solution.py:142
  44.2 1.9 %collective-permute-start = (bf16[768,512]{1,0:T(8,128)(2,1)S(1)}, bf16[768,512]{1,0:T(8,128)(2,1)S(1)}, u32[]{:S(2)}, u32[]{:S(2)}) collective-permute-start(bf16[768,512]{1,0:T(8,128)(2,1)S(1)} %bitcast.19), channel_id=1, source_target_pairs={{0,12},{12,0},{1,13},{13,1},{2,14},{14,2},{3,15},{15,3},{4,16},{16... | collective-permute-start | bytes 2359304 | tf_op jit(solution)/shard_map/ppermute | solution.py:146
  46.1 2.0 %prep.1 = (bf16[2,320,768]{2,1,0:T(8,128)(2,1)S(1)}, bf16[640,320]{1,0:T(8,128)(2,1)S(1)}, s32[8,128]{1,0:T(8,128)S(1)}) custom-call(s32[3]{0:T(128)S(1)} %pad_add_fusion.ids_ref, bf16[320,1408]{1,0:T(8,128)(2,1)S(1)} %bitcast.23, f32[1,1408]{1,0:T(1,128)S(1)} %broadcast_in_dim.32.gain_ref, f32[1,1408]{1,0:T(1,128)S(1)} %broadcast_in_dim.54.bias_ref, ...), custom_call_target="tpu_custom_call" | custom-call | flops 4000000000 | bytes 4000000 | tf_op jit(solution)/shard_map/prep/pallas_call | solution.py:149
  48.1 0.1 slice_reduce_fusion.1
  48.4 2.0 %embed.1 = bf16[2560,128]{1,0:T(8,128)(2,1)} custom-call(bf16[2,320,768]{2,1,0:T(8,128)(2,1)S(1)} %get-tuple-element.8.normed_ref, bf16[768,512]{1,0:T(8,128)(2,1)S(1)} %bitcast.20, bf16[768,512]{1,0:T(8,128)(2,1)S(1)} %collective-permute-done.other_ref, bf16[640,320]{1,0:T(8,128)(2,1)S(1)} %get-tuple-element.9.pick_ref), custom_call_target="tpu_custom_call" | custom-call | flops 1000000000 | bytes 4000000 | tf_op jit(solution)/shard_map/embed/pallas_call | solution.py:162
  50.5 6.1 %all-to-all-start.1 = ((bf16[64,40,128]{2,1,0:T(8,128)(2,1)}), bf16[64,40,128]{2,1,0:T(8,128)(2,1)S(1)}, u32[]{:S(2)}, u32[]{:S(2)}) async-start(bf16[64,40,128]{2,1,0:T(8,128)(2,1)} %bitcast.6), calls=%async_computation.1 | async-start | bytes 1310720 | tf_op jit(solution)/shard_map/all_to_all | solution.py:170
  56.6 7.8 %sine_add_fusion.base_ref = f32[1024,512]{1,0:T(8,128)S(1)} fusion(f32[512]{0:T(512)} %constant.47.clone, f32[512]{0:T(512)} %constant.46.clone, f32[1024]{0:T(1024)S(1)} %bitcast.27, f32[512]{0:T(512)S(1)} %copy-done.14, pred[1024]{0:T(1024)(128)(4,1)S(1)} %lt.52), kind=kLoop, calls=%fused_computation | loop fusion | flops 2097152 | bytes 2108416 | tf_op jit(solution)/shard_map/add | solution.py:178
  64.4 1.2 fusion
  65.7 0.1 mul.50
  65.9 0.1 add.82
  66.0 0.9 compare_convert_fusion.seat_ref
  67.0 24.3 %all-gather.2.cloned.1.call-done = bf16[512,1536]{0,1:T(8,128)(2,1)} async-done(((bf16[512,128]{0,1:T(8,128)(2,1)}), bf16[512,1536]{0,1:T(8,128)(2,1)}) %all-gather.2.cloned.1.call-update) | async-done | bytes 1572880 | tf_op jit(solution)/shard_map/all_gather | solution.py:138
  91.3 2.3 %slice.45 = bf16[512,1024]{0,1:T(8,128)(2,1)} slice(bf16[512,1536]{0,1:T(8,128)(2,1)} %all-gather.2.cloned.1.call-done), slice={[0:512], [0:1024]} | slice | bytes 2097152 | tf_op jit(solution)/shard_map/slice | solution.py:218
  93.5 2.3 %copy.32.wqk_ref = bf16[512,1024]{1,0:T(8,128)(2,1)} copy(bf16[512,1024]{0,1:T(8,128)(2,1)} %slice.45) | data formatting | bytes 2097152 | tf_op jit(solution)/shard_map/slice | solution.py:218
  95.8 1.1 slice_bitcast_fusion.wvt_ref
  97.0 1.2 %copy-done = bf16[512,1024]{1,0:T(8,128)(2,1)S(1)} copy-done((bf16[512,1024]{1,0:T(8,128)(2,1)S(1)}, bf16[512,1024]{1,0:T(8,128)(2,1)}, u32[]{:S(2)}) %copy-start) | copy-done | bytes 1048600
  98.2 1.0 copy-done.2
  99.2 1.0 copy-done.4
  100.3 12.4 %decode.1 = bf16[1,2,512,512]{3,2,1,0:T(8,128)(2,1)} custom-call(bf16[2560,128]{1,0:T(8,128)(2,1)S(1)} %bitcast.22, bf16[2,320,320]{2,1,0:T(8,128)(2,1)S(1)} %copy-done.2, f32[1024,512]{1,0:T(8,128)S(1)} %sine_add_fusion.base_ref, f32[1,512]{1,0:T(1,128)S(1)} %bitcast.24, f32[1,512]{1,0:T(1,128)S(1)} %bitcast.25, bf16[512,1024]{1,0:T(8,128)(2,1)S(1)} %copy-done, ...), custom_call_target="tpu_custom_call" | custom-call | flops 4000000000 | bytes 8000000 | tf_op jit(solution)/shard_map/decode/pallas_call | solution.py:191
  (44 shorter events, 0.6 us)
Async XLA Ops:
  6.5 18.1 %copy-start.10 = (bf16[512,128]{1,0:T(8,128)(2,1)S(1)}, bf16[512,128]{1,0:T(8,128)(2,1)}, u32[]{:S(2)}) copy-start(bf16[512,128]{1,0:T(8,128)(2,1)} %param.27) | copy-start | bytes 393220
  6.5 18.9 %copy-start.11 = (f32[1408]{0:T(1024)S(1)}, f32[1408]{0:T(1024)}, u32[]{:S(2)}) copy-start(f32[1408]{0:T(1024)} %param.17) | copy-start | bytes 16900
  6.5 18.9 %copy-start.12 = (f32[1408]{0:T(1024)S(1)}, f32[1408]{0:T(1024)}, u32[]{:S(2)}) copy-start(f32[1408]{0:T(1024)} %param.18) | copy-start | bytes 16900
  6.5 39.5 %copy-start.9 = (s32[1,128]{1,0:T(1,128)S(1)}, s32[1,128]{1,0:T(1,128)}, u32[]{:S(2)}) copy-start(s32[1,128]{1,0:T(1,128)} %owner_ref.1) | copy-start | bytes 1540
  6.5 39.5 %copy-start.8 = (s32[1,128]{1,0:T(1,128)S(1)}, s32[1,128]{1,0:T(1,128)}, u32[]{:S(2)}) copy-start(s32[1,128]{1,0:T(1,128)} %counts_ref.1) | copy-start | bytes 1540
  6.5 39.5 %copy-start.3 = (bf16[1,320,1408]{2,1,0:T(8,128)(2,1)S(1)}, bf16[1,320,1408]{2,1,0:T(8,128)(2,1)}, u32[]{:S(2)}) copy-start(bf16[1,320,1408]{2,1,0:T(8,128)(2,1)} %param.16) | copy-start | bytes 2703364
  11.4 32.7 %all-to-all-start = ((bf16[32,24,512]{2,1,0:T(8,128)(2,1)}), bf16[32,24,512]{2,1,0:T(8,128)(2,1)S(1)}, u32[]{:S(2)}, u32[]{:S(2)}) async-start(bf16[32,24,512]{2,1,0:T(8,128)(2,1)} %broadcast_in_dim.55), calls=%async_computation | async-start | bytes 1572864 | tf_op jit(solution)/shard_map/all_to_all | solution.py:142
  24.5 66.7 %all-gather.2.cloned.1.call-start = ((), (), s32[]{:S(2)}) async-start(), calls=%async_computation.2 | async-start | bytes 1703936 | tf_op jit(solution)/shard_map/all_gather | solution.py:138
  44.2 4.2 %collective-permute-start = (bf16[768,512]{1,0:T(8,128)(2,1)S(1)}, bf16[768,512]{1,0:T(8,128)(2,1)S(1)}, u32[]{:S(2)}, u32[]{:S(2)}) collective-permute-start(bf16[768,512]{1,0:T(8,128)(2,1)S(1)} %bitcast.19), channel_id=1, source_target_pairs={{0,12},{12,0},{1,13},{13,1},{2,14},{14,2},{3,15},{15,3},{4,16},{16... | collective-permute-start | bytes 2359304 | tf_op jit(solution)/shard_map/ppermute | solution.py:146
  46.1 2.2 %copy-start.13 = (s32[1,2,512]{2,1,0:T(2,128)S(1)}, s32[1,2,512]{2,1,0:T(2,128)}, u32[]{:S(2)}) copy-start(s32[1,2,512]{2,1,0:T(2,128)} %param.23) | copy-start | bytes 12292
  48.4 2.1 %copy-start.1 = (bf16[768,512]{1,0:T(8,128)(2,1)}, bf16[768,512]{1,0:T(8,128)(2,1)S(1)}, u32[]{:S(2)}) copy-start(bf16[768,512]{1,0:T(8,128)(2,1)S(1)} %collective-permute-done.other_ref) | copy-start | bytes 2359300
  48.4 8.2 %copy-start.14 = (f32[512]{0:T(512)S(1)}, f32[512]{0:T(512)}, u32[]{:S(2)}) copy-start(f32[512]{0:T(512)} %param.24) | copy-start | bytes 6148
  50.5 46.5 %all-to-all-start.1 = ((bf16[64,40,128]{2,1,0:T(8,128)(2,1)}), bf16[64,40,128]{2,1,0:T(8,128)(2,1)S(1)}, u32[]{:S(2)}, u32[]{:S(2)}) async-start(bf16[64,40,128]{2,1,0:T(8,128)(2,1)} %bitcast.6), calls=%async_computation.1 | async-start | bytes 1310720 | tf_op jit(solution)/shard_map/all_to_all | solution.py:170
  93.5 3.4 %copy-start.5 = (f32[512]{0:T(512)S(1)}, f32[512]{0:T(512)}, u32[]{:S(2)}) copy-start(f32[512]{0:T(512)} %param.25) | copy-start | bytes 6148
  93.5 3.4 %copy-start.6 = (f32[512]{0:T(512)S(1)}, f32[512]{0:T(512)}, u32[]{:S(2)}) copy-start(f32[512]{0:T(512)} %param.26) | copy-start | bytes 6148
  93.5 3.4 %copy-start.7 = (f32[512]{0:T(512)S(1)}, f32[512]{0:T(512)}, u32[]{:S(2)}) copy-start(f32[512]{0:T(512)} %param.29) | copy-start | bytes 6148
  97.0 1.2 %copy-start = (bf16[512,1024]{1,0:T(8,128)(2,1)S(1)}, bf16[512,1024]{1,0:T(8,128)(2,1)}, u32[]{:S(2)}) copy-start(bf16[512,1024]{1,0:T(8,128)(2,1)} %copy.32.wqk_ref) | copy-start | bytes 3145732
  98.2 1.0 copy-start.2
  99.2 1.0 copy-start.4
Sparse Core Ops, SparseCore 0:
  27.7 63.4 all-gather.1

commit v2 on v1

--- a/solution.py
+++ b/solution.py
@@ -78,27 +78,47 @@
 
 
 def decode_kernel(
-    recv_ref, seat_ref, base_ref, gain_ref, bias_ref, wqk_ref, wvt_ref, wproj_ref, pbias_ref,
-    out_ref, rows_ref, x_ref, vt_ref, att_ref,
+    recv_hbm, seat_hbm, base_hbm, wqk_hbm, wvt_hbm, wproj_hbm, gain_ref, bias_ref, pbias_ref,
+    out_ref, recv_ref, seat_ref, base_ref, wqk_ref, wvt_ref, wproj_ref, rows_ref, x_ref, vt_ref, att_ref, sems,
 ):
     clip = pl.program_id(0)
+    moves = [
+        pltpu.make_async_copy(source, into, sems.at[n])
+        for n, (source, into) in enumerate(
+            (
+                (recv_hbm, recv_ref), (seat_hbm, seat_ref), (base_hbm, base_ref),
+                (wqk_hbm, wqk_ref), (wvt_hbm, wvt_ref), (wproj_hbm, wproj_ref),
+            )
+        )
+    ]
 
     @pl.when(clip == 0)
     def _():
+        for move in moves:
+            move.start()
+        vt_ref[:, HEAD:, :] = jnp.ones((HEADS, 16, 512), BF)
+        moves[0].wait()
         rows_ref[...] = recv_ref[...].astype(F32)
-        vt_ref[:, HEAD:, :] = jnp.ones((HEADS, 16, 512), BF)
+        moves[1].wait()
+        moves[2].wait()
 
     tokens = jnp.concatenate(
         [rows_ref[pl.ds(4 * clip + part, VMAX, stride=8), :] for part in range(4)], axis=1
     ).astype(BF)
-    x_ref[:VMAX, :] = base_ref[:VMAX, :] + jnp.dot(seat_ref[0], tokens, preferred_element_type=F32)
-    x_ref[VMAX:, :] = base_ref[VMAX:, :]
+    x_ref[:VMAX, :] = base_ref[clip, :VMAX, :] + jnp.dot(seat_ref[clip], tokens, preferred_element_type=F32)
+    x_ref[VMAX:, :] = base_ref[clip, VMAX:, :]
     values = x_ref[...]
     average = jnp.mean(values, axis=1, keepdims=True)
     centred = values - average
     spread = jnp.mean(centred * centred, axis=1, keepdims=True)
     normed = (centred * lax.rsqrt(spread + EPS) * gain_ref[...] + bias_ref[...]).astype(BF)
     across = (((1,), (1,)), ((), ()))
+
+    @pl.when(clip == 0)
+    def _():
+        for move in moves[3:]:
+            move.wait()
+
     queries = jnp.dot(normed, wqk_ref[:, :512], preferred_element_type=F32)
     queries = (queries * (HEAD**-0.5 * math.log2(math.e))).astype(BF)
     keys = jnp.dot(normed, wqk_ref[:, 512:], preferred_element_type=F32).astype(BF)
@@ -124,6 +144,52 @@
     out_ref[0] = (x_ref[...] + result + pbias_ref[...]).astype(BF)
 
 
+def weights_kernel(where_ref, mine_ref, swap_ref, wqk_ref, wvt_ref):
+    core = where_ref[12]
+    for block in range(12):
+        at = where_ref[block]
+        for piece, side in ((mine_ref[at], core), (swap_ref[at], 1 - core)):
+            rows = pl.ds(pl.multiple_of(256 * side, 256), 256)
+            if block < 8:
+                wqk_ref[rows, 128 * block : 128 * (block + 1)] = piece
+            else:
+                wvt_ref[128 * (block - 8) : 128 * (block - 7), rows] = piece.T
+
+
+def gather_table():
+    table = np.zeros((12, 12), np.int32)
+    for z in range(12):
+        for f in range(12):
+            turn = (f // 4 - z // 4) % 3
+            table[z, f] = 6 * ((f ^ z) & 1) + 3 * (((f ^ z) >> 1) & 1) + (0, 2, 1)[turn]
+    return table
+
+
+def gather_qkv(w_qkv, core):
+    half = lax.dynamic_slice(w_qkv, (core * 256, 0), (256, 128))[None]
+    above = lax.ppermute(half, "fsdp", [(z, (z + 4) % 12) for z in range(12)])
+    below = lax.ppermute(half, "fsdp", [(z, (z + 8) % 12) for z in range(12)])
+    three = jnp.concatenate([half, above, below])
+    twin = lax.ppermute(three, "fsdp", [(z, z ^ 2) for z in range(12)])
+    return three, twin
+
+
+def place_qkv(three, twin, core):
+    six = jnp.concatenate([three, twin])
+    rest = lax.ppermute(six, "fsdp", [(z, z ^ 1) for z in range(12)])
+    mine = jnp.concatenate([six, rest])
+    swap = lax.ppermute(mine, "core", [(0, 1), (1, 0)])
+    where = jnp.concatenate([jnp.asarray(gather_table())[lax.axis_index("fsdp")], core[None]])
+    return pl.pallas_call(
+        weights_kernel,
+        out_shape=(pltpu.HBM((512, 1024), BF), pltpu.HBM((512, 512), BF)),
+        in_specs=[pl.BlockSpec(memory_space=pltpu.SMEM)] + [pl.BlockSpec(memory_space=pltpu.VMEM)] * 2,
+        compiler_params=pltpu.CompilerParams(vmem_limit_bytes=16 * MIB),
+        cost_estimate=pl.CostEstimate(flops=0, bytes_accessed=6_000_000, transcendentals=0),
+        name="weights",
+    )(where, mine, swap)
+
+
 def whole(shape):
     return pl.BlockSpec(shape, lambda *_: (0,) * len(shape))
 
@@ -135,13 +201,12 @@
     my_index = lax.axis_index(DP).astype(jnp.int32)
     core = lax.axis_index("core").astype(jnp.int32)
     residue = token_index[0, 0] % NDEV
-    w_full = lax.all_gather(w_qkv, "fsdp", axis=1, tiled=True)
+    three, twin = gather_qkv(w_qkv, core)
 
     mark = jnp.broadcast_to(residue.astype(BF), (2, 512))
     shard = jnp.concatenate([w_e2d, mark], axis=0)
-    gathered = lax.all_to_all(
-        jnp.broadcast_to(shard[None], (32, 24, 512)), PLANE, 0, 0, tiled=True
-    )
+    shards = jnp.broadcast_to(shard[None], (32, 24, 512))
+    gathered = lax.all_to_all(shards, PLANE, 0, 0, tiled=True)
     own = gathered.reshape(768, 512)
     other = lax.ppermute(own, "core", [(0, 1), (1, 0)])
 
@@ -167,7 +232,10 @@
         cost_estimate=pl.CostEstimate(flops=1_000_000_000, bytes_accessed=4_000_000, transcendentals=0),
         name="embed",
     )(normed, own, other, pick)
-    received = lax.all_to_all(sent.reshape(NDEV, 40, 128), DP, 0, 0, tiled=True).reshape(2560, 128)
+    twin = lax.optimization_barrier((twin, sent))[0]
+    wqk, wvt = place_qkv(three, twin, core)
+    received = lax.all_to_all(sent.reshape(NDEV, 40, 128), DP, 0, 0, tiled=True)
+    received = received.reshape(2560, 128)
 
     column = np.arange(512)
     rate = np.power(10000.0, -(2 * (column // 2)) / 512.0).astype(np.float32)
@@ -192,30 +260,26 @@
         decode_kernel,
         grid=(2,),
         out_shape=jax.ShapeDtypeStruct((1, 2, 512, 512), BF),
-        in_specs=[
-            whole((2560, 128)),
-            pl.BlockSpec((1, VMAX, VMAX), lambda clip: (clip, 0, 0)),
-            pl.BlockSpec((512, 512), lambda clip: (clip, 0)),
-            whole((1, 512)),
-            whole((1, 512)),
-            whole((512, 1024)),
-            whole((512, 512)),
-            whole((512, 512)),
-            whole((1, 512)),
-        ],
+        in_specs=[pl.BlockSpec(memory_space=pl.ANY)] + [pl.BlockSpec(memory_space=pltpu.HBM)] * 5 + [whole((1, 512))] * 3,
         out_specs=pl.BlockSpec((None, 1, 512, 512), lambda clip: (0, clip, 0, 0)),
         scratch_shapes=[
+            pltpu.VMEM((2560, 128), BF),
+            pltpu.VMEM((2, VMAX, VMAX), BF),
+            pltpu.VMEM((2, 512, 512), F32),
+            pltpu.VMEM((512, 1024), BF),
+            pltpu.VMEM((512, 512), BF),
+            pltpu.VMEM((512, 512), BF),
             pltpu.VMEM((2560, 128), F32),
             pltpu.VMEM((512, 512), F32),
             pltpu.VMEM((HEADS, HEAD + 16, 512), BF),
             pltpu.VMEM((512, 512), BF),
+            pltpu.SemaphoreType.DMA((6,)),
         ],
-        compiler_params=pltpu.CompilerParams(vmem_limit_bytes=32 * MIB),
+        compiler_params=pltpu.CompilerParams(vmem_limit_bytes=53 * MIB),
         cost_estimate=pl.CostEstimate(flops=4_000_000_000, bytes_accessed=8_000_000, transcendentals=4_000_000),
         name="decode",
     )(
-        received, seat, base.reshape(1024, 512), dec_gain[None], dec_bias[None],
-        w_full[:, :1024], w_full[:, 1024:].T, w_proj, proj_bias[None],
+        received, seat, base, wqk, wvt, w_proj, dec_gain[None], dec_bias[None], proj_bias[None],
     )
 
 

time: 120 us -> 109 us (0.908)
  the two profiles are of different devices: /device:TPU:2 before, /device:TPU:1 now
where the time goes in v2:
time: 109 us; the launch traced here: 108 us
  starting transfers between devices  50.4 us (46%)
  Pallas kernels  20.5 us (19%)
  waiting for transfers between devices  14.7 us (13%)
  other arithmetic  12.7 us (12%)
  local copies, waits for them, and re-layouts  7.82 us (7%)
  between operations  2.27 us (2%)
    pallas_call x1, Pallas kernels, on_device(): pl.pallas_call(decode_kernel, grid=(2,), out_shape=jax.ShapeDtypeStruct((...  14.4 us
    ppermute x1, starting transfers between devices, gather_qkv(): below = lax.ppermute(half, 'fsdp', [(z, (z + 8) % 12) for z in range(12)])  14.3 us
    all_to_all x1, starting transfers between devices, on_device(): gathered = lax.all_to_all(shards, PLANE, 0, 0, tiled=True)  10.5 us
    add x1, other arithmetic, on_device(): base = jnp.where(visible[..., None], 0.0, mask_token) + codes  9.24 us
    ppermute x1, waiting for transfers between devices, place_qkv(): rest = lax.ppermute(six, 'fsdp', [(z, z ^ 1) for z in range(12)])  7.26 us
    ppermute x1, waiting for transfers between devices, gather_qkv(): twin = lax.ppermute(three, 'fsdp', [(z, z ^ 2) for z in range(12)])  6.53 us
    ppermute x1, starting transfers between devices, on_device(): other = lax.ppermute(own, 'core', [(0, 1), (1, 0)])  6.45 us
    all_to_all x1, starting transfers between devices, on_device(): received = lax.all_to_all(sent.reshape(NDEV, 40, 128), DP, 0, 0, tiled=True)  6.05 us
  transfers between devices with their start and end apart: 8, of which 3 were waited for; matrix products, arithmetic and copies ran while one was open for 14% of the time, Pallas kernels for 6%

profile of v2, /device:TPU:1, one launch (start us, length us, event | category | flops | bytes accessed | tf_op | source)
XLA Modules:
  0.0 108.4 jit_solution(1378318101585659238)
XLA Ops:
  0.0 1.3 %slice.27 = s32[1,1]{1,0:T(1,128)} slice(s32[1,320]{1,0:T(1,128)} %param.21), slice={[0:1], [0:1]} | slice | bytes 8 | tf_op jit(solution)/shard_map/slice | solution.py:203
  4.0 0.9 broadcast_in_dim.59
  4.9 10.5 %all-to-all-start = ((bf16[32,24,512]{2,1,0:T(8,128)(2,1)}), bf16[32,24,512]{2,1,0:T(8,128)(2,1)S(1)}, u32[]{:S(2)}, u32[]{:S(2)}) async-start(bf16[32,24,512]{2,1,0:T(8,128)(2,1)} %broadcast_in_dim.59), calls=%async_computation | async-start | bytes 1572864 | tf_op jit(solution)/shard_map/all_to_all | solution.py:209
  15.5 14.3 %collective-permute-start.2 = (bf16[1,256,128]{2,1,0:T(8,128)(2,1)S(1)}, bf16[1,256,128]{2,1,0:T(8,128)(2,1)}, u32[]{:S(2)}, u32[]{:S(2)}) collective-permute-start(bf16[1,256,128]{2,1,0:T(8,128)(2,1)S(1)} %get-tuple-element.22), channel_id=1, source_target_pairs={{0,8},{1,9},{2,10},{3,11},{4,0},{5,1},{6,2},{7,3},{8,4},{9,5},{10,... | collective-permute-start | bytes 196616 | tf_op jit(solution)/shard_map/ppermute | solution.py:171
  29.8 1.9 %collective-permute-start.1 = (bf16[1,256,128]{2,1,0:T(8,128)(2,1)S(1)}, bf16[1,256,128]{2,1,0:T(8,128)(2,1)}, u32[]{:S(2)}, u32[]{:S(2)}) collective-permute-start(bf16[1,256,128]{2,1,0:T(8,128)(2,1)S(1)} %get-tuple-element.22), channel_id=1, source_target_pairs={{0,4},{1,5},{2,6},{3,7},{4,8},{5,9},{6,10},{7,11},{8,0},{9,1},{10,... | collective-permute-start | bytes 196616 | tf_op jit(solution)/shard_map/ppermute | solution.py:170
  31.9 2.0 %prep.1 = (bf16[2,320,768]{2,1,0:T(8,128)(2,1)S(1)}, bf16[640,320]{1,0:T(8,128)(2,1)S(1)}, s32[8,128]{1,0:T(8,128)S(1)}) custom-call(s32[3]{0:T(128)S(1)} %pad_add_fusion.ids_ref, bf16[320,1408]{1,0:T(8,128)(2,1)S(1)} %bitcast.24, f32[1,1408]{1,0:T(1,128)S(1)} %broadcast_in_dim.34.gain_ref, f32[1,1408]{1,0:T(1,128)S(1)} %broadcast_in_dim.58.bias_ref, ...), custom_call_target="tpu_custom_call" | custom-call | flops 4000000000 | bytes 4000000 | tf_op jit(solution)/shard_map/prep/pallas_call | solution.py:214
  33.9 0.8 copy-done
  34.9 6.5 %collective-permute-start = (bf16[768,512]{1,0:T(8,128)(2,1)S(1)}, bf16[768,512]{1,0:T(8,128)(2,1)S(1)}, u32[]{:S(2)}, u32[]{:S(2)}) collective-permute-start(bf16[768,512]{1,0:T(8,128)(2,1)S(1)} %bitcast.21), channel_id=1, source_target_pairs={{0,12},{12,0},{1,13},{13,1},{2,14},{14,2},{3,15},{15,3},{4,16},{16... | collective-permute-start | bytes 2359304 | tf_op jit(solution)/shard_map/ppermute | solution.py:211
  41.4 9.2 %sine_add_fusion.base_hbm = f32[2,512,512]{2,1,0:T(8,128)} fusion(f32[512]{0:T(512)} %constant.57.clone, f32[512]{0:T(512)} %constant.56.clone, f32[2,512]{1,0:T(2,128)S(1)} %convert_bitcast_fusion, f32[512]{0:T(512)} %param.25, pred[2,512]{1,0:T(4,128)(4,1)S(1)} %iota_compare_fusion), kind=kLoop, calls=%fused_computation | loop fusion | flops 2097152 | bytes 2108416 | tf_op jit(solution)/shard_map/add | solution.py:246
  50.7 1.6 %pad_maximum_fusion.1 = bf16[3,256,128]{2,1,0:T(8,128)(2,1)} fusion(bf16[1,256,128]{2,1,0:T(8,128)(2,1)} %collective-permute-done.2, bf16[1,256,128]{2,1,0:T(8,128)(2,1)} %collective-permute-done.1, bf16[1,256,128]{2,1,0:T(8,128)(2,1)S(1)} %get-tuple-element.22), kind=kLoop, calls=%fused_computation.3 | loop fusion | flops 196608 | bytes 393216 | tf_op jit(solution)/shard_map/concatenate | solution.py:172
  52.2 5.6 %collective-permute-start.3 = (bf16[3,256,128]{2,1,0:T(8,128)(2,1)}, bf16[3,256,128]{2,1,0:T(8,128)(2,1)S(1)}, u32[]{:S(2)}, u32[]{:S(2)}) collective-permute-start(bf16[3,256,128]{2,1,0:T(8,128)(2,1)} %pad_maximum_fusion.1), channel_id=1, source_target_pairs={{0,2},{1,3},{2,0},{3,1},{4,6},{5,7},{6,4},{7,5},{8,10},{9,11},{10,... | collective-permute-start | bytes 589832 | tf_op jit(solution)/shard_map/ppermute | solution.py:173
  57.9 1.0 copy-done.1
  59.0 2.0 %embed.1 = bf16[2560,128]{1,0:T(8,128)(2,1)} custom-call(bf16[2,320,768]{2,1,0:T(8,128)(2,1)S(1)} %get-tuple-element.11.normed_ref, bf16[768,512]{1,0:T(8,128)(2,1)S(1)} %bitcast.22, bf16[768,512]{1,0:T(8,128)(2,1)S(1)} %collective-permute-done.other_ref, bf16[640,320]{1,0:T(8,128)(2,1)S(1)} %copy-done.1), custom_call_target="tpu_custom_call" | custom-call | flops 1000000000 | bytes 4000000 | tf_op jit(solution)/shard_map/embed/pallas_call | solution.py:227
  61.0 6.5 %collective-permute-done.3 = bf16[3,256,128]{2,1,0:T(8,128)(2,1)S(1)} collective-permute-done((bf16[3,256,128]{2,1,0:T(8,128)(2,1)}, bf16[3,256,128]{2,1,0:T(8,128)(2,1)S(1)}, u32[]{:S(2)}, u32[]{:S(2)}) %collective-permute-start.3) | collective-permute-done | bytes 196640 | tf_op jit(solution)/shard_map/ppermute | solution.py:173
  67.5 6.1 %all-to-all-start.1 = ((bf16[64,40,128]{2,1,0:T(8,128)(2,1)}), bf16[64,40,128]{2,1,0:T(8,128)(2,1)}, u32[]{:S(2)}, u32[]{:S(2)}) async-start(bf16[64,40,128]{2,1,0:T(8,128)(2,1)} %bitcast.6), calls=%async_computation.1 | async-start | bytes 1310720 | tf_op jit(solution)/shard_map/all_to_all | solution.py:237
  73.6 1.0 pad_maximum_fusion
  74.6 2.4 %collective-permute-start.4 = (bf16[6,256,128]{2,1,0:T(8,128)(2,1)S(1)}, bf16[6,256,128]{2,1,0:T(8,128)(2,1)S(1)}, u32[]{:S(2)}, u32[]{:S(2)}) collective-permute-start(bf16[6,256,128]{2,1,0:T(8,128)(2,1)S(1)} %pad_maximum_fusion), channel_id=1, source_target_pairs={{0,1},{1,0},{2,3},{3,2},{4,5},{5,4},{6,7},{7,6},{8,9},{9,8},{10,11... | collective-permute-start | bytes 1179656 | tf_op jit(solution)/shard_map/ppermute | solution.py:179
  77.7 0.9 constant_dynamic-update-slice_fusion.3
  78.6 0.9 constant_dynamic-update-slice_fusion.2
  79.5 7.3 %collective-permute-done.4 = bf16[6,256,128]{2,1,0:T(8,128)(2,1)S(1)} collective-permute-done((bf16[6,256,128]{2,1,0:T(8,128)(2,1)S(1)}, bf16[6,256,128]{2,1,0:T(8,128)(2,1)S(1)}, u32[]{:S(2)}, u32[]{:S(2)}) %collective-permute-start.4) | collective-permute-done | bytes 393248 | tf_op jit(solution)/shard_map/ppermute | solution.py:179
  86.8 3.2 %collective-permute-start.5 = (bf16[12,256,128]{2,1,0:T(8,128)(2,1)S(1)}, bf16[12,256,128]{2,1,0:T(8,128)(2,1)S(1)}, u32[]{:S(2)}, u32[]{:S(2)}) collective-permute-start(bf16[12,256,128]{2,1,0:T(8,128)(2,1)S(1)} %constant_dynamic-update-slice_fusion.mine_ref), channel_id=1, source_target_pairs={{0,12},{12,0},{1,13},{13,1},{2,14},{14,2},{3,15},{15,3},{4,16},{16... | collective-permute-start | bytes 2359304 | tf_op jit(solution)/shard_map/ppermute | solution.py:181
  91.0 0.9 collective-permute-done.5.swap_ref
  91.9 2.1 %weights.1 = (bf16[512,1024]{1,0:T(8,128)(2,1)}, bf16[512,512]{1,0:T(8,128)(2,1)}) custom-call(s32[13]{0:T(128)S(1)} %pad_add_fusion.1.where_ref, bf16[12,256,128]{2,1,0:T(8,128)(2,1)S(1)} %constant_dynamic-update-slice_fusion.mine_ref, bf16[12,256,128]{2,1,0:T(8,128)(2,1)S(1)} %collective-permute-done.5.swap_ref), custom_call_target="tpu_custom_call" | custom-call | bytes 6000000 | tf_op jit(solution)/shard_map/weights/pallas_call | solution.py:183
  94.0 14.4 %decode.1 = bf16[1,2,512,512]{3,2,1,0:T(8,128)(2,1)} custom-call(bf16[2560,128]{1,0:T(8,128)(2,1)} %bitcast.7.recv_hbm, bf16[2,320,320]{2,1,0:T(8,128)(2,1)S(1)} %compare_convert_fusion.seat_hbm, f32[2,512,512]{2,1,0:T(8,128)} %sine_add_fusion.base_hbm, bf16[512,1024]{1,0:T(8,128)(2,1)} %get-tuple-element.15.wqk_hbm, ...), custom_call_target="tpu_custom_call" | custom-call | flops 4000000000 | bytes 8000000 | tf_op jit(solution)/shard_map/decode/pallas_call | solution.py:259
  (51 shorter events, 3.0 us)
Async XLA Ops:
  0.0 15.5 %copy-start.9 = (bf16[512,128]{1,0:T(8,128)(2,1)S(1)}, bf16[512,128]{1,0:T(8,128)(2,1)}, u32[]{:S(2)}) copy-start(bf16[512,128]{1,0:T(8,128)(2,1)} %param.28) | copy-start | bytes 393220
  0.0 31.7 %copy-start.10 = (f32[1408]{0:T(1024)S(1)}, f32[1408]{0:T(1024)}, u32[]{:S(2)}) copy-start(f32[1408]{0:T(1024)} %param.18) | copy-start | bytes 16900
  0.0 31.7 %copy-start.11 = (f32[1408]{0:T(1024)S(1)}, f32[1408]{0:T(1024)}, u32[]{:S(2)}) copy-start(f32[1408]{0:T(1024)} %param.19) | copy-start | bytes 16900
  0.0 31.8 %copy-start.7 = (s32[1,128]{1,0:T(1,128)S(1)}, s32[1,128]{1,0:T(1,128)}, u32[]{:S(2)}) copy-start(s32[1,128]{1,0:T(1,128)} %owner_ref.1) | copy-start | bytes 1540
  0.0 31.8 %copy-start.6 = (s32[1,128]{1,0:T(1,128)S(1)}, s32[1,128]{1,0:T(1,128)}, u32[]{:S(2)}) copy-start(s32[1,128]{1,0:T(1,128)} %counts_ref.1) | copy-start | bytes 1540
  0.0 31.8 %copy-start.2 = (bf16[1,320,1408]{2,1,0:T(8,128)(2,1)S(1)}, bf16[1,320,1408]{2,1,0:T(8,128)(2,1)}, u32[]{:S(2)}) copy-start(bf16[1,320,1408]{2,1,0:T(8,128)(2,1)} %param.17) | copy-start | bytes 2703364
  4.9 30.0 %all-to-all-start = ((bf16[32,24,512]{2,1,0:T(8,128)(2,1)}), bf16[32,24,512]{2,1,0:T(8,128)(2,1)S(1)}, u32[]{:S(2)}, u32[]{:S(2)}) async-start(bf16[32,24,512]{2,1,0:T(8,128)(2,1)} %broadcast_in_dim.59), calls=%async_computation | async-start | bytes 1572864 | tf_op jit(solution)/shard_map/all_to_all | solution.py:209
  15.5 35.2 %copy-start.8 = (bf16[1,256,128]{2,1,0:T(8,128)(2,1)}, bf16[1,256,128]{2,1,0:T(8,128)(2,1)S(1)}, u32[]{:S(2)}) copy-start(bf16[1,256,128]{2,1,0:T(8,128)(2,1)S(1)} %get-tuple-element.22) | copy-start | bytes 196612
  15.5 35.1 %collective-permute-start.2 = (bf16[1,256,128]{2,1,0:T(8,128)(2,1)S(1)}, bf16[1,256,128]{2,1,0:T(8,128)(2,1)}, u32[]{:S(2)}, u32[]{:S(2)}) collective-permute-start(bf16[1,256,128]{2,1,0:T(8,128)(2,1)S(1)} %get-tuple-element.22), channel_id=1, source_target_pairs={{0,8},{1,9},{2,10},{3,11},{4,0},{5,1},{6,2},{7,3},{8,4},{9,5},{10,... | collective-permute-start | bytes 196616 | tf_op jit(solution)/shard_map/ppermute | solution.py:171
  29.8 20.9 %collective-permute-start.1 = (bf16[1,256,128]{2,1,0:T(8,128)(2,1)S(1)}, bf16[1,256,128]{2,1,0:T(8,128)(2,1)}, u32[]{:S(2)}, u32[]{:S(2)}) collective-permute-start(bf16[1,256,128]{2,1,0:T(8,128)(2,1)S(1)} %get-tuple-element.22), channel_id=1, source_target_pairs={{0,4},{1,5},{2,6},{3,7},{4,8},{5,9},{6,10},{7,11},{8,0},{9,1},{10,... | collective-permute-start | bytes 196616 | tf_op jit(solution)/shard_map/ppermute | solution.py:170
  31.9 3.0 %copy-start.12 = (s32[1,2,512]{2,1,0:T(2,128)S(1)}, s32[1,2,512]{2,1,0:T(2,128)}, u32[]{:S(2)}) copy-start(s32[1,2,512]{2,1,0:T(2,128)} %param.24) | copy-start | bytes 12292
  33.9 0.8 copy-start
  34.9 23.0 %collective-permute-start = (bf16[768,512]{1,0:T(8,128)(2,1)S(1)}, bf16[768,512]{1,0:T(8,128)(2,1)S(1)}, u32[]{:S(2)}, u32[]{:S(2)}) collective-permute-start(bf16[768,512]{1,0:T(8,128)(2,1)S(1)} %bitcast.21), channel_id=1, source_target_pairs={{0,12},{12,0},{1,13},{13,1},{2,14},{14,2},{3,15},{15,3},{4,16},{16... | collective-permute-start | bytes 2359304 | tf_op jit(solution)/shard_map/ppermute | solution.py:211
  52.2 15.3 %collective-permute-start.3 = (bf16[3,256,128]{2,1,0:T(8,128)(2,1)}, bf16[3,256,128]{2,1,0:T(8,128)(2,1)S(1)}, u32[]{:S(2)}, u32[]{:S(2)}) collective-permute-start(bf16[3,256,128]{2,1,0:T(8,128)(2,1)} %pad_maximum_fusion.1), channel_id=1, source_target_pairs={{0,2},{1,3},{2,0},{3,1},{4,6},{5,7},{6,4},{7,5},{8,10},{9,11},{10,... | collective-permute-start | bytes 589832 | tf_op jit(solution)/shard_map/ppermute | solution.py:173
  57.9 1.0 copy-start.1
  67.5 26.4 %all-to-all-start.1 = ((bf16[64,40,128]{2,1,0:T(8,128)(2,1)}), bf16[64,40,128]{2,1,0:T(8,128)(2,1)}, u32[]{:S(2)}, u32[]{:S(2)}) async-start(bf16[64,40,128]{2,1,0:T(8,128)(2,1)} %bitcast.6), calls=%async_computation.1 | async-start | bytes 1310720 | tf_op jit(solution)/shard_map/all_to_all | solution.py:237
  73.6 20.4 %copy-start.3 = (f32[512]{0:T(512)S(1)}, f32[512]{0:T(512)}, u32[]{:S(2)}) copy-start(f32[512]{0:T(512)} %param.26) | copy-start | bytes 6148
  73.6 20.4 %copy-start.4 = (f32[512]{0:T(512)S(1)}, f32[512]{0:T(512)}, u32[]{:S(2)}) copy-start(f32[512]{0:T(512)} %param.27) | copy-start | bytes 6148
  73.6 20.4 %copy-start.5 = (f32[512]{0:T(512)S(1)}, f32[512]{0:T(512)}, u32[]{:S(2)}) copy-start(f32[512]{0:T(512)} %param.30) | copy-start | bytes 6148
  74.6 12.2 %collective-permute-start.4 = (bf16[6,256,128]{2,1,0:T(8,128)(2,1)S(1)}, bf16[6,256,128]{2,1,0:T(8,128)(2,1)S(1)}, u32[]{:S(2)}, u32[]{:S(2)}) collective-permute-start(bf16[6,256,128]{2,1,0:T(8,128)(2,1)S(1)} %pad_maximum_fusion), channel_id=1, source_target_pairs={{0,1},{1,0},{2,3},{3,2},{4,5},{5,4},{6,7},{7,6},{8,9},{9,8},{10,11... | collective-permute-start | bytes 1179656 | tf_op jit(solution)/shard_map/ppermute | solution.py:179
  86.8 5.1 %collective-permute-start.5 = (bf16[12,256,128]{2,1,0:T(8,128)(2,1)S(1)}, bf16[12,256,128]{2,1,0:T(8,128)(2,1)S(1)}, u32[]{:S(2)}, u32[]{:S(2)}) collective-permute-start(bf16[12,256,128]{2,1,0:T(8,128)(2,1)S(1)} %constant_dynamic-update-slice_fusion.mine_ref), channel_id=1, source_target_pairs={{0,12},{12,0},{1,13},{13,1},{2,14},{14,2},{3,15},{15,3},{4,16},{16... | collective-permute-start | bytes 2359304 | tf_op jit(solution)/shard_map/ppermute | solution.py:181

commit v3 on v1

--- a/solution.py
+++ b/solution.py
@@ -10,11 +10,12 @@
 
 DP = ("y", "x", "core")
 PLANE = ("y", "x")
-HEADS = 8
 HEAD = 64
 VMAX = 320
 NDEV = 64
 PER = 5
+FIRST = 53
+SECOND = 53
 EPS = 1e-06
 MIB = 1 << 20
 BF = jnp.bfloat16
@@ -77,51 +78,119 @@
     out_ref[...] = rows_ref[...].astype(BF)
 
 
-def decode_kernel(
-    recv_ref, seat_ref, base_ref, gain_ref, bias_ref, wqk_ref, wvt_ref, wproj_ref, pbias_ref,
-    out_ref, rows_ref, x_ref, vt_ref, att_ref,
+def shard_kernel(ids_ref, rows_ref, out_ref):
+    residue = (ids_ref[0, 0] & 63).astype(F32)
+    mark = jnp.full((2, 512), residue, F32)
+    block = jnp.concatenate([rows_ref[...].astype(F32), mark], axis=0).astype(BF)
+    for chip in range(32):
+        out_ref[chip] = block
+
+
+def fetch_blocks(where_ref, mine_hbm, swap_hbm, weights_ref, sems):
+    moves = []
+    for pair in range(2):
+        for kind in range(3):
+            at = 3 * pair + where_ref[kind]
+            column = 384 * pair + 128 * kind
+            for source, side in ((mine_hbm, where_ref[3]), (swap_hbm, 1 - where_ref[3])):
+                rows = pl.ds(pl.multiple_of(256 * side, 256), 256)
+                moves.append(
+                    pltpu.make_async_copy(
+                        source.at[at], weights_ref.at[rows, column : column + 128], sems.at[len(moves)]
+                    )
+                )
+    return moves
+
+
+def two_pairs(normed, weights_ref, wproj_ref, where_ref, first, total):
+    across = (((1,), (1,)), ((), ()))
+    left = iota((512, 128), 1) < HEAD
+    zero = jnp.zeros((512, 128), BF)
+    ones = jnp.ones((16, 512), BF)
+    for pair in range(2):
+        made = jnp.dot(normed, weights_ref[:, 384 * pair : 384 * (pair + 1)], preferred_element_type=F32)
+        queries = (made[:, :128] * (HEAD**-0.5 * math.log2(math.e))).astype(BF)
+        keys = made[:, 128:256].astype(BF)
+        values = made[:, 256:].T.astype(BF)
+        parts = []
+        for head in range(2):
+            key = jnp.where(left, keys, zero) if head == 0 else jnp.where(left, zero, keys)
+            scores = lax.dot_general(key, queries, across, preferred_element_type=F32)
+            top = jnp.max(scores, axis=0, keepdims=True)
+            weights = jnp.exp2(scores - top).astype(BF)
+            stacked = jnp.concatenate([values[HEAD * head : HEAD * (head + 1)], ones], axis=0)
+            mixed = jnp.dot(stacked, weights, preferred_element_type=F32)
+            parts.append(mixed[:HEAD] * (1.0 / mixed[HEAD : HEAD + 1]))
+        attended = jnp.concatenate(parts, axis=0).T.astype(BF)
+        rows = pl.ds(pl.multiple_of(128 * where_ref[first + pair], 128), 128)
+        total = total + jnp.dot(attended, wproj_ref[rows, :], preferred_element_type=F32)
+    return total
+
+
+def first_kernel(
+    where_ref, recv_hbm, seat_hbm, base_hbm, mine_hbm, swap_hbm, wproj_hbm, gain_ref, bias_ref, pbias_ref,
+    total_ref, normed_ref, recv_ref, seat_ref, base_ref, weights_ref, wproj_ref, rows_ref, sems,
 ):
     clip = pl.program_id(0)
+    moves = [
+        pltpu.make_async_copy(source, into, sems.at[12 + n])
+        for n, (source, into) in enumerate(
+            ((recv_hbm, recv_ref), (seat_hbm, seat_ref), (base_hbm, base_ref), (wproj_hbm, wproj_ref))
+        )
+    ]
 
     @pl.when(clip == 0)
     def _():
+        for move in moves:
+            move.start()
+        for move in fetch_blocks(where_ref, mine_hbm, swap_hbm, weights_ref, sems):
+            move.start()
+        moves[0].wait()
         rows_ref[...] = recv_ref[...].astype(F32)
-        vt_ref[:, HEAD:, :] = jnp.ones((HEADS, 16, 512), BF)
+        moves[1].wait()
+        moves[2].wait()
 
     tokens = jnp.concatenate(
         [rows_ref[pl.ds(4 * clip + part, VMAX, stride=8), :] for part in range(4)], axis=1
     ).astype(BF)
-    x_ref[:VMAX, :] = base_ref[:VMAX, :] + jnp.dot(seat_ref[0], tokens, preferred_element_type=F32)
-    x_ref[VMAX:, :] = base_ref[VMAX:, :]
-    values = x_ref[...]
+    placed = jnp.dot(seat_ref[clip], tokens, preferred_element_type=F32)
+    values = jnp.concatenate([base_ref[clip, :VMAX, :] + placed, base_ref[clip, VMAX:, :]], axis=0)
     average = jnp.mean(values, axis=1, keepdims=True)
     centred = values - average
     spread = jnp.mean(centred * centred, axis=1, keepdims=True)
     normed = (centred * lax.rsqrt(spread + EPS) * gain_ref[...] + bias_ref[...]).astype(BF)
-    across = (((1,), (1,)), ((), ()))
-    queries = jnp.dot(normed, wqk_ref[:, :512], preferred_element_type=F32)
-    queries = (queries * (HEAD**-0.5 * math.log2(math.e))).astype(BF)
-    keys = jnp.dot(normed, wqk_ref[:, 512:], preferred_element_type=F32).astype(BF)
-    vt = lax.dot_general(wvt_ref[...], normed, across, preferred_element_type=F32).astype(BF)
-    for head in range(HEADS):
-        vt_ref[head, :HEAD, :] = vt[HEAD * head : HEAD * (head + 1), :]
-    left = iota((512, 128), 1) < HEAD
-    zero = jnp.zeros((512, 128), BF)
-    for head in range(HEADS):
-        pair = slice(128 * (head // 2), 128 * (head // 2 + 1))
-        key = keys[:, pair]
-        key = jnp.where(left, key, zero) if head % 2 == 0 else jnp.where(left, zero, key)
-        scores = lax.dot_general(key, queries[:, pair], across, preferred_element_type=F32)
-        top = jnp.max(scores, axis=0, keepdims=True)
-        weights = jnp.exp2(scores - top).astype(BF)
-        mixed = jnp.dot(vt_ref[head], weights, preferred_element_type=F32)
-        att_ref[HEAD * head : HEAD * (head + 1), :] = (
-            mixed[:HEAD] * (1.0 / mixed[HEAD : HEAD + 1])
-        ).astype(BF)
-    result = lax.dot_general(
-        att_ref[...], wproj_ref[...], (((0,), (0,)), ((), ())), preferred_element_type=F32
-    )
-    out_ref[0] = (x_ref[...] + result + pbias_ref[...]).astype(BF)
+    normed_ref[0] = normed
+    total_ref[0] = values + pbias_ref[...]
+
+    @pl.when(clip == 0)
+    def _():
+        for move in fetch_blocks(where_ref, mine_hbm, swap_hbm, weights_ref, sems):
+            move.wait()
+        moves[3].wait()
+
+    total_ref[0] = two_pairs(normed, weights_ref, wproj_ref, where_ref, 4, total_ref[0])
+
+
+def second_kernel(
+    where_ref, total_ref, normed_ref, mine_hbm, swap_hbm, wproj_ref, out_ref, weights_ref, sems
+):
+    @pl.when(pl.program_id(0) == 0)
+    def _():
+        moves = fetch_blocks(where_ref, mine_hbm, swap_hbm, weights_ref, sems)
+        for move in moves:
+            move.start()
+        for move in moves:
+            move.wait()
+
+    out_ref[0] = two_pairs(normed_ref[0], weights_ref, wproj_ref, where_ref, 6, total_ref[0]).astype(BF)
+
+
+def gather_table():
+    table = np.zeros((12, 8), np.int32)
+    for z in range(12):
+        table[z, :3] = [(0, 2, 1)[(kind - z // 4) % 3] for kind in range(3)]
+        table[z, 4:] = [z % 4, (z ^ 2) % 4, (z ^ 1) % 4, (z ^ 3) % 4]
+    return table
 
 
 def whole(shape):
@@ -132,20 +201,28 @@
     enc_out, norm_gain, norm_bias, w_e2d, token_index, counts, owner, dec_tubes,
     mask_token, dec_gain, dec_bias, w_qkv, w_proj, proj_bias,
 ):
+    vmem = pl.BlockSpec(memory_space=pltpu.VMEM)
+    smem = pl.BlockSpec(memory_space=pltpu.SMEM)
+    hbm = pl.BlockSpec(memory_space=pltpu.HBM)
     my_index = lax.axis_index(DP).astype(jnp.int32)
     core = lax.axis_index("core").astype(jnp.int32)
-    residue = token_index[0, 0] % NDEV
-    w_full = lax.all_gather(w_qkv, "fsdp", axis=1, tiled=True)
-
-    mark = jnp.broadcast_to(residue.astype(BF), (2, 512))
-    shard = jnp.concatenate([w_e2d, mark], axis=0)
-    gathered = lax.all_to_all(
-        jnp.broadcast_to(shard[None], (32, 24, 512)), PLANE, 0, 0, tiled=True
-    )
+
+    shards = pl.pallas_call(
+        shard_kernel,
+        out_shape=jax.ShapeDtypeStruct((32, 24, 512), BF),
+        in_specs=[smem, vmem],
+        compiler_params=pltpu.CompilerParams(vmem_limit_bytes=8 * MIB),
+        name="shards",
+    )(token_index, w_e2d)
+    gathered = lax.all_to_all(shards, PLANE, 0, 0, tiled=True)
     own = gathered.reshape(768, 512)
     other = lax.ppermute(own, "core", [(0, 1), (1, 0)])
 
-    ids = jnp.stack([residue, my_index, core])
+    half = lax.dynamic_slice(w_qkv, (core * 256, 0), (256, 128))[None]
+    above = lax.ppermute(half, "fsdp", [(z, (z + 4) % 12) for z in range(12)])
+    below = lax.ppermute(half, "fsdp", [(z, (z + 8) % 12) for z in range(12)])
+
+    ids = jnp.stack([token_index[0, 0] & 63, my_index, core])
     normed, pick, info = pl.pallas_call(
         prep_kernel,
         out_shape=(
@@ -153,7 +230,7 @@
             jax.ShapeDtypeStruct((640, VMAX), BF),
             jax.ShapeDtypeStruct((8, 128), jnp.int32),
         ),
-        in_specs=[pl.BlockSpec(memory_space=pltpu.SMEM)] + [pl.BlockSpec(memory_space=pltpu.VMEM)] * 5,
+        in_specs=[smem] + [vmem] * 5,
         compiler_params=pltpu.CompilerParams(vmem_limit_bytes=24 * MIB),
         cost_estimate=pl.CostEstimate(flops=4_000_000_000, bytes_accessed=4_000_000, transcendentals=0),
         name="prep",
@@ -167,14 +244,25 @@
         cost_estimate=pl.CostEstimate(flops=1_000_000_000, bytes_accessed=4_000_000, transcendentals=0),
         name="embed",
     )(normed, own, other, pick)
-    received = lax.all_to_all(sent.reshape(NDEV, 40, 128), DP, 0, 0, tiled=True).reshape(2560, 128)
+
+    above, below = lax.optimization_barrier((above, below, sent))[:2]
+    three = jnp.concatenate([half, above, below])
+    twin = lax.ppermute(three, "fsdp", [(z, z ^ 2) for z in range(12)])
+    received = lax.all_to_all(sent.reshape(NDEV, 40, 128), DP, 0, 0, tiled=True)
+    received = received.reshape(2560, 128)
+    six = jnp.concatenate([three, twin])
+    rest = lax.ppermute(six, "fsdp", [(z, z ^ 1) for z in range(12)])
+    six_swap = lax.ppermute(six, "core", [(0, 1), (1, 0)])
+    rest_swap = lax.ppermute(rest, "core", [(0, 1), (1, 0)])
+    where = jnp.asarray(gather_table())[lax.axis_index("fsdp")]
+    where = where + core * jnp.asarray(np.arange(8) == 3, np.int32)
 
     column = np.arange(512)
     rate = np.power(10000.0, -(2 * (column // 2)) / 512.0).astype(np.float32)
     phase = np.where(column % 2 == 0, 0.0, math.pi / 2).astype(np.float32)
-    codes = jnp.sin(dec_tubes[0].astype(F32)[..., None] * rate + phase)
     position = jnp.arange(512, dtype=jnp.int32)
     visible = position[None, :] < info[2:4, :1]
+    codes = jnp.sin(dec_tubes[0].astype(F32)[..., None] * rate + phase)
     base = jnp.where(visible[..., None], 0.0, mask_token) + codes
 
     own_mark = own.reshape(32, 24, 512)[:, 22, 0]
@@ -188,35 +276,37 @@
     wanted = jnp.where(rank[None, :] < info[2:4, :1], wanted, -1)
     seat = (wanted[:, :, None] == offered[None, None, :]).astype(BF)
 
+    clip_block = pl.BlockSpec((1, 512, 512), lambda clip: (clip, 0, 0))
+    total, dec_normed = pl.pallas_call(
+        first_kernel,
+        grid=(2,),
+        out_shape=(jax.ShapeDtypeStruct((2, 512, 512), F32), jax.ShapeDtypeStruct((2, 512, 512), BF)),
+        in_specs=[smem, pl.BlockSpec(memory_space=pl.ANY)] + [hbm] * 5 + [whole((1, 512))] * 3,
+        out_specs=(clip_block, clip_block),
+        scratch_shapes=[
+            pltpu.VMEM((2560, 128), BF),
+            pltpu.VMEM((2, VMAX, VMAX), BF),
+            pltpu.VMEM((2, 512, 512), F32),
+            pltpu.VMEM((512, 768), BF),
+            pltpu.VMEM((512, 512), BF),
+            pltpu.VMEM((2560, 128), F32),
+            pltpu.SemaphoreType.DMA((16,)),
+        ],
+        compiler_params=pltpu.CompilerParams(vmem_limit_bytes=FIRST * MIB),
+        cost_estimate=pl.CostEstimate(flops=2_000_000_000, bytes_accessed=8_000_000, transcendentals=2_000_000),
+        name="heads1",
+    )(where, received, seat, base, six, six_swap, w_proj, dec_gain[None], dec_bias[None], proj_bias[None])
     return pl.pallas_call(
-        decode_kernel,
+        second_kernel,
         grid=(2,),
         out_shape=jax.ShapeDtypeStruct((1, 2, 512, 512), BF),
-        in_specs=[
-            whole((2560, 128)),
-            pl.BlockSpec((1, VMAX, VMAX), lambda clip: (clip, 0, 0)),
-            pl.BlockSpec((512, 512), lambda clip: (clip, 0)),
-            whole((1, 512)),
-            whole((1, 512)),
-            whole((512, 1024)),
-            whole((512, 512)),
-            whole((512, 512)),
-            whole((1, 512)),
-        ],
+        in_specs=[smem, clip_block, clip_block, hbm, hbm, whole((512, 512))],
         out_specs=pl.BlockSpec((None, 1, 512, 512), lambda clip: (0, clip, 0, 0)),
-        scratch_shapes=[
-            pltpu.VMEM((2560, 128), F32),
-            pltpu.VMEM((512, 512), F32),
-            pltpu.VMEM((HEADS, HEAD + 16, 512), BF),
-            pltpu.VMEM((512, 512), BF),
-        ],
-        compiler_params=pltpu.CompilerParams(vmem_limit_bytes=32 * MIB),
-        cost_estimate=pl.CostEstimate(flops=4_000_000_000, bytes_accessed=8_000_000, transcendentals=4_000_000),
-        name="decode",
-    )(
-        received, seat, base.reshape(1024, 512), dec_gain[None], dec_bias[None],
-        w_full[:, :1024], w_full[:, 1024:].T, w_proj, proj_bias[None],
-    )
+        scratch_shapes=[pltpu.VMEM((512, 768), BF), pltpu.SemaphoreType.DMA((12,))],
+        compiler_params=pltpu.CompilerParams(vmem_limit_bytes=SECOND * MIB),
+        cost_estimate=pl.CostEstimate(flops=2_000_000_000, bytes_accessed=8_000_000, transcendentals=2_000_000),
+        name="heads2",
+    )(where, total, dec_normed, rest, rest_swap, w_proj)
 
 
 def solution(mesh):

time: 120 us -> 111 us (0.925)
  the two profiles are of different devices: /device:TPU:2 before, /device:TPU:1 now
where the time goes in v3:
time: 111 us; the launch traced here: 110 us
  starting transfers between devices  53.8 us (48%)
  Pallas kernels  25.8 us (23%)
  waiting for transfers between devices  13.2 us (12%)
  other arithmetic  10.9 us (10%)
  local copies, waits for them, and re-layouts  5.19 us (5%)
    pallas_call x1, Pallas kernels, on_device(): pl.pallas_call(first_kernel, grid=(2,), out_shape=(jax.ShapeDtypeStruct((...  11.3 us
    ppermute x1, starting transfers between devices, on_device(): above = lax.ppermute(half, 'fsdp', [(z, (z + 4) % 12) for z in range(12)])  10.6 us
    all_to_all x1, starting transfers between devices, on_device(): gathered = lax.all_to_all(shards, PLANE, 0, 0, tiled=True)  10.5 us
    pallas_call x1, Pallas kernels, on_device(): pl.pallas_call(second_kernel, grid=(2,), out_shape=jax.ShapeDtypeStruct((...  8.99 us
    all_to_all x1, starting transfers between devices, on_device(): received = lax.all_to_all(sent.reshape(NDEV, 40, 128), DP, 0, 0, tiled=True)  8.96 us
    add x1, other arithmetic, on_device(): base = jnp.where(visible[..., None], 0.0, mask_token) + codes  8.46 us
    ppermute x1, waiting for transfers between devices, on_device(): twin = lax.ppermute(three, 'fsdp', [(z, z ^ 2) for z in range(12)])  8.28 us
    ppermute x1, starting transfers between devices, on_device(): below = lax.ppermute(half, 'fsdp', [(z, (z + 8) % 12) for z in range(12)])  5.56 us
  transfers between devices with their start and end apart: 9, of which 2 were waited for; matrix products, arithmetic and copies ran while one was open for 11% of the time, Pallas kernels for 14%

profile of v3, /device:TPU:1, one launch (start us, length us, event | category | flops | bytes accessed | tf_op | source)
XLA Modules:
  0.0 109.9 jit_solution(14463590591004128162)
XLA Ops:
  0.0 0.8 copy-done.1
  0.8 0.7 copy-done.2
  1.5 1.5 %shards.1 = bf16[32,24,512]{2,1,0:T(8,128)(2,1)} custom-call(s32[1,320]{1,0:T(1,128)S(1)} %copy-done.2, bf16[22,512]{1,0:T(8,128)(2,1)S(1)} %copy-done.1), custom_call_target="tpu_custom_call" | custom-call | tf_op jit(solution)/shard_map/shards/pallas_call | solution.py:210
  3.0 10.5 %all-to-all-start = ((bf16[32,24,512]{2,1,0:T(8,128)(2,1)}), bf16[32,24,512]{2,1,0:T(8,128)(2,1)S(1)}, u32[]{:S(2)}, u32[]{:S(2)}) async-start(bf16[32,24,512]{2,1,0:T(8,128)(2,1)} %shards.1), calls=%async_computation | async-start | bytes 1572864 | tf_op jit(solution)/shard_map/all_to_all | solution.py:217
  13.5 10.6 %collective-permute-start.1 = (bf16[1,256,128]{2,1,0:T(8,128)(2,1)S(1)}, bf16[1,256,128]{2,1,0:T(8,128)(2,1)S(1)}, u32[]{:S(2)}, u32[]{:S(2)}) collective-permute-start(bf16[1,256,128]{2,1,0:T(8,128)(2,1)S(1)} %dynamic-slice_bitcast_fusion), channel_id=1, source_target_pairs={{0,4},{1,5},{2,6},{3,7},{4,8},{5,9},{6,10},{7,11},{8,0},{9,1},{10,... | collective-permute-start | bytes 196616 | tf_op jit(solution)/shard_map/ppermute | solution.py:222
  24.1 5.6 %collective-permute-start.2 = (bf16[1,256,128]{2,1,0:T(8,128)(2,1)S(1)}, bf16[1,256,128]{2,1,0:T(8,128)(2,1)S(1)}, u32[]{:S(2)}, u32[]{:S(2)}) collective-permute-start(bf16[1,256,128]{2,1,0:T(8,128)(2,1)S(1)} %dynamic-slice_bitcast_fusion), channel_id=1, source_target_pairs={{0,8},{1,9},{2,10},{3,11},{4,0},{5,1},{6,2},{7,3},{8,4},{9,5},{10,... | collective-permute-start | bytes 196616 | tf_op jit(solution)/shard_map/ppermute | solution.py:223
  29.7 1.2 %slice.27 = s32[1,1]{1,0:T(1,128)} slice(s32[1,320]{1,0:T(1,128)} %ids_ref.1), slice={[0:1], [0:1]} | slice | bytes 8 | tf_op jit(solution)/shard_map/slice | solution.py:225
  31.6 1.2 %copy-done.3 = bf16[1,320,1408]{2,1,0:T(8,128)(2,1)S(1)} copy-done((bf16[1,320,1408]{2,1,0:T(8,128)(2,1)S(1)}, bf16[1,320,1408]{2,1,0:T(8,128)(2,1)}, u32[]{:S(2)}) %copy-start.3) | copy-done | bytes 901144
  32.8 2.0 %prep.1 = (bf16[2,320,768]{2,1,0:T(8,128)(2,1)S(1)}, bf16[640,320]{1,0:T(8,128)(2,1)S(1)}, s32[8,128]{1,0:T(8,128)S(1)}) custom-call(s32[3]{0:T(128)S(1)} %pad_add_fusion.ids_ref, bf16[320,1408]{1,0:T(8,128)(2,1)S(1)} %bitcast.22, f32[1,1408]{1,0:T(1,128)S(1)} %broadcast_in_dim.49.gain_ref, f32[1,1408]{1,0:T(1,128)S(1)} %broadcast_in_dim.50.bias_ref, ...), custom_call_target="tpu_custom_call" | custom-call | flops 4000000000 | bytes 4000000 | tf_op jit(solution)/shard_map/prep/pallas_call | solution.py:226
  35.0 4.4 %collective-permute-start = (bf16[768,512]{1,0:T(8,128)(2,1)S(1)}, bf16[768,512]{1,0:T(8,128)(2,1)S(1)}, u32[]{:S(2)}, u32[]{:S(2)}) collective-permute-start(bf16[768,512]{1,0:T(8,128)(2,1)S(1)} %bitcast.19), channel_id=1, source_target_pairs={{0,12},{12,0},{1,13},{13,1},{2,14},{14,2},{3,15},{15,3},{4,16},{16... | collective-permute-start | bytes 2359304 | tf_op jit(solution)/shard_map/ppermute | solution.py:219
  39.5 8.5 %sine_add_fusion.base_hbm = f32[2,512,512]{2,1,0:T(8,128)} fusion(f32[512]{0:T(512)S(1)} %copy-done.15, f32[512]{0:T(512)S(1)} %copy-done.14, f32[2,512]{1,0:T(2,128)S(1)} %convert_bitcast_fusion, f32[512]{0:T(512)S(1)} %copy-done.13, pred[2,512]{1,0:T(4,128)(4,1)S(1)} %iota_compare_fusion), kind=kLoop, calls=%fused_computation | loop fusion | flops 2097152 | bytes 2108416 | tf_op jit(solution)/shard_map/add | solution.py:266
  47.9 2.0 %embed.1 = bf16[2560,128]{1,0:T(8,128)(2,1)} custom-call(bf16[2,320,768]{2,1,0:T(8,128)(2,1)S(1)} %get-tuple-element.12.normed_ref, bf16[768,512]{1,0:T(8,128)(2,1)S(1)} %bitcast.20, bf16[768,512]{1,0:T(8,128)(2,1)S(1)} %collective-permute-done.other_ref, bf16[640,320]{1,0:T(8,128)(2,1)S(1)} %get-tuple-element.13.pick_ref), custom_call_target="tpu_custom_call" | custom-call | flops 1000000000 | bytes 4000000 | tf_op jit(solution)/shard_map/embed/pallas_call | solution.py:239
  50.0 9.0 %all-to-all-start.1 = ((bf16[64,40,128]{2,1,0:T(8,128)(2,1)}), bf16[64,40,128]{2,1,0:T(8,128)(2,1)S(1)}, u32[]{:S(2)}, u32[]{:S(2)}) async-start(bf16[64,40,128]{2,1,0:T(8,128)(2,1)} %bitcast.6), calls=%async_computation.1 | async-start | bytes 1310720 | tf_op jit(solution)/shard_map/all_to_all | solution.py:251
  59.1 4.0 %collective-permute-start.3 = (bf16[3,256,128]{2,1,0:T(8,128)(2,1)S(1)}, bf16[3,256,128]{2,1,0:T(8,128)(2,1)S(1)}, u32[]{:S(2)}, u32[]{:S(2)}) collective-permute-start(bf16[3,256,128]{2,1,0:T(8,128)(2,1)S(1)} %pad_maximum_fusion.1), channel_id=1, source_target_pairs={{0,2},{1,3},{2,0},{3,1},{4,6},{5,7},{6,4},{7,5},{8,10},{9,11},{10,... | collective-permute-start | bytes 589832 | tf_op jit(solution)/shard_map/ppermute | solution.py:250
  63.1 0.7 bitcast_add_fusion.where_ref
  63.8 8.3 %collective-permute-done.3 = bf16[3,256,128]{2,1,0:T(8,128)(2,1)S(1)} collective-permute-done((bf16[3,256,128]{2,1,0:T(8,128)(2,1)S(1)}, bf16[3,256,128]{2,1,0:T(8,128)(2,1)S(1)}, u32[]{:S(2)}, u32[]{:S(2)}) %collective-permute-start.3) | collective-permute-done | bytes 196640 | tf_op jit(solution)/shard_map/ppermute | solution.py:250
  72.1 2.9 %collective-permute-start.5 = (bf16[6,256,128]{2,1,0:T(8,128)(2,1)S(1)}, bf16[6,256,128]{2,1,0:T(8,128)(2,1)S(1)}, u32[]{:S(2)}, u32[]{:S(2)}) collective-permute-start(bf16[6,256,128]{2,1,0:T(8,128)(2,1)S(1)} %pad_maximum_fusion.mine_hbm), channel_id=1, source_target_pairs={{0,1},{1,0},{2,3},{3,2},{4,5},{5,4},{6,7},{7,6},{8,9},{9,8},{10,11... | collective-permute-start | bytes 1179656 | tf_op jit(solution)/shard_map/ppermute | solution.py:254
  75.6 2.7 %collective-permute-start.4 = (bf16[6,256,128]{2,1,0:T(8,128)(2,1)S(1)}, bf16[6,256,128]{2,1,0:T(8,128)(2,1)S(1)}, u32[]{:S(2)}, u32[]{:S(2)}) collective-permute-start(bf16[6,256,128]{2,1,0:T(8,128)(2,1)S(1)} %pad_maximum_fusion.mine_hbm), channel_id=1, source_target_pairs={{0,12},{12,0},{1,13},{13,1},{2,14},{14,2},{3,15},{15,3},{4,16},{16... | collective-permute-start | bytes 1179656 | tf_op jit(solution)/shard_map/ppermute | solution.py:255
  78.5 4.9 %collective-permute-done.5.mine_hbm = bf16[6,256,128]{2,1,0:T(8,128)(2,1)S(1)} collective-permute-done((bf16[6,256,128]{2,1,0:T(8,128)(2,1)S(1)}, bf16[6,256,128]{2,1,0:T(8,128)(2,1)S(1)}, u32[]{:S(2)}, u32[]{:S(2)}) %collective-permute-start.5) | collective-permute-done | bytes 393248 | tf_op jit(solution)/shard_map/ppermute | solution.py:254
  83.4 4.2 %collective-permute-start.6 = (bf16[6,256,128]{2,1,0:T(8,128)(2,1)S(1)}, bf16[6,256,128]{2,1,0:T(8,128)(2,1)S(1)}, u32[]{:S(2)}, u32[]{:S(2)}) collective-permute-start(bf16[6,256,128]{2,1,0:T(8,128)(2,1)S(1)} %collective-permute-done.5.mine_hbm), channel_id=1, source_target_pairs={{0,12},{12,0},{1,13},{13,1},{2,14},{14,2},{3,15},{15,3},{4,16},{16... | collective-permute-start | bytes 1179656 | tf_op jit(solution)/shard_map/ppermute | solution.py:256
  87.6 1.0 compare_convert_fusion.seat_hbm
  88.6 0.8 copy-done.9
  89.4 11.3 %heads1.1 = (f32[2,512,512]{2,1,0:T(8,128)}, bf16[2,512,512]{2,1,0:T(8,128)(2,1)}) custom-call(s32[8]{0:T(128)S(1)} %bitcast_add_fusion.where_ref, bf16[2560,128]{1,0:T(8,128)(2,1)} %bitcast.26, bf16[2,320,320]{2,1,0:T(8,128)(2,1)} %compare_convert_fusion.seat_hbm, f32[2,512,512]{2,1,0:T(8,128)} %sine_add_fusion.base_hbm, ...), custom_call_target="tpu_custom_call" | custom-call | flops 2000000000 | bytes 8000000 | tf_op jit(solution)/shard_map/heads1/pallas_call | solution.py:280
  100.8 9.0 %heads2.1 = bf16[1,2,512,512]{3,2,1,0:T(8,128)(2,1)} custom-call(s32[8]{0:T(128)S(1)} %bitcast_add_fusion.where_ref, f32[2,512,512]{2,1,0:T(8,128)} %get-tuple-element.17.total_ref, bf16[2,512,512]{2,1,0:T(8,128)(2,1)} %get-tuple-element.18.normed_ref, bf16[6,256,128]{2,1,0:T(8,128)(2,1)S(1)} %collective-permute-done.5.mine_hbm, ...), custom_call_target="tpu_custom_call" | custom-call | flops 2000000000 | bytes 8000000 | tf_op jit(solution)/shard_map/heads2/pallas_call | solution.py:299
  (53 shorter events, 1.3 us)
Async XLA Ops:
  0.0 13.5 %copy-start = (bf16[512,128]{1,0:T(8,128)(2,1)S(1)}, bf16[512,128]{1,0:T(8,128)(2,1)}, u32[]{:S(2)}) copy-start(bf16[512,128]{1,0:T(8,128)(2,1)} %param.29) | copy-start | bytes 393220
  0.0 0.8 copy-start.1
  1.5 29.4 %copy-start.10 = (f32[1408]{0:T(1024)S(1)}, f32[1408]{0:T(1024)}, u32[]{:S(2)}) copy-start(f32[1408]{0:T(1024)} %param.19) | copy-start | bytes 16900
  1.5 29.4 %copy-start.11 = (f32[1408]{0:T(1024)S(1)}, f32[1408]{0:T(1024)}, u32[]{:S(2)}) copy-start(f32[1408]{0:T(1024)} %param.20) | copy-start | bytes 16900
  1.5 30.2 %copy-start.7 = (s32[1,128]{1,0:T(1,128)S(1)}, s32[1,128]{1,0:T(1,128)}, u32[]{:S(2)}) copy-start(s32[1,128]{1,0:T(1,128)} %counts_ref.1) | copy-start | bytes 1540
  1.5 30.2 %copy-start.8 = (s32[1,128]{1,0:T(1,128)S(1)}, s32[1,128]{1,0:T(1,128)}, u32[]{:S(2)}) copy-start(s32[1,128]{1,0:T(1,128)} %owner_ref.1) | copy-start | bytes 1540
  3.0 32.0 %all-to-all-start = ((bf16[32,24,512]{2,1,0:T(8,128)(2,1)}), bf16[32,24,512]{2,1,0:T(8,128)(2,1)S(1)}, u32[]{:S(2)}, u32[]{:S(2)}) async-start(bf16[32,24,512]{2,1,0:T(8,128)(2,1)} %shards.1), calls=%async_computation | async-start | bytes 1572864 | tf_op jit(solution)/shard_map/all_to_all | solution.py:217
  13.5 45.5 %collective-permute-start.1 = (bf16[1,256,128]{2,1,0:T(8,128)(2,1)S(1)}, bf16[1,256,128]{2,1,0:T(8,128)(2,1)S(1)}, u32[]{:S(2)}, u32[]{:S(2)}) collective-permute-start(bf16[1,256,128]{2,1,0:T(8,128)(2,1)S(1)} %dynamic-slice_bitcast_fusion), channel_id=1, source_target_pairs={{0,4},{1,5},{2,6},{3,7},{4,8},{5,9},{6,10},{7,11},{8,0},{9,1},{10,... | collective-permute-start | bytes 196616 | tf_op jit(solution)/shard_map/ppermute | solution.py:222
  24.1 34.9 %collective-permute-start.2 = (bf16[1,256,128]{2,1,0:T(8,128)(2,1)S(1)}, bf16[1,256,128]{2,1,0:T(8,128)(2,1)S(1)}, u32[]{:S(2)}, u32[]{:S(2)}) collective-permute-start(bf16[1,256,128]{2,1,0:T(8,128)(2,1)S(1)} %dynamic-slice_bitcast_fusion), channel_id=1, source_target_pairs={{0,8},{1,9},{2,10},{3,11},{4,0},{5,1},{6,2},{7,3},{8,4},{9,5},{10,... | collective-permute-start | bytes 196616 | tf_op jit(solution)/shard_map/ppermute | solution.py:223
  31.6 1.2 %copy-start.3 = (bf16[1,320,1408]{2,1,0:T(8,128)(2,1)S(1)}, bf16[1,320,1408]{2,1,0:T(8,128)(2,1)}, u32[]{:S(2)}) copy-start(bf16[1,320,1408]{2,1,0:T(8,128)(2,1)} %param.18) | copy-start | bytes 2703364
  32.8 6.6 %copy-start.12 = (s32[1,2,512]{2,1,0:T(2,128)S(1)}, s32[1,2,512]{2,1,0:T(2,128)}, u32[]{:S(2)}) copy-start(s32[1,2,512]{2,1,0:T(2,128)} %param.25) | copy-start | bytes 12292
  32.8 6.6 %copy-start.13 = (f32[512]{0:T(512)S(1)}, f32[512]{0:T(512)}, u32[]{:S(2)}) copy-start(f32[512]{0:T(512)} %param.26) | copy-start | bytes 6148
  32.8 6.6 %copy-start.14 = (f32[512]{0:T(512)S(1)}, f32[512]{0:T(512)}, u32[]{:S(2)}) copy-start(f32[512]{0:T(512)} %constant.51.clone) | copy-start | bytes 6148
  32.8 6.7 %copy-start.15 = (f32[512]{0:T(512)S(1)}, f32[512]{0:T(512)}, u32[]{:S(2)}) copy-start(f32[512]{0:T(512)} %constant.52.clone) | copy-start | bytes 6148
  35.0 13.0 %collective-permute-start = (bf16[768,512]{1,0:T(8,128)(2,1)S(1)}, bf16[768,512]{1,0:T(8,128)(2,1)S(1)}, u32[]{:S(2)}, u32[]{:S(2)}) collective-permute-start(bf16[768,512]{1,0:T(8,128)(2,1)S(1)} %bitcast.19), channel_id=1, source_target_pairs={{0,12},{12,0},{1,13},{13,1},{2,14},{14,2},{3,15},{15,3},{4,16},{16... | collective-permute-start | bytes 2359304 | tf_op jit(solution)/shard_map/ppermute | solution.py:219
  50.0 39.5 %copy-start.4 = (f32[512]{0:T(512)S(1)}, f32[512]{0:T(512)}, u32[]{:S(2)}) copy-start(f32[512]{0:T(512)} %param.27) | copy-start | bytes 6148
  50.0 39.5 %copy-start.5 = (f32[512]{0:T(512)S(1)}, f32[512]{0:T(512)}, u32[]{:S(2)}) copy-start(f32[512]{0:T(512)} %param.28) | copy-start | bytes 6148
  50.0 39.5 %copy-start.6 = (f32[512]{0:T(512)S(1)}, f32[512]{0:T(512)}, u32[]{:S(2)}) copy-start(f32[512]{0:T(512)} %param.31) | copy-start | bytes 6148
  50.0 38.6 %all-to-all-start.1 = ((bf16[64,40,128]{2,1,0:T(8,128)(2,1)}), bf16[64,40,128]{2,1,0:T(8,128)(2,1)S(1)}, u32[]{:S(2)}, u32[]{:S(2)}) async-start(bf16[64,40,128]{2,1,0:T(8,128)(2,1)} %bitcast.6), calls=%async_computation.1 | async-start | bytes 1310720 | tf_op jit(solution)/shard_map/all_to_all | solution.py:251
  59.1 13.0 %collective-permute-start.3 = (bf16[3,256,128]{2,1,0:T(8,128)(2,1)S(1)}, bf16[3,256,128]{2,1,0:T(8,128)(2,1)S(1)}, u32[]{:S(2)}, u32[]{:S(2)}) collective-permute-start(bf16[3,256,128]{2,1,0:T(8,128)(2,1)S(1)} %pad_maximum_fusion.1), channel_id=1, source_target_pairs={{0,2},{1,3},{2,0},{3,1},{4,6},{5,7},{6,4},{7,5},{8,10},{9,11},{10,... | collective-permute-start | bytes 589832 | tf_op jit(solution)/shard_map/ppermute | solution.py:250
  72.1 11.3 %collective-permute-start.5 = (bf16[6,256,128]{2,1,0:T(8,128)(2,1)S(1)}, bf16[6,256,128]{2,1,0:T(8,128)(2,1)S(1)}, u32[]{:S(2)}, u32[]{:S(2)}) collective-permute-start(bf16[6,256,128]{2,1,0:T(8,128)(2,1)S(1)} %pad_maximum_fusion.mine_hbm), channel_id=1, source_target_pairs={{0,1},{1,0},{2,3},{3,2},{4,5},{5,4},{6,7},{7,6},{8,9},{9,8},{10,11... | collective-permute-start | bytes 1179656 | tf_op jit(solution)/shard_map/ppermute | solution.py:254
  75.6 13.0 %collective-permute-start.4 = (bf16[6,256,128]{2,1,0:T(8,128)(2,1)S(1)}, bf16[6,256,128]{2,1,0:T(8,128)(2,1)S(1)}, u32[]{:S(2)}, u32[]{:S(2)}) collective-permute-start(bf16[6,256,128]{2,1,0:T(8,128)(2,1)S(1)} %pad_maximum_fusion.mine_hbm), channel_id=1, source_target_pairs={{0,12},{12,0},{1,13},{13,1},{2,14},{14,2},{3,15},{15,3},{4,16},{16... | collective-permute-start | bytes 1179656 | tf_op jit(solution)/shard_map/ppermute | solution.py:255
  83.4 17.4 %collective-permute-start.6 = (bf16[6,256,128]{2,1,0:T(8,128)(2,1)S(1)}, bf16[6,256,128]{2,1,0:T(8,128)(2,1)S(1)}, u32[]{:S(2)}, u32[]{:S(2)}) collective-permute-start(bf16[6,256,128]{2,1,0:T(8,128)(2,1)S(1)} %collective-permute-done.5.mine_hbm), channel_id=1, source_target_pairs={{0,12},{12,0},{1,13},{13,1},{2,14},{14,2},{3,15},{15,3},{4,16},{16... | collective-permute-start | bytes 1179656 | tf_op jit(solution)/shard_map/ppermute | solution.py:256
  88.6 0.8 copy-start.9
  (1 other events, 0.7 us)

commit v4 on v3

--- a/solution.py
+++ b/solution.py
@@ -16,6 +16,8 @@
 PER = 5
 FIRST = 53
 SECOND = 53
+AHEAD = 2
+CHUNK = 64
 EPS = 1e-06
 MIB = 1 << 20
 BF = jnp.bfloat16
@@ -26,10 +28,10 @@
     return lax.broadcasted_iota(jnp.int32, shape, dim)
 
 
-def prep_kernel(ids_ref, enc_ref, gain_ref, bias_ref, counts_ref, owner_ref, normed_ref, pick_ref, info_ref):
-    residue = ids_ref[0]
-    my_index = ids_ref[1]
-    core = ids_ref[2]
+def prep_kernel(ids_ref, token_ref, enc_ref, gain_ref, bias_ref, counts_ref, owner_ref, normed_ref, pick_ref, info_ref):
+    residue = token_ref[0, 0] & 63
+    my_index = ids_ref[0]
+    core = ids_ref[1]
     counts = counts_ref[...].astype(F32)
     row_id = iota((128, 128), 0)
     col_id = iota((128, 128), 1)
@@ -86,45 +88,55 @@
         out_ref[chip] = block
 
 
-def fetch_blocks(where_ref, mine_hbm, swap_hbm, weights_ref, sems):
+def fetch_blocks(where_ref, first, mine_hbm, swap_hbm, wproj_hbm, weights_ref, wproj_ref, sems):
     moves = []
+
+    def move(source, into):
+        moves.append(pltpu.make_async_copy(source, into, sems.at[len(moves)]))
+
     for pair in range(2):
         for kind in range(3):
             at = 3 * pair + where_ref[kind]
-            column = 384 * pair + 128 * kind
+            column = 256 * kind + 128 * pair
             for source, side in ((mine_hbm, where_ref[3]), (swap_hbm, 1 - where_ref[3])):
                 rows = pl.ds(pl.multiple_of(256 * side, 256), 256)
-                moves.append(
-                    pltpu.make_async_copy(
-                        source.at[at], weights_ref.at[rows, column : column + 128], sems.at[len(moves)]
-                    )
-                )
+                move(source.at[at], weights_ref.at[rows, column : column + 128])
+        rows = pl.ds(pl.multiple_of(128 * where_ref[first + pair], 128), 128)
+        move(wproj_hbm.at[rows, :], wproj_ref.at[128 * pair : 128 * (pair + 1), :])
     return moves
 
 
-def two_pairs(normed, weights_ref, wproj_ref, where_ref, first, total):
+def four_heads(normed, weights_ref, wproj_ref):
     across = (((1,), (1,)), ((), ()))
     left = iota((512, 128), 1) < HEAD
     zero = jnp.zeros((512, 128), BF)
     ones = jnp.ones((16, 512), BF)
-    for pair in range(2):
-        made = jnp.dot(normed, weights_ref[:, 384 * pair : 384 * (pair + 1)], preferred_element_type=F32)
-        queries = (made[:, :128] * (HEAD**-0.5 * math.log2(math.e))).astype(BF)
-        keys = made[:, 128:256].astype(BF)
-        values = made[:, 256:].T.astype(BF)
-        parts = []
-        for head in range(2):
-            key = jnp.where(left, keys, zero) if head == 0 else jnp.where(left, zero, keys)
-            scores = lax.dot_general(key, queries, across, preferred_element_type=F32)
-            top = jnp.max(scores, axis=0, keepdims=True)
-            weights = jnp.exp2(scores - top).astype(BF)
-            stacked = jnp.concatenate([values[HEAD * head : HEAD * (head + 1)], ones], axis=0)
-            mixed = jnp.dot(stacked, weights, preferred_element_type=F32)
-            parts.append(mixed[:HEAD] * (1.0 / mixed[HEAD : HEAD + 1]))
-        attended = jnp.concatenate(parts, axis=0).T.astype(BF)
-        rows = pl.ds(pl.multiple_of(128 * where_ref[first + pair], 128), 128)
-        total = total + jnp.dot(attended, wproj_ref[rows, :], preferred_element_type=F32)
-    return total
+    made = jnp.dot(normed, weights_ref[...], preferred_element_type=F32)
+    queries = (made[:, :256] * (HEAD**-0.5 * math.log2(math.e))).astype(BF)
+    keys = made[:, 256:512].astype(BF)
+    values = made[:, 512:].T.astype(BF)
+
+    def score(head):
+        pair = slice(128 * (head // 2), 128 * (head // 2 + 1))
+        key = keys[:, pair]
+        key = jnp.where(left, key, zero) if head % 2 == 0 else jnp.where(left, zero, key)
+        return lax.dot_general(key, queries[:, pair], across, preferred_element_type=F32)
+
+    def mix(head, scores):
+        top = jnp.max(scores, axis=0, keepdims=True)
+        weights = jnp.exp2(scores - top).astype(BF)
+        stacked = jnp.concatenate([values[HEAD * head : HEAD * (head + 1)], ones], axis=0)
+        mixed = jnp.dot(stacked, weights, preferred_element_type=F32)
+        return mixed[:HEAD] * (1.0 / mixed[HEAD : HEAD + 1])
+
+    scored = [score(head) for head in range(AHEAD)]
+    parts = []
+    for head in range(4):
+        if head + AHEAD < 4:
+            scored.append(score(head + AHEAD))
+        parts.append(mix(head, scored[head]))
+    attended = jnp.concatenate(parts, axis=0).T.astype(BF)
+    return jnp.dot(attended, wproj_ref[...], preferred_element_type=F32)
 
 
 def first_kernel(
@@ -133,17 +145,16 @@
 ):
     clip = pl.program_id(0)
     moves = [
-        pltpu.make_async_copy(source, into, sems.at[12 + n])
+        pltpu.make_async_copy(source, into, sems.at[14 + n])
         for n, (source, into) in enumerate(
-            ((recv_hbm, recv_ref), (seat_hbm, seat_ref), (base_hbm, base_ref), (wproj_hbm, wproj_ref))
+            ((recv_hbm, recv_ref), (seat_hbm, seat_ref), (base_hbm, base_ref))
         )
     ]
+    blocks = fetch_blocks(where_ref, 4, mine_hbm, swap_hbm, wproj_hbm, weights_ref, wproj_ref, sems)
 
     @pl.when(clip == 0)
     def _():
-        for move in moves:
-            move.start()
-        for move in fetch_blocks(where_ref, mine_hbm, swap_hbm, weights_ref, sems):
+        for move in moves + blocks:
             move.start()
         moves[0].wait()
         rows_ref[...] = recv_ref[...].astype(F32)
@@ -153,36 +164,41 @@
     tokens = jnp.concatenate(
         [rows_ref[pl.ds(4 * clip + part, VMAX, stride=8), :] for part in range(4)], axis=1
     ).astype(BF)
-    placed = jnp.dot(seat_ref[clip], tokens, preferred_element_type=F32)
-    values = jnp.concatenate([base_ref[clip, :VMAX, :] + placed, base_ref[clip, VMAX:, :]], axis=0)
-    average = jnp.mean(values, axis=1, keepdims=True)
-    centred = values - average
-    spread = jnp.mean(centred * centred, axis=1, keepdims=True)
-    normed = (centred * lax.rsqrt(spread + EPS) * gain_ref[...] + bias_ref[...]).astype(BF)
-    normed_ref[0] = normed
-    total_ref[0] = values + pbias_ref[...]
+    total_ref[0, :VMAX, :] = jnp.dot(seat_ref[clip], tokens, preferred_element_type=F32)
+    for low in range(0, 512, CHUNK):
+        rows = slice(low, low + CHUNK)
+        values = base_ref[clip, rows, :]
+        if low < VMAX:
+            values = values + total_ref[0, rows, :]
+        average = jnp.mean(values, axis=1, keepdims=True)
+        centred = values - average
+        spread = jnp.mean(centred * centred, axis=1, keepdims=True)
+        normed_ref[0, rows, :] = (
+            centred * lax.rsqrt(spread + EPS) * gain_ref[...] + bias_ref[...]
+        ).astype(BF)
+        total_ref[0, rows, :] = values + pbias_ref[...]
 
     @pl.when(clip == 0)
     def _():
-        for move in fetch_blocks(where_ref, mine_hbm, swap_hbm, weights_ref, sems):
+        for move in blocks:
             move.wait()
-        moves[3].wait()
-
-    total_ref[0] = two_pairs(normed, weights_ref, wproj_ref, where_ref, 4, total_ref[0])
+
+    total_ref[0] += four_heads(normed_ref[0], weights_ref, wproj_ref)
 
 
 def second_kernel(
-    where_ref, total_ref, normed_ref, mine_hbm, swap_hbm, wproj_ref, out_ref, weights_ref, sems
+    where_ref, total_ref, normed_ref, mine_hbm, swap_hbm, wproj_hbm, out_ref, weights_ref, wproj_ref, sems
 ):
     @pl.when(pl.program_id(0) == 0)
     def _():
-        moves = fetch_blocks(where_ref, mine_hbm, swap_hbm, weights_ref, sems)
+        moves = fetch_blocks(where_ref, 6, mine_hbm, swap_hbm, wproj_hbm, weights_ref, wproj_ref, sems)
         for move in moves:
             move.start()
         for move in moves:
             move.wait()
 
-    out_ref[0] = two_pairs(normed_ref[0], weights_ref, wproj_ref, where_ref, 6, total_ref[0]).astype(BF)
+    share = four_heads(normed_ref[0], weights_ref, wproj_ref)
+    out_ref[0] = (total_ref[0] + share).astype(BF)
 
 
 def gather_table():
@@ -222,7 +238,7 @@
     above = lax.ppermute(half, "fsdp", [(z, (z + 4) % 12) for z in range(12)])
     below = lax.ppermute(half, "fsdp", [(z, (z + 8) % 12) for z in range(12)])
 
-    ids = jnp.stack([token_index[0, 0] & 63, my_index, core])
+    ids = jnp.stack([my_index, core])
     normed, pick, info = pl.pallas_call(
         prep_kernel,
         out_shape=(
@@ -230,11 +246,11 @@
             jax.ShapeDtypeStruct((640, VMAX), BF),
             jax.ShapeDtypeStruct((8, 128), jnp.int32),
         ),
-        in_specs=[smem] + [vmem] * 5,
+        in_specs=[smem] * 2 + [vmem] * 5,
         compiler_params=pltpu.CompilerParams(vmem_limit_bytes=24 * MIB),
         cost_estimate=pl.CostEstimate(flops=4_000_000_000, bytes_accessed=4_000_000, transcendentals=0),
         name="prep",
-    )(ids, enc_out[0], norm_gain[None], norm_bias[None], counts, owner)
+    )(ids, token_index, enc_out[0], norm_gain[None], norm_bias[None], counts, owner)
 
     sent = pl.pallas_call(
         embed_kernel,
@@ -288,9 +304,9 @@
             pltpu.VMEM((2, VMAX, VMAX), BF),
             pltpu.VMEM((2, 512, 512), F32),
             pltpu.VMEM((512, 768), BF),
-            pltpu.VMEM((512, 512), BF),
+            pltpu.VMEM((256, 512), BF),
             pltpu.VMEM((2560, 128), F32),
-            pltpu.SemaphoreType.DMA((16,)),
+            pltpu.SemaphoreType.DMA((17,)),
         ],
         compiler_params=pltpu.CompilerParams(vmem_limit_bytes=FIRST * MIB),
         cost_estimate=pl.CostEstimate(flops=2_000_000_000, bytes_accessed=8_000_000, transcendentals=2_000_000),
@@ -300,9 +316,13 @@
         second_kernel,
         grid=(2,),
         out_shape=jax.ShapeDtypeStruct((1, 2, 512, 512), BF),
-        in_specs=[smem, clip_block, clip_block, hbm, hbm, whole((512, 512))],
+        in_specs=[smem, clip_block, clip_block, hbm, hbm, hbm],
         out_specs=pl.BlockSpec((None, 1, 512, 512), lambda clip: (0, clip, 0, 0)),
-        scratch_shapes=[pltpu.VMEM((512, 768), BF), pltpu.SemaphoreType.DMA((12,))],
+        scratch_shapes=[
+            pltpu.VMEM((512, 768), BF),
+            pltpu.VMEM((256, 512), BF),
+            pltpu.SemaphoreType.DMA((14,)),
+        ],
         compiler_params=pltpu.CompilerParams(vmem_limit_bytes=SECOND * MIB),
         cost_estimate=pl.CostEstimate(flops=2_000_000_000, bytes_accessed=8_000_000, transcendentals=2_000_000),
         name="heads2",

time: 111 us -> 105 us (0.946)
  Pallas kernels: 25.8 us -> 21.9 us
  local copies, waits for them, and re-layouts: 5.19 us -> 4.01 us
    pallas_call x1, Pallas kernels: 11.3 us -> 8.92 us  [on_device(): pl.pallas_call(first_kernel, grid=(2,), out_shape=(jax.ShapeDtypeStruct((...]
    all_to_all x1, starting transfers between devices: 8.96 us -> 7.2 us  [on_device(): received = lax.all_to_all(sent.reshape(NDEV, 40, 128), DP, 0, 0, tiled=True)]
    ppermute x1, starting transfers between devices: 4.36 us -> 6.13 us  [on_device(): other = lax.ppermute(own, 'core', [(0, 1), (1, 0)])]
    pallas_call x1, Pallas kernels: 8.99 us -> 7.43 us  [on_device(): pl.pallas_call(second_kernel, grid=(2,), out_shape=jax.ShapeDtypeStruct((...]
    slice x1 -> x0, local copies, waits for them, and re-layouts: 1.18 us -> none  [on_device(): ids = jnp.stack([token_index[0, 0] & 63, my_index, core])]
    unnamed x32 -> x34, local copies, waits for them, and re-layouts: 3.5 us -> 3.51 us
  transfers between devices with their start and end apart: 9 -> 9, of which waited for: 2 -> 2; matrix products, arithmetic and copies ran while one was open for 11% -> 11% of each run, Pallas kernels for 14% -> 12%
where the time goes in v4:
time: 105 us; the launch traced here: 104 us
  starting transfers between devices  53.7 us (51%)
  Pallas kernels  21.9 us (21%)
  waiting for transfers between devices  13.2 us (13%)
  other arithmetic  10.9 us (10%)
  local copies, waits for them, and re-layouts  4.01 us (4%)
    ppermute x1, starting transfers between devices, on_device(): above = lax.ppermute(half, 'fsdp', [(z, (z + 4) % 12) for z in range(12)])  10.6 us
    all_to_all x1, starting transfers between devices, on_device(): gathered = lax.all_to_all(shards, PLANE, 0, 0, tiled=True)  10.5 us
    pallas_call x1, Pallas kernels, on_device(): pl.pallas_call(first_kernel, grid=(2,), out_shape=(jax.ShapeDtypeStruct((...  8.92 us
    add x1, other arithmetic, on_device(): base = jnp.where(visible[..., None], 0.0, mask_token) + codes  8.46 us
    ppermute x1, waiting for transfers between devices, on_device(): twin = lax.ppermute(three, 'fsdp', [(z, z ^ 2) for z in range(12)])  8.28 us
    pallas_call x1, Pallas kernels, on_device(): pl.pallas_call(second_kernel, grid=(2,), out_shape=jax.ShapeDtypeStruct((...  7.43 us
    all_to_all x1, starting transfers between devices, on_device(): received = lax.all_to_all(sent.reshape(NDEV, 40, 128), DP, 0, 0, tiled=True)  7.2 us
    ppermute x1, starting transfers between devices, on_device(): other = lax.ppermute(own, 'core', [(0, 1), (1, 0)])  6.13 us
  transfers between devices with their start and end apart: 9, of which 2 were waited for; matrix products, arithmetic and copies ran while one was open for 11% of the time, Pallas kernels for 12%

profile of v4, /device:TPU:1, one launch (start us, length us, event | category | flops | bytes accessed | tf_op | source)
XLA Modules:
  0.0 103.9 jit_solution(10481118701324665428)
XLA Ops:
  0.0 0.8 copy-done.1
  0.8 0.7 copy-done.2
  1.5 1.5 %shards.1 = bf16[32,24,512]{2,1,0:T(8,128)(2,1)} custom-call(s32[1,320]{1,0:T(1,128)S(1)} %copy-done.2, bf16[22,512]{1,0:T(8,128)(2,1)S(1)} %copy-done.1), custom_call_target="tpu_custom_call" | custom-call | tf_op jit(solution)/shard_map/shards/pallas_call | solution.py:226
  3.0 10.5 %all-to-all-start = ((bf16[32,24,512]{2,1,0:T(8,128)(2,1)}), bf16[32,24,512]{2,1,0:T(8,128)(2,1)S(1)}, u32[]{:S(2)}, u32[]{:S(2)}) async-start(bf16[32,24,512]{2,1,0:T(8,128)(2,1)} %shards.1), calls=%async_computation | async-start | bytes 1572864 | tf_op jit(solution)/shard_map/all_to_all | solution.py:233
  13.5 10.6 %collective-permute-start.1 = (bf16[1,256,128]{2,1,0:T(8,128)(2,1)S(1)}, bf16[1,256,128]{2,1,0:T(8,128)(2,1)S(1)}, u32[]{:S(2)}, u32[]{:S(2)}) collective-permute-start(bf16[1,256,128]{2,1,0:T(8,128)(2,1)S(1)} %dynamic-slice_bitcast_fusion), channel_id=1, source_target_pairs={{0,4},{1,5},{2,6},{3,7},{4,8},{5,9},{6,10},{7,11},{8,0},{9,1},{10,... | collective-permute-start | bytes 196616 | tf_op jit(solution)/shard_map/ppermute | solution.py:238
  24.1 5.6 %collective-permute-start.2 = (bf16[1,256,128]{2,1,0:T(8,128)(2,1)S(1)}, bf16[1,256,128]{2,1,0:T(8,128)(2,1)S(1)}, u32[]{:S(2)}, u32[]{:S(2)}) collective-permute-start(bf16[1,256,128]{2,1,0:T(8,128)(2,1)S(1)} %dynamic-slice_bitcast_fusion), channel_id=1, source_target_pairs={{0,8},{1,9},{2,10},{3,11},{4,0},{5,1},{6,2},{7,3},{8,4},{9,5},{10,... | collective-permute-start | bytes 196616 | tf_op jit(solution)/shard_map/ppermute | solution.py:239
  29.9 1.2 %copy-done.4 = bf16[1,320,1408]{2,1,0:T(8,128)(2,1)S(1)} copy-done((bf16[1,320,1408]{2,1,0:T(8,128)(2,1)S(1)}, bf16[1,320,1408]{2,1,0:T(8,128)(2,1)}, u32[]{:S(2)}) %copy-start.4) | copy-done | bytes 901144
  31.0 2.0 %prep.1 = (bf16[2,320,768]{2,1,0:T(8,128)(2,1)S(1)}, bf16[640,320]{1,0:T(8,128)(2,1)S(1)}, s32[8,128]{1,0:T(8,128)S(1)}) custom-call(s32[2]{0:T(128)S(1)} %pad_add_fusion.ids_ref, s32[1,320]{1,0:T(1,128)S(1)} %copy-done.3, bf16[320,1408]{1,0:T(8,128)(2,1)S(1)} %bitcast.21, f32[1,1408]{1,0:T(1,128)S(1)} %broadcast_in_dim.49.gain_ref, ...), custom_call_target="tpu_custom_call" | custom-call | flops 4000000000 | bytes 4000000 | tf_op jit(solution)/shard_map/prep/pallas_call | solution.py:242
  33.2 6.1 %collective-permute-start = (bf16[768,512]{1,0:T(8,128)(2,1)S(1)}, bf16[768,512]{1,0:T(8,128)(2,1)S(1)}, u32[]{:S(2)}, u32[]{:S(2)}) collective-permute-start(bf16[768,512]{1,0:T(8,128)(2,1)S(1)} %bitcast.18), channel_id=1, source_target_pairs={{0,12},{12,0},{1,13},{13,1},{2,14},{14,2},{3,15},{15,3},{4,16},{16... | collective-permute-start | bytes 2359304 | tf_op jit(solution)/shard_map/ppermute | solution.py:235
  39.5 8.5 %sine_add_fusion.base_hbm = f32[2,512,512]{2,1,0:T(8,128)} fusion(f32[512]{0:T(512)S(1)} %copy-done.16, f32[512]{0:T(512)S(1)} %copy-done.15, f32[2,512]{1,0:T(2,128)S(1)} %convert_bitcast_fusion, f32[512]{0:T(512)S(1)} %copy-done.14, pred[2,512]{1,0:T(4,128)(4,1)S(1)} %iota_compare_fusion), kind=kLoop, calls=%fused_computation | loop fusion | flops 2097152 | bytes 2108416 | tf_op jit(solution)/shard_map/add | solution.py:282
  48.0 2.0 %embed.1 = bf16[2560,128]{1,0:T(8,128)(2,1)} custom-call(bf16[2,320,768]{2,1,0:T(8,128)(2,1)S(1)} %get-tuple-element.12.normed_ref, bf16[768,512]{1,0:T(8,128)(2,1)S(1)} %bitcast.19, bf16[768,512]{1,0:T(8,128)(2,1)S(1)} %collective-permute-done.other_ref, bf16[640,320]{1,0:T(8,128)(2,1)S(1)} %get-tuple-element.13.pick_ref), custom_call_target="tpu_custom_call" | custom-call | flops 1000000000 | bytes 4000000 | tf_op jit(solution)/shard_map/embed/pallas_call | solution.py:255
  50.0 7.2 %all-to-all-start.1 = ((bf16[64,40,128]{2,1,0:T(8,128)(2,1)}), bf16[64,40,128]{2,1,0:T(8,128)(2,1)S(1)}, u32[]{:S(2)}, u32[]{:S(2)}) async-start(bf16[64,40,128]{2,1,0:T(8,128)(2,1)} %bitcast.5), calls=%async_computation.1 | async-start | bytes 1310720 | tf_op jit(solution)/shard_map/all_to_all | solution.py:267
  57.3 4.0 %collective-permute-start.3 = (bf16[3,256,128]{2,1,0:T(8,128)(2,1)S(1)}, bf16[3,256,128]{2,1,0:T(8,128)(2,1)S(1)}, u32[]{:S(2)}, u32[]{:S(2)}) collective-permute-start(bf16[3,256,128]{2,1,0:T(8,128)(2,1)S(1)} %pad_maximum_fusion.1), channel_id=1, source_target_pairs={{0,2},{1,3},{2,0},{3,1},{4,6},{5,7},{6,4},{7,5},{8,10},{9,11},{10,... | collective-permute-start | bytes 589832 | tf_op jit(solution)/shard_map/ppermute | solution.py:266
  61.3 0.7 bitcast_add_fusion.where_ref
  62.0 8.3 %collective-permute-done.3 = bf16[3,256,128]{2,1,0:T(8,128)(2,1)S(1)} collective-permute-done((bf16[3,256,128]{2,1,0:T(8,128)(2,1)S(1)}, bf16[3,256,128]{2,1,0:T(8,128)(2,1)S(1)}, u32[]{:S(2)}, u32[]{:S(2)}) %collective-permute-start.3) | collective-permute-done | bytes 196640 | tf_op jit(solution)/shard_map/ppermute | solution.py:266
  70.4 2.9 %collective-permute-start.5 = (bf16[6,256,128]{2,1,0:T(8,128)(2,1)S(1)}, bf16[6,256,128]{2,1,0:T(8,128)(2,1)S(1)}, u32[]{:S(2)}, u32[]{:S(2)}) collective-permute-start(bf16[6,256,128]{2,1,0:T(8,128)(2,1)S(1)} %pad_maximum_fusion.mine_hbm), channel_id=1, source_target_pairs={{0,1},{1,0},{2,3},{3,2},{4,5},{5,4},{6,7},{7,6},{8,9},{9,8},{10,11... | collective-permute-start | bytes 1179656 | tf_op jit(solution)/shard_map/ppermute | solution.py:270
  73.3 0.3 fusion
  73.8 2.7 %collective-permute-start.4 = (bf16[6,256,128]{2,1,0:T(8,128)(2,1)S(1)}, bf16[6,256,128]{2,1,0:T(8,128)(2,1)S(1)}, u32[]{:S(2)}, u32[]{:S(2)}) collective-permute-start(bf16[6,256,128]{2,1,0:T(8,128)(2,1)S(1)} %pad_maximum_fusion.mine_hbm), channel_id=1, source_target_pairs={{0,12},{12,0},{1,13},{13,1},{2,14},{14,2},{3,15},{15,3},{4,16},{16... | collective-permute-start | bytes 1179656 | tf_op jit(solution)/shard_map/ppermute | solution.py:271
  76.7 4.9 %collective-permute-done.5.mine_hbm = bf16[6,256,128]{2,1,0:T(8,128)(2,1)S(1)} collective-permute-done((bf16[6,256,128]{2,1,0:T(8,128)(2,1)S(1)}, bf16[6,256,128]{2,1,0:T(8,128)(2,1)S(1)}, u32[]{:S(2)}, u32[]{:S(2)}) %collective-permute-start.5) | collective-permute-done | bytes 393248 | tf_op jit(solution)/shard_map/ppermute | solution.py:270
  81.6 4.1 %collective-permute-start.6 = (bf16[6,256,128]{2,1,0:T(8,128)(2,1)S(1)}, bf16[6,256,128]{2,1,0:T(8,128)(2,1)S(1)}, u32[]{:S(2)}, u32[]{:S(2)}) collective-permute-start(bf16[6,256,128]{2,1,0:T(8,128)(2,1)S(1)} %collective-permute-done.5.mine_hbm), channel_id=1, source_target_pairs={{0,12},{12,0},{1,13},{13,1},{2,14},{14,2},{3,15},{15,3},{4,16},{16... | collective-permute-start | bytes 1179656 | tf_op jit(solution)/shard_map/ppermute | solution.py:272
  85.7 1.0 compare_convert_fusion.seat_hbm
  86.7 0.8 copy-done.10
  87.5 8.9 %heads1.1 = (f32[2,512,512]{2,1,0:T(8,128)}, bf16[2,512,512]{2,1,0:T(8,128)(2,1)}) custom-call(s32[8]{0:T(128)S(1)} %bitcast_add_fusion.where_ref, bf16[2560,128]{1,0:T(8,128)(2,1)} %bitcast.25, bf16[2,320,320]{2,1,0:T(8,128)(2,1)} %compare_convert_fusion.seat_hbm, f32[2,512,512]{2,1,0:T(8,128)} %sine_add_fusion.base_hbm, ...), custom_call_target="tpu_custom_call" | custom-call | flops 2000000000 | bytes 8000000 | tf_op jit(solution)/shard_map/heads1/pallas_call | solution.py:296
  96.5 7.4 %heads2.1 = bf16[1,2,512,512]{3,2,1,0:T(8,128)(2,1)} custom-call(s32[8]{0:T(128)S(1)} %bitcast_add_fusion.where_ref, f32[2,512,512]{2,1,0:T(8,128)} %get-tuple-element.17.total_ref, bf16[2,512,512]{2,1,0:T(8,128)(2,1)} %get-tuple-element.18.normed_ref, bf16[6,256,128]{2,1,0:T(8,128)(2,1)S(1)} %collective-permute-done.5.mine_hbm, ...), custom_call_target="tpu_custom_call" | custom-call | flops 2000000000 | bytes 8000000 | tf_op jit(solution)/shard_map/heads2/pallas_call | solution.py:315
  (54 shorter events, 1.0 us)
Async XLA Ops:
  0.0 13.5 %copy-start = (bf16[512,128]{1,0:T(8,128)(2,1)S(1)}, bf16[512,128]{1,0:T(8,128)(2,1)}, u32[]{:S(2)}) copy-start(bf16[512,128]{1,0:T(8,128)(2,1)} %param.29) | copy-start | bytes 393220
  1.5 28.3 %copy-start.11 = (f32[1408]{0:T(1024)S(1)}, f32[1408]{0:T(1024)}, u32[]{:S(2)}) copy-start(f32[1408]{0:T(1024)} %param.19) | copy-start | bytes 16900
  1.5 28.3 %copy-start.12 = (f32[1408]{0:T(1024)S(1)}, f32[1408]{0:T(1024)}, u32[]{:S(2)}) copy-start(f32[1408]{0:T(1024)} %param.20) | copy-start | bytes 16900
  1.5 28.4 %copy-start.3 = (s32[1,320]{1,0:T(1,128)S(1)}, s32[1,320]{1,0:T(1,128)}, u32[]{:S(2)}) copy-start(s32[1,320]{1,0:T(1,128)} %ids_ref.1) | copy-start | bytes 3844
  1.5 28.4 %copy-start.8 = (s32[1,128]{1,0:T(1,128)S(1)}, s32[1,128]{1,0:T(1,128)}, u32[]{:S(2)}) copy-start(s32[1,128]{1,0:T(1,128)} %counts_ref.1) | copy-start | bytes 1540
  1.5 28.4 %copy-start.9 = (s32[1,128]{1,0:T(1,128)S(1)}, s32[1,128]{1,0:T(1,128)}, u32[]{:S(2)}) copy-start(s32[1,128]{1,0:T(1,128)} %owner_ref.1) | copy-start | bytes 1540
  3.0 30.3 %all-to-all-start = ((bf16[32,24,512]{2,1,0:T(8,128)(2,1)}), bf16[32,24,512]{2,1,0:T(8,128)(2,1)S(1)}, u32[]{:S(2)}, u32[]{:S(2)}) async-start(bf16[32,24,512]{2,1,0:T(8,128)(2,1)} %shards.1), calls=%async_computation | async-start | bytes 1572864 | tf_op jit(solution)/shard_map/all_to_all | solution.py:233
  13.5 43.8 %collective-permute-start.1 = (bf16[1,256,128]{2,1,0:T(8,128)(2,1)S(1)}, bf16[1,256,128]{2,1,0:T(8,128)(2,1)S(1)}, u32[]{:S(2)}, u32[]{:S(2)}) collective-permute-start(bf16[1,256,128]{2,1,0:T(8,128)(2,1)S(1)} %dynamic-slice_bitcast_fusion), channel_id=1, source_target_pairs={{0,4},{1,5},{2,6},{3,7},{4,8},{5,9},{6,10},{7,11},{8,0},{9,1},{10,... | collective-permute-start | bytes 196616 | tf_op jit(solution)/shard_map/ppermute | solution.py:238
  24.1 33.1 %collective-permute-start.2 = (bf16[1,256,128]{2,1,0:T(8,128)(2,1)S(1)}, bf16[1,256,128]{2,1,0:T(8,128)(2,1)S(1)}, u32[]{:S(2)}, u32[]{:S(2)}) collective-permute-start(bf16[1,256,128]{2,1,0:T(8,128)(2,1)S(1)} %dynamic-slice_bitcast_fusion), channel_id=1, source_target_pairs={{0,8},{1,9},{2,10},{3,11},{4,0},{5,1},{6,2},{7,3},{8,4},{9,5},{10,... | collective-permute-start | bytes 196616 | tf_op jit(solution)/shard_map/ppermute | solution.py:239
  29.9 1.2 %copy-start.4 = (bf16[1,320,1408]{2,1,0:T(8,128)(2,1)S(1)}, bf16[1,320,1408]{2,1,0:T(8,128)(2,1)}, u32[]{:S(2)}) copy-start(bf16[1,320,1408]{2,1,0:T(8,128)(2,1)} %param.18) | copy-start | bytes 2703364
  31.0 8.4 %copy-start.13 = (s32[1,2,512]{2,1,0:T(2,128)S(1)}, s32[1,2,512]{2,1,0:T(2,128)}, u32[]{:S(2)}) copy-start(s32[1,2,512]{2,1,0:T(2,128)} %param.25) | copy-start | bytes 12292
  31.0 8.4 %copy-start.14 = (f32[512]{0:T(512)S(1)}, f32[512]{0:T(512)}, u32[]{:S(2)}) copy-start(f32[512]{0:T(512)} %param.26) | copy-start | bytes 6148
  31.0 8.4 %copy-start.15 = (f32[512]{0:T(512)S(1)}, f32[512]{0:T(512)}, u32[]{:S(2)}) copy-start(f32[512]{0:T(512)} %constant.48.clone) | copy-start | bytes 6148
  31.0 8.4 %copy-start.16 = (f32[512]{0:T(512)S(1)}, f32[512]{0:T(512)}, u32[]{:S(2)}) copy-start(f32[512]{0:T(512)} %constant.49.clone) | copy-start | bytes 6148
  33.2 14.7 %collective-permute-start = (bf16[768,512]{1,0:T(8,128)(2,1)S(1)}, bf16[768,512]{1,0:T(8,128)(2,1)S(1)}, u32[]{:S(2)}, u32[]{:S(2)}) collective-permute-start(bf16[768,512]{1,0:T(8,128)(2,1)S(1)} %bitcast.18), channel_id=1, source_target_pairs={{0,12},{12,0},{1,13},{13,1},{2,14},{14,2},{3,15},{15,3},{4,16},{16... | collective-permute-start | bytes 2359304 | tf_op jit(solution)/shard_map/ppermute | solution.py:235
  50.0 37.5 %copy-start.5 = (f32[512]{0:T(512)S(1)}, f32[512]{0:T(512)}, u32[]{:S(2)}) copy-start(f32[512]{0:T(512)} %param.27) | copy-start | bytes 6148
  50.0 37.5 %copy-start.6 = (f32[512]{0:T(512)S(1)}, f32[512]{0:T(512)}, u32[]{:S(2)}) copy-start(f32[512]{0:T(512)} %param.28) | copy-start | bytes 6148
  50.0 37.5 %copy-start.7 = (f32[512]{0:T(512)S(1)}, f32[512]{0:T(512)}, u32[]{:S(2)}) copy-start(f32[512]{0:T(512)} %param.31) | copy-start | bytes 6148
  50.0 36.7 %all-to-all-start.1 = ((bf16[64,40,128]{2,1,0:T(8,128)(2,1)}), bf16[64,40,128]{2,1,0:T(8,128)(2,1)S(1)}, u32[]{:S(2)}, u32[]{:S(2)}) async-start(bf16[64,40,128]{2,1,0:T(8,128)(2,1)} %bitcast.5), calls=%async_computation.1 | async-start | bytes 1310720 | tf_op jit(solution)/shard_map/all_to_all | solution.py:267
  57.3 13.0 %collective-permute-start.3 = (bf16[3,256,128]{2,1,0:T(8,128)(2,1)S(1)}, bf16[3,256,128]{2,1,0:T(8,128)(2,1)S(1)}, u32[]{:S(2)}, u32[]{:S(2)}) collective-permute-start(bf16[3,256,128]{2,1,0:T(8,128)(2,1)S(1)} %pad_maximum_fusion.1), channel_id=1, source_target_pairs={{0,2},{1,3},{2,0},{3,1},{4,6},{5,7},{6,4},{7,5},{8,10},{9,11},{10,... | collective-permute-start | bytes 589832 | tf_op jit(solution)/shard_map/ppermute | solution.py:266
  70.4 11.3 %collective-permute-start.5 = (bf16[6,256,128]{2,1,0:T(8,128)(2,1)S(1)}, bf16[6,256,128]{2,1,0:T(8,128)(2,1)S(1)}, u32[]{:S(2)}, u32[]{:S(2)}) collective-permute-start(bf16[6,256,128]{2,1,0:T(8,128)(2,1)S(1)} %pad_maximum_fusion.mine_hbm), channel_id=1, source_target_pairs={{0,1},{1,0},{2,3},{3,2},{4,5},{5,4},{6,7},{7,6},{8,9},{9,8},{10,11... | collective-permute-start | bytes 1179656 | tf_op jit(solution)/shard_map/ppermute | solution.py:270
  73.8 12.8 %collective-permute-start.4 = (bf16[6,256,128]{2,1,0:T(8,128)(2,1)S(1)}, bf16[6,256,128]{2,1,0:T(8,128)(2,1)S(1)}, u32[]{:S(2)}, u32[]{:S(2)}) collective-permute-start(bf16[6,256,128]{2,1,0:T(8,128)(2,1)S(1)} %pad_maximum_fusion.mine_hbm), channel_id=1, source_target_pairs={{0,12},{12,0},{1,13},{13,1},{2,14},{14,2},{3,15},{15,3},{4,16},{16... | collective-permute-start | bytes 1179656 | tf_op jit(solution)/shard_map/ppermute | solution.py:271
  81.6 14.8 %collective-permute-start.6 = (bf16[6,256,128]{2,1,0:T(8,128)(2,1)S(1)}, bf16[6,256,128]{2,1,0:T(8,128)(2,1)S(1)}, u32[]{:S(2)}, u32[]{:S(2)}) collective-permute-start(bf16[6,256,128]{2,1,0:T(8,128)(2,1)S(1)} %collective-permute-done.5.mine_hbm), channel_id=1, source_target_pairs={{0,12},{12,0},{1,13},{13,1},{2,14},{14,2},{3,15},{15,3},{4,16},{16... | collective-permute-start | bytes 1179656 | tf_op jit(solution)/shard_map/ppermute | solution.py:272
  86.7 0.8 copy-start.10
  (2 other events, 1.5 us)

commit v5 on v4

--- a/solution.py
+++ b/solution.py
@@ -15,6 +15,7 @@
 NDEV = 64
 PER = 5
 FIRST = 53
+CODES = 16
 SECOND = 53
 AHEAD = 2
 CHUNK = 64
@@ -88,6 +89,40 @@
         out_ref[chip] = block
 
 
+def turn_table():
+    column = np.arange(512)
+    turns = np.power(10000.0, -(2 * (column // 2)) / 512.0) / (2 * math.pi)
+    scale = np.exp2(np.floor(np.log2(turns)) - 10)
+    high = np.floor(turns / scale) * scale
+    return np.stack([high, turns - high, 0.25 * (column % 2)]).astype(np.float32)
+
+
+def codes_kernel(tubes_ref, table_ref, mask_ref, info_ref, offered_ref, base_ref, seat_ref):
+    info = info_ref[...]
+    for clip in range(2):
+        tubes = jnp.broadcast_to(tubes_ref[clip : clip + 1, :].astype(F32), (8, 512)).T[:, :1]
+        count = info[2 + clip : 3 + clip, :1]
+        for low in range(0, 512, 64):
+            tube = tubes[low : low + 64]
+            whole_turns = tube * table_ref[0:1, :]
+            turn = whole_turns - jnp.round(whole_turns) + (tube * table_ref[1:2, :] + table_ref[2:3, :])
+            turn = turn - jnp.round(turn)
+            size = jnp.abs(turn)
+            angle = jnp.minimum(size, 0.5 - size) * (2 * math.pi)
+            square = angle * angle
+            series = 1.0 / 362880 - square * (1.0 / 39916800)
+            for power in (5040, 120, 6, 1):
+                series = 1.0 / power - square * series
+            sine = angle * series
+            code = jnp.where(turn < 0, -sine, sine)
+            hidden = iota((64, 512), 0) + low >= count
+            base_ref[clip, low : low + 64, :] = jnp.where(hidden, mask_ref[...], 0.0) + code
+        rank = iota((VMAX, 1), 0)
+        wanted = ((info[clip : clip + 1, :1] + rank) & 63) * 8 + (rank >> 6)
+        wanted = jnp.where(rank < count, wanted, -1)
+        seat_ref[clip] = jnp.where(offered_ref[...] == wanted, 1.0, 0.0).astype(BF)
+
+
 def fetch_blocks(where_ref, first, mine_hbm, swap_hbm, wproj_hbm, weights_ref, wproj_ref, sems):
     moves = []
 
@@ -147,7 +182,10 @@
     moves = [
         pltpu.make_async_copy(source, into, sems.at[14 + n])
         for n, (source, into) in enumerate(
-            ((recv_hbm, recv_ref), (seat_hbm, seat_ref), (base_hbm, base_ref))
+            (
+                (recv_hbm, recv_ref), (seat_hbm, seat_ref),
+                (base_hbm.at[0], base_ref.at[0]), (base_hbm.at[1], base_ref.at[1]),
+            )
         )
     ]
     blocks = fetch_blocks(where_ref, 4, mine_hbm, swap_hbm, wproj_hbm, weights_ref, wproj_ref, sems)
@@ -160,6 +198,10 @@
         rows_ref[...] = recv_ref[...].astype(F32)
         moves[1].wait()
         moves[2].wait()
+
+    @pl.when(clip == 1)
+    def _():
+        moves[3].wait()
 
     tokens = jnp.concatenate(
         [rows_ref[pl.ds(4 * clip + part, VMAX, stride=8), :] for part in range(4)], axis=1
@@ -273,24 +315,20 @@
     where = jnp.asarray(gather_table())[lax.axis_index("fsdp")]
     where = where + core * jnp.asarray(np.arange(8) == 3, np.int32)
 
-    column = np.arange(512)
-    rate = np.power(10000.0, -(2 * (column // 2)) / 512.0).astype(np.float32)
-    phase = np.where(column % 2 == 0, 0.0, math.pi / 2).astype(np.float32)
-    position = jnp.arange(512, dtype=jnp.int32)
-    visible = position[None, :] < info[2:4, :1]
-    codes = jnp.sin(dec_tubes[0].astype(F32)[..., None] * rate + phase)
-    base = jnp.where(visible[..., None], 0.0, mask_token) + codes
-
     own_mark = own.reshape(32, 24, 512)[:, 22, 0]
     other_mark = other.reshape(32, 24, 512)[:, 22, 0]
     first_mark = jnp.where(core == 0, own_mark, other_mark)
     second_mark = jnp.where(core == 0, other_mark, own_mark)
     marks = jnp.stack([first_mark, second_mark], axis=1).reshape(NDEV).astype(jnp.int32)
     offered = (marks[:, None] * 8 + jnp.arange(PER, dtype=jnp.int32)).reshape(NDEV * PER)
-    rank = position[:VMAX]
-    wanted = ((info[0:2, :1] + rank[None, :]) & 63) * 8 + (rank >> 6)[None, :]
-    wanted = jnp.where(rank[None, :] < info[2:4, :1], wanted, -1)
-    seat = (wanted[:, :, None] == offered[None, None, :]).astype(BF)
+    base, seat = pl.pallas_call(
+        codes_kernel,
+        out_shape=(pltpu.HBM((2, 512, 512), F32), pltpu.HBM((2, VMAX, VMAX), BF)),
+        in_specs=[vmem] * 5,
+        compiler_params=pltpu.CompilerParams(vmem_limit_bytes=CODES * MIB),
+        cost_estimate=pl.CostEstimate(flops=500_000_000, bytes_accessed=3_000_000, transcendentals=0),
+        name="codes",
+    )(dec_tubes[0], jnp.asarray(turn_table()), mask_token[None], info, offered[None])
 
     clip_block = pl.BlockSpec((1, 512, 512), lambda clip: (clip, 0, 0))
     total, dec_normed = pl.pallas_call(
@@ -306,7 +344,7 @@
             pltpu.VMEM((512, 768), BF),
             pltpu.VMEM((256, 512), BF),
             pltpu.VMEM((2560, 128), F32),
-            pltpu.SemaphoreType.DMA((17,)),
+            pltpu.SemaphoreType.DMA((18,)),
         ],
         compiler_params=pltpu.CompilerParams(vmem_limit_bytes=FIRST * MIB),
         cost_estimate=pl.CostEstimate(flops=2_000_000_000, bytes_accessed=8_000_000, transcendentals=2_000_000),

time: 105 us -> 117 us (1.11)
  blocking collectives: 0 us -> 29 us
  other arithmetic: 10.9 us -> 1.26 us
  starting transfers between devices: 53.7 us -> 49.4 us
  waiting for transfers between devices: 13.2 us -> 9.7 us
  Pallas kernels: 21.9 us -> 24.6 us
  local copies, waits for them, and re-layouts: 4.01 us -> 1.88 us
    all_to_all x0 -> x1, blocking collectives: none -> 29 us  [on_device(): gathered = lax.all_to_all(shards, PLANE, 0, 0, tiled=True)]
    all_to_all x1 -> x0, starting transfers between devices: 10.5 us -> none  [on_device(): gathered = lax.all_to_all(shards, PLANE, 0, 0, tiled=True)]
    add x1 -> x0, other arithmetic: 8.46 us -> none  [on_device(): base = jnp.where(visible[..., None], 0.0, mask_token) + codes]
    ppermute x1, waiting for transfers between devices: 4.89 us -> 0.01 us  [on_device(): rest = lax.ppermute(six, 'fsdp', [(z, z ^ 1) for z in range(12)])]
    ppermute x1, starting transfers between devices: 2.67 us -> 7.38 us  [on_device(): six_swap = lax.ppermute(six, 'core', [(0, 1), (1, 0)])]
    ppermute x1, waiting for transfers between devices: 0.01 us -> 4.44 us  [on_device(): below = lax.ppermute(half, 'fsdp', [(z, (z + 8) % 12) for z in range(12)])]
    pallas_call x0 -> x1, Pallas kernels: none -> 3.96 us  [on_device(): pl.pallas_call(codes_kernel, out_shape=(pltpu.HBM((2, 512, 512), F32), pl...]
    ppermute x1, waiting for transfers between devices: 8.28 us -> 5.13 us  [on_device(): twin = lax.ppermute(three, 'fsdp', [(z, z ^ 2) for z in range(12)])]
  transfers between devices with their start and end apart: 9 -> 8, of which waited for: 2 -> 3; matrix products, arithmetic and copies ran while one was open for 11% -> 1% of each run, Pallas kernels for 12% -> 12%
where the time goes in v5:
time: 117 us; the launch traced here: 116 us
  starting transfers between devices  49.4 us (42%)
  blocking collectives  29 us (25%)
  Pallas kernels  24.6 us (21%)
  waiting for transfers between devices  9.7 us (8%)
  local copies, waits for them, and re-layouts  1.88 us (2%)
  other arithmetic  1.26 us (1%)
    all_to_all x1, blocking collectives, on_device(): gathered = lax.all_to_all(shards, PLANE, 0, 0, tiled=True)  29 us
    ppermute x1, starting transfers between devices, on_device(): above = lax.ppermute(half, 'fsdp', [(z, (z + 4) % 12) for z in range(12)])  10.6 us
    pallas_call x1, Pallas kernels, on_device(): pl.pallas_call(first_kernel, grid=(2,), out_shape=(jax.ShapeDtypeStruct((...  8.53 us
    pallas_call x1, Pallas kernels, on_device(): pl.pallas_call(second_kernel, grid=(2,), out_shape=jax.ShapeDtypeStruct((...  7.43 us
    ppermute x1, starting transfers between devices, on_device(): six_swap = lax.ppermute(six, 'core', [(0, 1), (1, 0)])  7.38 us
    ppermute x1, starting transfers between devices, on_device(): other = lax.ppermute(own, 'core', [(0, 1), (1, 0)])  7.34 us
    ppermute x1, starting transfers between devices, on_device(): rest_swap = lax.ppermute(rest, 'core', [(0, 1), (1, 0)])  5.69 us
    ppermute x1, starting transfers between devices, on_device(): below = lax.ppermute(half, 'fsdp', [(z, (z + 8) % 12) for z in range(12)])  5.56 us
  transfers between devices with their start and end apart: 8, of which 3 were waited for; matrix products, arithmetic and copies ran while one was open for 1% of the time, Pallas kernels for 12%

profile of v5, /device:TPU:1, one launch (start us, length us, event | category | flops | bytes accessed | tf_op | source)
XLA Modules:
  0.0 116.3 jit_solution(5810488964062734031)
XLA Ops:
  0.0 0.8 copy-done.1
  0.8 0.7 copy-done.2
  1.5 0.6 shards.1
  2.1 29.0 %all_to_all.10 = bf16[32,24,512]{2,1,0:T(8,128)(2,1)S(1)} all-to-all(bf16[32,24,512]{2,1,0:T(8,128)(2,1)S(1)} %shards.1), channel_id=1, replica_groups=mesh['y'=8,'x'=4,'core'=2,'fsdp'=12] {'y','x'}, dimensions={0} | all-to-all | bytes 1572864 | tf_op jit(solution)/shard_map/all_to_all | solution.py:275
  31.1 7.3 %collective-permute-start = (bf16[768,512]{1,0:T(8,128)(2,1)S(1)}, bf16[768,512]{1,0:T(8,128)(2,1)S(1)}, u32[]{:S(2)}, u32[]{:S(2)}) collective-permute-start(bf16[768,512]{1,0:T(8,128)(2,1)S(1)} %bitcast.18), channel_id=1, source_target_pairs={{0,12},{12,0},{1,13},{13,1},{2,14},{14,2},{3,15},{15,3},{4,16},{16... | collective-permute-start | bytes 2359304 | tf_op jit(solution)/shard_map/ppermute | solution.py:277
  38.6 2.0 %prep.1 = (bf16[2,320,768]{2,1,0:T(8,128)(2,1)S(1)}, bf16[640,320]{1,0:T(8,128)(2,1)S(1)}, s32[8,128]{1,0:T(8,128)S(1)}) custom-call(s32[2]{0:T(128)S(1)} %pad_add_fusion.ids_ref, s32[1,320]{1,0:T(1,128)S(1)} %copy-done.3, bf16[320,1408]{1,0:T(8,128)(2,1)S(1)} %bitcast.21, f32[1,1408]{1,0:T(1,128)S(1)} %broadcast_in_dim.23.gain_ref, ...), custom_call_target="tpu_custom_call" | custom-call | flops 4000000000 | bytes 4000000 | tf_op jit(solution)/shard_map/prep/pallas_call | solution.py:284
  40.6 2.0 %embed.1 = bf16[2560,128]{1,0:T(8,128)(2,1)} custom-call(bf16[2,320,768]{2,1,0:T(8,128)(2,1)S(1)} %get-tuple-element.14.normed_ref, bf16[768,512]{1,0:T(8,128)(2,1)S(1)} %bitcast.19, bf16[768,512]{1,0:T(8,128)(2,1)S(1)} %collective-permute-done.other_ref, bf16[640,320]{1,0:T(8,128)(2,1)S(1)} %get-tuple-element.15.pick_ref), custom_call_target="tpu_custom_call" | custom-call | flops 1000000000 | bytes 4000000 | tf_op jit(solution)/shard_map/embed/pallas_call | solution.py:297
  42.7 5.4 %all-to-all-start.1 = ((bf16[64,40,128]{2,1,0:T(8,128)(2,1)}), bf16[64,40,128]{2,1,0:T(8,128)(2,1)}, u32[]{:S(2)}, u32[]{:S(2)}) async-start(bf16[64,40,128]{2,1,0:T(8,128)(2,1)} %bitcast.5), calls=%async_computation.1 | async-start | bytes 1310720 | tf_op jit(solution)/shard_map/all_to_all | solution.py:309
  48.2 10.6 %collective-permute-start.1 = (bf16[1,256,128]{2,1,0:T(8,128)(2,1)S(1)}, bf16[1,256,128]{2,1,0:T(8,128)(2,1)S(1)}, u32[]{:S(2)}, u32[]{:S(2)}) collective-permute-start(bf16[1,256,128]{2,1,0:T(8,128)(2,1)S(1)} %dynamic-slice_bitcast_fusion), channel_id=1, source_target_pairs={{0,4},{1,5},{2,6},{3,7},{4,8},{5,9},{6,10},{7,11},{8,0},{9,1},{10,... | collective-permute-start | bytes 196616 | tf_op jit(solution)/shard_map/ppermute | solution.py:280
  58.8 5.6 %collective-permute-start.2 = (bf16[1,256,128]{2,1,0:T(8,128)(2,1)S(1)}, bf16[1,256,128]{2,1,0:T(8,128)(2,1)S(1)}, u32[]{:S(2)}, u32[]{:S(2)}) collective-permute-start(bf16[1,256,128]{2,1,0:T(8,128)(2,1)S(1)} %dynamic-slice_bitcast_fusion), channel_id=1, source_target_pairs={{0,8},{1,9},{2,10},{3,11},{4,0},{5,1},{6,2},{7,3},{8,4},{9,5},{10,... | collective-permute-start | bytes 196616 | tf_op jit(solution)/shard_map/ppermute | solution.py:281
  64.4 0.1 collective-permute-done.1
  64.5 4.4 %collective-permute-done.2 = bf16[1,256,128]{2,1,0:T(8,128)(2,1)S(1)} collective-permute-done((bf16[1,256,128]{2,1,0:T(8,128)(2,1)S(1)}, bf16[1,256,128]{2,1,0:T(8,128)(2,1)S(1)}, u32[]{:S(2)}, u32[]{:S(2)}) %collective-permute-start.2) | collective-permute-done | bytes 65568 | tf_op jit(solution)/shard_map/ppermute | solution.py:281
  69.0 4.8 %collective-permute-start.3 = (bf16[3,256,128]{2,1,0:T(8,128)(2,1)S(1)}, bf16[3,256,128]{2,1,0:T(8,128)(2,1)S(1)}, u32[]{:S(2)}, u32[]{:S(2)}) collective-permute-start(bf16[3,256,128]{2,1,0:T(8,128)(2,1)S(1)} %pad_maximum_fusion.1), channel_id=1, source_target_pairs={{0,2},{1,3},{2,0},{3,1},{4,6},{5,7},{6,4},{7,5},{8,10},{9,11},{10,... | collective-permute-start | bytes 589832 | tf_op jit(solution)/shard_map/ppermute | solution.py:308
  73.8 5.1 %collective-permute-done.3 = bf16[3,256,128]{2,1,0:T(8,128)(2,1)S(1)} collective-permute-done((bf16[3,256,128]{2,1,0:T(8,128)(2,1)S(1)}, bf16[3,256,128]{2,1,0:T(8,128)(2,1)S(1)}, u32[]{:S(2)}, u32[]{:S(2)}) %collective-permute-start.3) | collective-permute-done | bytes 196640 | tf_op jit(solution)/shard_map/ppermute | solution.py:308
  78.9 2.6 %collective-permute-start.5 = (bf16[6,256,128]{2,1,0:T(8,128)(2,1)S(1)}, bf16[6,256,128]{2,1,0:T(8,128)(2,1)S(1)}, u32[]{:S(2)}, u32[]{:S(2)}) collective-permute-start(bf16[6,256,128]{2,1,0:T(8,128)(2,1)S(1)} %pad_maximum_fusion.mine_hbm), channel_id=1, source_target_pairs={{0,1},{1,0},{2,3},{3,2},{4,5},{5,4},{6,7},{7,6},{8,9},{9,8},{10,11... | collective-permute-start | bytes 1179656 | tf_op jit(solution)/shard_map/ppermute | solution.py:312
  81.6 0.7 bitcast_add_fusion.where_ref
  82.3 7.4 %collective-permute-start.4 = (bf16[6,256,128]{2,1,0:T(8,128)(2,1)S(1)}, bf16[6,256,128]{2,1,0:T(8,128)(2,1)S(1)}, u32[]{:S(2)}, u32[]{:S(2)}) collective-permute-start(bf16[6,256,128]{2,1,0:T(8,128)(2,1)S(1)} %pad_maximum_fusion.mine_hbm), channel_id=1, source_target_pairs={{0,12},{12,0},{1,13},{13,1},{2,14},{14,2},{3,15},{15,3},{4,16},{16... | collective-permute-start | bytes 1179656 | tf_op jit(solution)/shard_map/ppermute | solution.py:313
  89.7 0.3 fusion
  90.1 0.1 mul.35
  90.2 5.7 %collective-permute-start.6 = (bf16[6,256,128]{2,1,0:T(8,128)(2,1)S(1)}, bf16[6,256,128]{2,1,0:T(8,128)(2,1)S(1)}, u32[]{:S(2)}, u32[]{:S(2)}) collective-permute-start(bf16[6,256,128]{2,1,0:T(8,128)(2,1)S(1)} %collective-permute-done.5.mine_hbm), channel_id=1, source_target_pairs={{0,12},{12,0},{1,13},{13,1},{2,14},{14,2},{3,15},{15,3},{4,16},{16... | collective-permute-start | bytes 1179656 | tf_op jit(solution)/shard_map/ppermute | solution.py:314
  96.0 0.1 add.45.offered_ref
  96.2 4.0 %codes.1 = (f32[2,512,512]{2,1,0:T(8,128)}, bf16[2,320,320]{2,1,0:T(8,128)(2,1)}) custom-call(s32[2,512]{1,0:T(2,128)S(1)} %bitcast.22, f32[3,512]{1,0:T(4,128)S(1)} %copy-done.12, f32[1,512]{1,0:T(1,128)S(1)} %bitcast.23, s32[8,128]{1,0:T(8,128)S(1)} %get-tuple-element.16.info_ref, s32[1,320]{1,0:T(1,128)S(1)} %add.45.offered_ref), custom_call_target="tpu_custom_call" | custom-call | flops 500000000 | bytes 3000000 | tf_op jit(solution)/shard_map/codes/pallas_call | solution.py:324
  100.2 8.5 %heads1.1 = (f32[2,512,512]{2,1,0:T(8,128)}, bf16[2,512,512]{2,1,0:T(8,128)(2,1)}) custom-call(s32[8]{0:T(128)S(1)} %bitcast_add_fusion.where_ref, bf16[2560,128]{1,0:T(8,128)(2,1)} %bitcast.6.recv_hbm, bf16[2,320,320]{2,1,0:T(8,128)(2,1)} %get-tuple-element.17.seat_hbm, f32[2,512,512]{2,1,0:T(8,128)} %get-tuple-element.18.base_hbm, ...), custom_call_target="tpu_custom_call" | custom-call | flops 2000000000 | bytes 8000000 | tf_op jit(solution)/shard_map/heads1/pallas_call | solution.py:334
  108.7 7.4 %heads2.1 = bf16[1,2,512,512]{3,2,1,0:T(8,128)(2,1)} custom-call(s32[8]{0:T(128)S(1)} %bitcast_add_fusion.where_ref, f32[2,512,512]{2,1,0:T(8,128)} %get-tuple-element.21.total_ref, bf16[2,512,512]{2,1,0:T(8,128)(2,1)} %get-tuple-element.22.normed_ref, bf16[6,256,128]{2,1,0:T(8,128)(2,1)S(1)} %collective-permute-done.5.mine_hbm, ...), custom_call_target="tpu_custom_call" | custom-call | flops 2000000000 | bytes 8000000 | tf_op jit(solution)/shard_map/heads2/pallas_call | solution.py:353
  (44 shorter events, 0.4 us)
Async XLA Ops:
  0.0 48.1 %copy-start = (bf16[512,128]{1,0:T(8,128)(2,1)S(1)}, bf16[512,128]{1,0:T(8,128)(2,1)}, u32[]{:S(2)}) copy-start(bf16[512,128]{1,0:T(8,128)(2,1)} %param.28) | copy-start | bytes 393220
  0.0 0.8 copy-start.1
  0.8 0.7 copy-start.2
  1.5 37.0 %copy-start.13 = (f32[1408]{0:T(1024)S(1)}, f32[1408]{0:T(1024)}, u32[]{:S(2)}) copy-start(f32[1408]{0:T(1024)} %param.18) | copy-start | bytes 16900
  1.5 37.0 %copy-start.14 = (f32[1408]{0:T(1024)S(1)}, f32[1408]{0:T(1024)}, u32[]{:S(2)}) copy-start(f32[1408]{0:T(1024)} %param.19) | copy-start | bytes 16900
  1.5 37.1 %copy-start.3 = (s32[1,320]{1,0:T(1,128)S(1)}, s32[1,320]{1,0:T(1,128)}, u32[]{:S(2)}) copy-start(s32[1,320]{1,0:T(1,128)} %ids_ref.1) | copy-start | bytes 3844
  1.5 37.1 %copy-start.4 = (bf16[1,320,1408]{2,1,0:T(8,128)(2,1)S(1)}, bf16[1,320,1408]{2,1,0:T(8,128)(2,1)}, u32[]{:S(2)}) copy-start(bf16[1,320,1408]{2,1,0:T(8,128)(2,1)} %param.17) | copy-start | bytes 2703364
  1.5 37.1 %copy-start.10 = (s32[1,128]{1,0:T(1,128)S(1)}, s32[1,128]{1,0:T(1,128)}, u32[]{:S(2)}) copy-start(s32[1,128]{1,0:T(1,128)} %counts_ref.1) | copy-start | bytes 1540
  1.5 37.1 %copy-start.11 = (s32[1,128]{1,0:T(1,128)S(1)}, s32[1,128]{1,0:T(1,128)}, u32[]{:S(2)}) copy-start(s32[1,128]{1,0:T(1,128)} %owner_ref.1) | copy-start | bytes 1540
  31.1 9.5 %collective-permute-start = (bf16[768,512]{1,0:T(8,128)(2,1)S(1)}, bf16[768,512]{1,0:T(8,128)(2,1)S(1)}, u32[]{:S(2)}, u32[]{:S(2)}) collective-permute-start(bf16[768,512]{1,0:T(8,128)(2,1)S(1)} %bitcast.18), channel_id=1, source_target_pairs={{0,12},{12,0},{1,13},{13,1},{2,14},{14,2},{3,15},{15,3},{4,16},{16... | collective-permute-start | bytes 2359304 | tf_op jit(solution)/shard_map/ppermute | solution.py:277
  42.7 38.9 %copy-start.15 = (s32[8]{0:T(128)S(1)}, s32[8]{0:T(128)}, u32[]{:S(2)}) copy-start(s32[8]{0:T(128)} %constant.36.clone) | copy-start | bytes 100
  42.7 53.5 %copy-start.5 = (s32[1,2,512]{2,1,0:T(2,128)S(1)}, s32[1,2,512]{2,1,0:T(2,128)}, u32[]{:S(2)}) copy-start(s32[1,2,512]{2,1,0:T(2,128)} %param.24) | copy-start | bytes 12292
  42.7 53.5 %copy-start.6 = (f32[512]{0:T(512)S(1)}, f32[512]{0:T(512)}, u32[]{:S(2)}) copy-start(f32[512]{0:T(512)} %param.25) | copy-start | bytes 6148
  42.7 53.5 %copy-start.12 = (f32[3,512]{1,0:T(4,128)S(1)}, f32[3,512]{1,0:T(4,128)}, u32[]{:S(2)}) copy-start(f32[3,512]{1,0:T(4,128)} %constant.37.clone.table_ref) | copy-start | bytes 18436
  42.7 57.5 %copy-start.7 = (f32[512]{0:T(512)S(1)}, f32[512]{0:T(512)}, u32[]{:S(2)}) copy-start(f32[512]{0:T(512)} %param.26) | copy-start | bytes 6148
  42.7 57.5 %copy-start.8 = (f32[512]{0:T(512)S(1)}, f32[512]{0:T(512)}, u32[]{:S(2)}) copy-start(f32[512]{0:T(512)} %param.27) | copy-start | bytes 6148
  42.7 57.5 %copy-start.9 = (f32[512]{0:T(512)S(1)}, f32[512]{0:T(512)}, u32[]{:S(2)}) copy-start(f32[512]{0:T(512)} %param.30) | copy-start | bytes 6148
  42.7 57.4 %all-to-all-start.1 = ((bf16[64,40,128]{2,1,0:T(8,128)(2,1)}), bf16[64,40,128]{2,1,0:T(8,128)(2,1)}, u32[]{:S(2)}, u32[]{:S(2)}) async-start(bf16[64,40,128]{2,1,0:T(8,128)(2,1)} %bitcast.5), calls=%async_computation.1 | async-start | bytes 1310720 | tf_op jit(solution)/shard_map/all_to_all | solution.py:309
  48.2 16.3 %collective-permute-start.1 = (bf16[1,256,128]{2,1,0:T(8,128)(2,1)S(1)}, bf16[1,256,128]{2,1,0:T(8,128)(2,1)S(1)}, u32[]{:S(2)}, u32[]{:S(2)}) collective-permute-start(bf16[1,256,128]{2,1,0:T(8,128)(2,1)S(1)} %dynamic-slice_bitcast_fusion), channel_id=1, source_target_pairs={{0,4},{1,5},{2,6},{3,7},{4,8},{5,9},{6,10},{7,11},{8,0},{9,1},{10,... | collective-permute-start | bytes 196616 | tf_op jit(solution)/shard_map/ppermute | solution.py:280
  58.8 10.1 %collective-permute-start.2 = (bf16[1,256,128]{2,1,0:T(8,128)(2,1)S(1)}, bf16[1,256,128]{2,1,0:T(8,128)(2,1)S(1)}, u32[]{:S(2)}, u32[]{:S(2)}) collective-permute-start(bf16[1,256,128]{2,1,0:T(8,128)(2,1)S(1)} %dynamic-slice_bitcast_fusion), channel_id=1, source_target_pairs={{0,8},{1,9},{2,10},{3,11},{4,0},{5,1},{6,2},{7,3},{8,4},{9,5},{10,... | collective-permute-start | bytes 196616 | tf_op jit(solution)/shard_map/ppermute | solution.py:281
  69.0 9.9 %collective-permute-start.3 = (bf16[3,256,128]{2,1,0:T(8,128)(2,1)S(1)}, bf16[3,256,128]{2,1,0:T(8,128)(2,1)S(1)}, u32[]{:S(2)}, u32[]{:S(2)}) collective-permute-start(bf16[3,256,128]{2,1,0:T(8,128)(2,1)S(1)} %pad_maximum_fusion.1), channel_id=1, source_target_pairs={{0,2},{1,3},{2,0},{3,1},{4,6},{5,7},{6,4},{7,5},{8,10},{9,11},{10,... | collective-permute-start | bytes 589832 | tf_op jit(solution)/shard_map/ppermute | solution.py:308
  78.9 11.3 %collective-permute-start.5 = (bf16[6,256,128]{2,1,0:T(8,128)(2,1)S(1)}, bf16[6,256,128]{2,1,0:T(8,128)(2,1)S(1)}, u32[]{:S(2)}, u32[]{:S(2)}) collective-permute-start(bf16[6,256,128]{2,1,0:T(8,128)(2,1)S(1)} %pad_maximum_fusion.mine_hbm), channel_id=1, source_target_pairs={{0,1},{1,0},{2,3},{3,2},{4,5},{5,4},{6,7},{7,6},{8,9},{9,8},{10,11... | collective-permute-start | bytes 1179656 | tf_op jit(solution)/shard_map/ppermute | solution.py:312
  82.3 17.8 %collective-permute-start.4 = (bf16[6,256,128]{2,1,0:T(8,128)(2,1)S(1)}, bf16[6,256,128]{2,1,0:T(8,128)(2,1)S(1)}, u32[]{:S(2)}, u32[]{:S(2)}) collective-permute-start(bf16[6,256,128]{2,1,0:T(8,128)(2,1)S(1)} %pad_maximum_fusion.mine_hbm), channel_id=1, source_target_pairs={{0,12},{12,0},{1,13},{13,1},{2,14},{14,2},{3,15},{15,3},{4,16},{16... | collective-permute-start | bytes 1179656 | tf_op jit(solution)/shard_map/ppermute | solution.py:313
  90.2 18.5 %collective-permute-start.6 = (bf16[6,256,128]{2,1,0:T(8,128)(2,1)S(1)}, bf16[6,256,128]{2,1,0:T(8,128)(2,1)S(1)}, u32[]{:S(2)}, u32[]{:S(2)}) collective-permute-start(bf16[6,256,128]{2,1,0:T(8,128)(2,1)S(1)} %collective-permute-done.5.mine_hbm), channel_id=1, source_target_pairs={{0,12},{12,0},{1,13},{13,1},{2,14},{14,2},{3,15},{15,3},{4,16},{16... | collective-permute-start | bytes 1179656 | tf_op jit(solution)/shard_map/ppermute | solution.py:314

commit v6 on v5

--- a/solution.py
+++ b/solution.py
@@ -78,7 +78,7 @@
     packed = jnp.dot(pick_ref[...], embedded, preferred_element_type=F32)
     for part in range(4):
         rows_ref[pl.ds(part, 640, stride=4), :] = packed[:, 128 * part : 128 * (part + 1)]
-    out_ref[...] = rows_ref[...].astype(BF)
+    out_ref[...] = rows_ref[:2560, :].astype(BF)
 
 
 def shard_kernel(ids_ref, rows_ref, out_ref):
@@ -195,7 +195,7 @@
         for move in moves + blocks:
             move.start()
         moves[0].wait()
-        rows_ref[...] = recv_ref[...].astype(F32)
+        rows_ref[:2560, :] = recv_ref[...].astype(F32)
         moves[1].wait()
         moves[2].wait()
 
@@ -297,7 +297,7 @@
     sent = pl.pallas_call(
         embed_kernel,
         out_shape=jax.ShapeDtypeStruct((2560, 128), BF),
-        scratch_shapes=[pltpu.VMEM((2560, 128), F32)],
+        scratch_shapes=[pltpu.VMEM((2624, 128), F32)],
         compiler_params=pltpu.CompilerParams(vmem_limit_bytes=24 * MIB),
         cost_estimate=pl.CostEstimate(flops=1_000_000_000, bytes_accessed=4_000_000, transcendentals=0),
         name="embed",
@@ -343,7 +343,7 @@
             pltpu.VMEM((2, 512, 512), F32),
             pltpu.VMEM((512, 768), BF),
             pltpu.VMEM((256, 512), BF),
-            pltpu.VMEM((2560, 128), F32),
+            pltpu.VMEM((2624, 128), F32),
             pltpu.SemaphoreType.DMA((18,)),
         ],
         compiler_params=pltpu.CompilerParams(vmem_limit_bytes=FIRST * MIB),

time: 117 us -> 117 us (level)
  no operation moved by 1% of the time
where the time goes in v6:
time: 117 us; the launch traced here: 116 us
  starting transfers between devices  49.4 us (42%)
  blocking collectives  29 us (25%)
  Pallas kernels  24.6 us (21%)
  waiting for transfers between devices  9.7 us (8%)
  local copies, waits for them, and re-layouts  1.88 us (2%)
  other arithmetic  1.26 us (1%)
    all_to_all x1, blocking collectives, on_device(): gathered = lax.all_to_all(shards, PLANE, 0, 0, tiled=True)  29 us
    ppermute x1, starting transfers between devices, on_device(): above = lax.ppermute(half, 'fsdp', [(z, (z + 4) % 12) for z in range(12)])  10.6 us
    pallas_call x1, Pallas kernels, on_device(): pl.pallas_call(first_kernel, grid=(2,), out_shape=(jax.ShapeDtypeStruct((...  8.53 us
    pallas_call x1, Pallas kernels, on_device(): pl.pallas_call(second_kernel, grid=(2,), out_shape=jax.ShapeDtypeStruct((...  7.43 us
    ppermute x1, starting transfers between devices, on_device(): six_swap = lax.ppermute(six, 'core', [(0, 1), (1, 0)])  7.38 us
    ppermute x1, starting transfers between devices, on_device(): other = lax.ppermute(own, 'core', [(0, 1), (1, 0)])  7.34 us
    ppermute x1, starting transfers between devices, on_device(): rest_swap = lax.ppermute(rest, 'core', [(0, 1), (1, 0)])  5.69 us
    ppermute x1, starting transfers between devices, on_device(): below = lax.ppermute(half, 'fsdp', [(z, (z + 8) % 12) for z in range(12)])  5.56 us
  transfers between devices with their start and end apart: 8, of which 3 were waited for; matrix products, arithmetic and copies ran while one was open for 1% of the time, Pallas kernels for 12%

profile of v6, /device:TPU:1, one launch (start us, length us, event | category | flops | bytes accessed | tf_op | source)
XLA Modules:
  0.0 116.3 jit_solution(10091901458053325699)
XLA Ops:
  0.0 0.8 copy-done.1
  0.8 0.7 copy-done.2
  1.5 0.6 shards.1
  2.1 29.0 %all_to_all.10 = bf16[32,24,512]{2,1,0:T(8,128)(2,1)S(1)} all-to-all(bf16[32,24,512]{2,1,0:T(8,128)(2,1)S(1)} %shards.1), channel_id=1, replica_groups=mesh['y'=8,'x'=4,'core'=2,'fsdp'=12] {'y','x'}, dimensions={0} | all-to-all | bytes 1572864 | tf_op jit(solution)/shard_map/all_to_all | solution.py:275
  31.1 7.3 %collective-permute-start = (bf16[768,512]{1,0:T(8,128)(2,1)S(1)}, bf16[768,512]{1,0:T(8,128)(2,1)S(1)}, u32[]{:S(2)}, u32[]{:S(2)}) collective-permute-start(bf16[768,512]{1,0:T(8,128)(2,1)S(1)} %bitcast.18), channel_id=1, source_target_pairs={{0,12},{12,0},{1,13},{13,1},{2,14},{14,2},{3,15},{15,3},{4,16},{16... | collective-permute-start | bytes 2359304 | tf_op jit(solution)/shard_map/ppermute | solution.py:277
  38.6 2.0 %prep.1 = (bf16[2,320,768]{2,1,0:T(8,128)(2,1)S(1)}, bf16[640,320]{1,0:T(8,128)(2,1)S(1)}, s32[8,128]{1,0:T(8,128)S(1)}) custom-call(s32[2]{0:T(128)S(1)} %pad_add_fusion.ids_ref, s32[1,320]{1,0:T(1,128)S(1)} %copy-done.3, bf16[320,1408]{1,0:T(8,128)(2,1)S(1)} %bitcast.21, f32[1,1408]{1,0:T(1,128)S(1)} %broadcast_in_dim.23.gain_ref, ...), custom_call_target="tpu_custom_call" | custom-call | flops 4000000000 | bytes 4000000 | tf_op jit(solution)/shard_map/prep/pallas_call | solution.py:284
  40.6 2.0 %embed.1 = bf16[2560,128]{1,0:T(8,128)(2,1)} custom-call(bf16[2,320,768]{2,1,0:T(8,128)(2,1)S(1)} %get-tuple-element.14.normed_ref, bf16[768,512]{1,0:T(8,128)(2,1)S(1)} %bitcast.19, bf16[768,512]{1,0:T(8,128)(2,1)S(1)} %collective-permute-done.other_ref, bf16[640,320]{1,0:T(8,128)(2,1)S(1)} %get-tuple-element.15.pick_ref), custom_call_target="tpu_custom_call" | custom-call | flops 1000000000 | bytes 4000000 | tf_op jit(solution)/shard_map/embed/pallas_call | solution.py:297
  42.7 5.4 %all-to-all-start.1 = ((bf16[64,40,128]{2,1,0:T(8,128)(2,1)}), bf16[64,40,128]{2,1,0:T(8,128)(2,1)}, u32[]{:S(2)}, u32[]{:S(2)}) async-start(bf16[64,40,128]{2,1,0:T(8,128)(2,1)} %bitcast.5), calls=%async_computation.1 | async-start | bytes 1310720 | tf_op jit(solution)/shard_map/all_to_all | solution.py:309
  48.2 10.6 %collective-permute-start.1 = (bf16[1,256,128]{2,1,0:T(8,128)(2,1)S(1)}, bf16[1,256,128]{2,1,0:T(8,128)(2,1)S(1)}, u32[]{:S(2)}, u32[]{:S(2)}) collective-permute-start(bf16[1,256,128]{2,1,0:T(8,128)(2,1)S(1)} %dynamic-slice_bitcast_fusion), channel_id=1, source_target_pairs={{0,4},{1,5},{2,6},{3,7},{4,8},{5,9},{6,10},{7,11},{8,0},{9,1},{10,... | collective-permute-start | bytes 196616 | tf_op jit(solution)/shard_map/ppermute | solution.py:280
  58.8 5.6 %collective-permute-start.2 = (bf16[1,256,128]{2,1,0:T(8,128)(2,1)S(1)}, bf16[1,256,128]{2,1,0:T(8,128)(2,1)S(1)}, u32[]{:S(2)}, u32[]{:S(2)}) collective-permute-start(bf16[1,256,128]{2,1,0:T(8,128)(2,1)S(1)} %dynamic-slice_bitcast_fusion), channel_id=1, source_target_pairs={{0,8},{1,9},{2,10},{3,11},{4,0},{5,1},{6,2},{7,3},{8,4},{9,5},{10,... | collective-permute-start | bytes 196616 | tf_op jit(solution)/shard_map/ppermute | solution.py:281
  64.4 0.1 collective-permute-done.1
  64.5 4.4 %collective-permute-done.2 = bf16[1,256,128]{2,1,0:T(8,128)(2,1)S(1)} collective-permute-done((bf16[1,256,128]{2,1,0:T(8,128)(2,1)S(1)}, bf16[1,256,128]{2,1,0:T(8,128)(2,1)S(1)}, u32[]{:S(2)}, u32[]{:S(2)}) %collective-permute-start.2) | collective-permute-done | bytes 65568 | tf_op jit(solution)/shard_map/ppermute | solution.py:281
  69.0 4.8 %collective-permute-start.3 = (bf16[3,256,128]{2,1,0:T(8,128)(2,1)S(1)}, bf16[3,256,128]{2,1,0:T(8,128)(2,1)S(1)}, u32[]{:S(2)}, u32[]{:S(2)}) collective-permute-start(bf16[3,256,128]{2,1,0:T(8,128)(2,1)S(1)} %pad_maximum_fusion.1), channel_id=1, source_target_pairs={{0,2},{1,3},{2,0},{3,1},{4,6},{5,7},{6,4},{7,5},{8,10},{9,11},{10,... | collective-permute-start | bytes 589832 | tf_op jit(solution)/shard_map/ppermute | solution.py:308
  73.8 5.1 %collective-permute-done.3 = bf16[3,256,128]{2,1,0:T(8,128)(2,1)S(1)} collective-permute-done((bf16[3,256,128]{2,1,0:T(8,128)(2,1)S(1)}, bf16[3,256,128]{2,1,0:T(8,128)(2,1)S(1)}, u32[]{:S(2)}, u32[]{:S(2)}) %collective-permute-start.3) | collective-permute-done | bytes 196640 | tf_op jit(solution)/shard_map/ppermute | solution.py:308
  78.9 2.6 %collective-permute-start.5 = (bf16[6,256,128]{2,1,0:T(8,128)(2,1)S(1)}, bf16[6,256,128]{2,1,0:T(8,128)(2,1)S(1)}, u32[]{:S(2)}, u32[]{:S(2)}) collective-permute-start(bf16[6,256,128]{2,1,0:T(8,128)(2,1)S(1)} %pad_maximum_fusion.mine_hbm), channel_id=1, source_target_pairs={{0,1},{1,0},{2,3},{3,2},{4,5},{5,4},{6,7},{7,6},{8,9},{9,8},{10,11... | collective-permute-start | bytes 1179656 | tf_op jit(solution)/shard_map/ppermute | solution.py:312
  81.6 0.7 bitcast_add_fusion.where_ref
  82.3 7.4 %collective-permute-start.4 = (bf16[6,256,128]{2,1,0:T(8,128)(2,1)S(1)}, bf16[6,256,128]{2,1,0:T(8,128)(2,1)S(1)}, u32[]{:S(2)}, u32[]{:S(2)}) collective-permute-start(bf16[6,256,128]{2,1,0:T(8,128)(2,1)S(1)} %pad_maximum_fusion.mine_hbm), channel_id=1, source_target_pairs={{0,12},{12,0},{1,13},{13,1},{2,14},{14,2},{3,15},{15,3},{4,16},{16... | collective-permute-start | bytes 1179656 | tf_op jit(solution)/shard_map/ppermute | solution.py:313
  89.7 0.3 fusion
  90.1 0.1 mul.35
  90.2 5.7 %collective-permute-start.6 = (bf16[6,256,128]{2,1,0:T(8,128)(2,1)S(1)}, bf16[6,256,128]{2,1,0:T(8,128)(2,1)S(1)}, u32[]{:S(2)}, u32[]{:S(2)}) collective-permute-start(bf16[6,256,128]{2,1,0:T(8,128)(2,1)S(1)} %collective-permute-done.5.mine_hbm), channel_id=1, source_target_pairs={{0,12},{12,0},{1,13},{13,1},{2,14},{14,2},{3,15},{15,3},{4,16},{16... | collective-permute-start | bytes 1179656 | tf_op jit(solution)/shard_map/ppermute | solution.py:314
  96.0 0.1 add.45.offered_ref
  96.2 4.0 %codes.1 = (f32[2,512,512]{2,1,0:T(8,128)}, bf16[2,320,320]{2,1,0:T(8,128)(2,1)}) custom-call(s32[2,512]{1,0:T(2,128)S(1)} %bitcast.22, f32[3,512]{1,0:T(4,128)S(1)} %copy-done.12, f32[1,512]{1,0:T(1,128)S(1)} %bitcast.23, s32[8,128]{1,0:T(8,128)S(1)} %get-tuple-element.16.info_ref, s32[1,320]{1,0:T(1,128)S(1)} %add.45.offered_ref), custom_call_target="tpu_custom_call" | custom-call | flops 500000000 | bytes 3000000 | tf_op jit(solution)/shard_map/codes/pallas_call | solution.py:324
  100.2 8.5 %heads1.1 = (f32[2,512,512]{2,1,0:T(8,128)}, bf16[2,512,512]{2,1,0:T(8,128)(2,1)}) custom-call(s32[8]{0:T(128)S(1)} %bitcast_add_fusion.where_ref, bf16[2560,128]{1,0:T(8,128)(2,1)} %bitcast.6.recv_hbm, bf16[2,320,320]{2,1,0:T(8,128)(2,1)} %get-tuple-element.17.seat_hbm, f32[2,512,512]{2,1,0:T(8,128)} %get-tuple-element.18.base_hbm, ...), custom_call_target="tpu_custom_call" | custom-call | flops 2000000000 | bytes 8000000 | tf_op jit(solution)/shard_map/heads1/pallas_call | solution.py:334
  108.7 7.4 %heads2.1 = bf16[1,2,512,512]{3,2,1,0:T(8,128)(2,1)} custom-call(s32[8]{0:T(128)S(1)} %bitcast_add_fusion.where_ref, f32[2,512,512]{2,1,0:T(8,128)} %get-tuple-element.21.total_ref, bf16[2,512,512]{2,1,0:T(8,128)(2,1)} %get-tuple-element.22.normed_ref, bf16[6,256,128]{2,1,0:T(8,128)(2,1)S(1)} %collective-permute-done.5.mine_hbm, ...), custom_call_target="tpu_custom_call" | custom-call | flops 2000000000 | bytes 8000000 | tf_op jit(solution)/shard_map/heads2/pallas_call | solution.py:353
  (44 shorter events, 0.4 us)
Async XLA Ops:
  0.0 48.1 %copy-start = (bf16[512,128]{1,0:T(8,128)(2,1)S(1)}, bf16[512,128]{1,0:T(8,128)(2,1)}, u32[]{:S(2)}) copy-start(bf16[512,128]{1,0:T(8,128)(2,1)} %param.28) | copy-start | bytes 393220
  0.0 0.8 copy-start.1
  0.8 0.7 copy-start.2
  1.5 37.0 %copy-start.13 = (f32[1408]{0:T(1024)S(1)}, f32[1408]{0:T(1024)}, u32[]{:S(2)}) copy-start(f32[1408]{0:T(1024)} %param.18) | copy-start | bytes 16900
  1.5 37.0 %copy-start.14 = (f32[1408]{0:T(1024)S(1)}, f32[1408]{0:T(1024)}, u32[]{:S(2)}) copy-start(f32[1408]{0:T(1024)} %param.19) | copy-start | bytes 16900
  1.5 37.1 %copy-start.3 = (s32[1,320]{1,0:T(1,128)S(1)}, s32[1,320]{1,0:T(1,128)}, u32[]{:S(2)}) copy-start(s32[1,320]{1,0:T(1,128)} %ids_ref.1) | copy-start | bytes 3844
  1.5 37.1 %copy-start.4 = (bf16[1,320,1408]{2,1,0:T(8,128)(2,1)S(1)}, bf16[1,320,1408]{2,1,0:T(8,128)(2,1)}, u32[]{:S(2)}) copy-start(bf16[1,320,1408]{2,1,0:T(8,128)(2,1)} %param.17) | copy-start | bytes 2703364
  1.5 37.1 %copy-start.10 = (s32[1,128]{1,0:T(1,128)S(1)}, s32[1,128]{1,0:T(1,128)}, u32[]{:S(2)}) copy-start(s32[1,128]{1,0:T(1,128)} %counts_ref.1) | copy-start | bytes 1540
  1.5 37.1 %copy-start.11 = (s32[1,128]{1,0:T(1,128)S(1)}, s32[1,128]{1,0:T(1,128)}, u32[]{:S(2)}) copy-start(s32[1,128]{1,0:T(1,128)} %owner_ref.1) | copy-start | bytes 1540
  31.1 9.5 %collective-permute-start = (bf16[768,512]{1,0:T(8,128)(2,1)S(1)}, bf16[768,512]{1,0:T(8,128)(2,1)S(1)}, u32[]{:S(2)}, u32[]{:S(2)}) collective-permute-start(bf16[768,512]{1,0:T(8,128)(2,1)S(1)} %bitcast.18), channel_id=1, source_target_pairs={{0,12},{12,0},{1,13},{13,1},{2,14},{14,2},{3,15},{15,3},{4,16},{16... | collective-permute-start | bytes 2359304 | tf_op jit(solution)/shard_map/ppermute | solution.py:277
  42.7 38.9 %copy-start.15 = (s32[8]{0:T(128)S(1)}, s32[8]{0:T(128)}, u32[]{:S(2)}) copy-start(s32[8]{0:T(128)} %constant.36.clone) | copy-start | bytes 100
  42.7 53.5 %copy-start.5 = (s32[1,2,512]{2,1,0:T(2,128)S(1)}, s32[1,2,512]{2,1,0:T(2,128)}, u32[]{:S(2)}) copy-start(s32[1,2,512]{2,1,0:T(2,128)} %param.24) | copy-start | bytes 12292
  42.7 53.5 %copy-start.6 = (f32[512]{0:T(512)S(1)}, f32[512]{0:T(512)}, u32[]{:S(2)}) copy-start(f32[512]{0:T(512)} %param.25) | copy-start | bytes 6148
  42.7 53.5 %copy-start.12 = (f32[3,512]{1,0:T(4,128)S(1)}, f32[3,512]{1,0:T(4,128)}, u32[]{:S(2)}) copy-start(f32[3,512]{1,0:T(4,128)} %constant.37.clone.table_ref) | copy-start | bytes 18436
  42.7 57.5 %copy-start.7 = (f32[512]{0:T(512)S(1)}, f32[512]{0:T(512)}, u32[]{:S(2)}) copy-start(f32[512]{0:T(512)} %param.26) | copy-start | bytes 6148
  42.7 57.5 %copy-start.8 = (f32[512]{0:T(512)S(1)}, f32[512]{0:T(512)}, u32[]{:S(2)}) copy-start(f32[512]{0:T(512)} %param.27) | copy-start | bytes 6148
  42.7 57.5 %copy-start.9 = (f32[512]{0:T(512)S(1)}, f32[512]{0:T(512)}, u32[]{:S(2)}) copy-start(f32[512]{0:T(512)} %param.30) | copy-start | bytes 6148
  42.7 57.4 %all-to-all-start.1 = ((bf16[64,40,128]{2,1,0:T(8,128)(2,1)}), bf16[64,40,128]{2,1,0:T(8,128)(2,1)}, u32[]{:S(2)}, u32[]{:S(2)}) async-start(bf16[64,40,128]{2,1,0:T(8,128)(2,1)} %bitcast.5), calls=%async_computation.1 | async-start | bytes 1310720 | tf_op jit(solution)/shard_map/all_to_all | solution.py:309
  48.2 16.3 %collective-permute-start.1 = (bf16[1,256,128]{2,1,0:T(8,128)(2,1)S(1)}, bf16[1,256,128]{2,1,0:T(8,128)(2,1)S(1)}, u32[]{:S(2)}, u32[]{:S(2)}) collective-permute-start(bf16[1,256,128]{2,1,0:T(8,128)(2,1)S(1)} %dynamic-slice_bitcast_fusion), channel_id=1, source_target_pairs={{0,4},{1,5},{2,6},{3,7},{4,8},{5,9},{6,10},{7,11},{8,0},{9,1},{10,... | collective-permute-start | bytes 196616 | tf_op jit(solution)/shard_map/ppermute | solution.py:280
  58.8 10.1 %collective-permute-start.2 = (bf16[1,256,128]{2,1,0:T(8,128)(2,1)S(1)}, bf16[1,256,128]{2,1,0:T(8,128)(2,1)S(1)}, u32[]{:S(2)}, u32[]{:S(2)}) collective-permute-start(bf16[1,256,128]{2,1,0:T(8,128)(2,1)S(1)} %dynamic-slice_bitcast_fusion), channel_id=1, source_target_pairs={{0,8},{1,9},{2,10},{3,11},{4,0},{5,1},{6,2},{7,3},{8,4},{9,5},{10,... | collective-permute-start | bytes 196616 | tf_op jit(solution)/shard_map/ppermute | solution.py:281
  69.0 9.9 %collective-permute-start.3 = (bf16[3,256,128]{2,1,0:T(8,128)(2,1)S(1)}, bf16[3,256,128]{2,1,0:T(8,128)(2,1)S(1)}, u32[]{:S(2)}, u32[]{:S(2)}) collective-permute-start(bf16[3,256,128]{2,1,0:T(8,128)(2,1)S(1)} %pad_maximum_fusion.1), channel_id=1, source_target_pairs={{0,2},{1,3},{2,0},{3,1},{4,6},{5,7},{6,4},{7,5},{8,10},{9,11},{10,... | collective-permute-start | bytes 589832 | tf_op jit(solution)/shard_map/ppermute | solution.py:308
  78.9 11.3 %collective-permute-start.5 = (bf16[6,256,128]{2,1,0:T(8,128)(2,1)S(1)}, bf16[6,256,128]{2,1,0:T(8,128)(2,1)S(1)}, u32[]{:S(2)}, u32[]{:S(2)}) collective-permute-start(bf16[6,256,128]{2,1,0:T(8,128)(2,1)S(1)} %pad_maximum_fusion.mine_hbm), channel_id=1, source_target_pairs={{0,1},{1,0},{2,3},{3,2},{4,5},{5,4},{6,7},{7,6},{8,9},{9,8},{10,11... | collective-permute-start | bytes 1179656 | tf_op jit(solution)/shard_map/ppermute | solution.py:312
  82.3 17.8 %collective-permute-start.4 = (bf16[6,256,128]{2,1,0:T(8,128)(2,1)S(1)}, bf16[6,256,128]{2,1,0:T(8,128)(2,1)S(1)}, u32[]{:S(2)}, u32[]{:S(2)}) collective-permute-start(bf16[6,256,128]{2,1,0:T(8,128)(2,1)S(1)} %pad_maximum_fusion.mine_hbm), channel_id=1, source_target_pairs={{0,12},{12,0},{1,13},{13,1},{2,14},{14,2},{3,15},{15,3},{4,16},{16... | collective-permute-start | bytes 1179656 | tf_op jit(solution)/shard_map/ppermute | solution.py:313
  90.2 18.5 %collective-permute-start.6 = (bf16[6,256,128]{2,1,0:T(8,128)(2,1)S(1)}, bf16[6,256,128]{2,1,0:T(8,128)(2,1)S(1)}, u32[]{:S(2)}, u32[]{:S(2)}) collective-permute-start(bf16[6,256,128]{2,1,0:T(8,128)(2,1)S(1)} %collective-permute-done.5.mine_hbm), channel_id=1, source_target_pairs={{0,12},{12,0},{1,13},{13,1},{2,14},{14,2},{3,15},{15,3},{4,16},{16... | collective-permute-start | bytes 1179656 | tf_op jit(solution)/shard_map/ppermute | solution.py:314
